TPU v7x, 32 devices: a whole 2x2x4 slice. The times are simulated.
32 devices in a mesh: dp: 16 (over z, x, core), mp: 2 (over y).
Axes of the slice: x: 2, y: 2, z: 4, core: 2. Of those that a mesh axis runs over, the one named last changes fastest.
Arguments:
- frames_in: float32 [12288, 768], P(('dp', 'mp')), may hold values from -6 to 6
- frames_cot: float32 [12288, 768], P(('dp', 'mp')), may hold values from -6 to 6
- clip_ids: int32 [12288], replicated, may hold values from 0 to 16, never falling along the last dimension, each value on 1 to 768 neighbouring positions
- frame_mask: int32 [12288], replicated, may hold values 0 or 1
- norm_gain: float32 [2, 2, 768], replicated, may hold values from 0.25 to 1.75
- norm_bias: float32 [2, 2, 768], replicated, may hold values from -2 to 2
- qkv_weight: bfloat16 [2, 768, 3, 768], P(None, 'dp', None, 'mp'), as said below
- qv_bias: float32 [2, 2, 768], P(None, None, 'mp'), may hold values from -0.4 to 0.4
- proj_weight: bfloat16 [2, 768, 768], P(None, ('mp', 'dp')), may hold values from -4 to 4
- up_weight: bfloat16 [2, 768, 3072], P(None, 'dp', 'mp'), may hold values from -0.21875 to 0.21875
- up_bias: float32 [2, 3072], P(None, 'mp'), may hold values from -3 to 3
- down_weight: bfloat16 [2, 3072, 768], P(None, ('mp', 'dp')), may hold values from -0.109375 to 0.109375
- out_biases: float32 [2, 2, 768], replicated, may hold values from -2 to 2
Outputs:
- frames_out: float32 [12288, 768], P(('dp', 'mp'))
- frames_grad: float32 [12288, 768], P(('dp', 'mp'))
- grad_qkv: float32 [2, 768, 3, 768], P(None, 'dp', None, 'mp')
- grad_qv_bias: float32 [2, 2, 768], P(None, None, 'mp')
- grad_proj: float32 [2, 768, 768], P(None, ('mp', 'dp'))
- grad_up: float32 [2, 768, 3072], P(None, 'dp', 'mp')
- grad_up_bias: float32 [2, 3072], P(None, 'mp')
- grad_down: float32 [2, 3072, 768], P(None, ('mp', 'dp'))
- grad_gain: float32 [2, 2, 768], replicated
- grad_norm_bias: float32 [2, 2, 768], replicated
- grad_out_biases: float32 [2, 2, 768], replicated
Inputs may be any that keep to these rules, and one draw needn't show every extreme that they name: `clip_ids`: clip numbers never fall from one frame to the next; each clip holds 1 to 768 frames and one holds exactly 768. `qkv_weight`: projection weights for queries, keys and values.
All inputs are finite; a program needn't handle non-finite values.
Results may differ from a plain program's by a relative error of at most 0.013.
Values may be sent and summed in bfloat16 or wider, within the bound.
A program may use at most 320 MiB of HBM per device.

v0:
```python
import jax
import jax.numpy as jnp
from jax import lax
from jax.sharding import PartitionSpec as P

HD = 64


epsilon = 1e-05


def padded_2(block, sides, width):
    for axis, dim in sides:
        count = lax.axis_size(axis)
        forward = [(i, i + 1) for i in range(count - 1)]
        backward = [(target, source) for source, target in forward]
        low = lax.ppermute(
            lax.slice_in_dim(block, block.shape[dim] - width, None, axis=dim), axis, forward
        )
        high = lax.ppermute(lax.slice_in_dim(block, 0, width, axis=dim), axis, backward)
        block = jnp.concatenate([low, block, high], axis=dim)
    return block


def shifted(x, axis, by):
    size = lax.axis_size(axis)
    pairs = [(i, i + by) for i in range(size) if 0 <= i + by < size]
    return lax.ppermute(x, axis, pairs)


def norm_forward(values, gain_vec, bias_vec):
    row_mean = jnp.mean(values, axis=-1, keepdims=True)
    centred = values - row_mean
    inverse = lax.rsqrt(jnp.mean(centred * centred, axis=-1, keepdims=True) + epsilon)
    normed = centred * inverse
    return ((normed * gain_vec + bias_vec).astype(jnp.bfloat16), normed, inverse)


def norm_backward(grad_out, normed, inverse, gain_vec):
    scaled = grad_out * gain_vec
    projected = (
        scaled
        - jnp.mean(scaled, axis=-1, keepdims=True)
        - normed * jnp.mean(scaled * normed, axis=-1, keepdims=True)
    )
    return (inverse * projected, jnp.sum(grad_out * normed, axis=0), jnp.sum(grad_out, axis=0))


def gelu_value(preact):
    return 0.5 * preact * (1.0 + jax.scipy.special.erf(preact * 0.7071067811865476))


def gelu_slope(preact):
    return (
        0.5 * (1.0 + jax.scipy.special.erf(preact * 0.7071067811865476))
        + preact * jnp.exp(-0.5 * preact * preact) * 0.3989422804014327
    )


def padded(values, tok_span, fill):
    border = jnp.full((tok_span,) + values.shape[1:], fill, values.dtype)
    return jnp.concatenate([border, values, border], axis=0)


def block_mask(query_ids, block_start, key_ids, key_valid, tok_span):
    query_pos = block_start + jnp.arange(query_ids.shape[0], dtype=jnp.int32)
    key_pos = jnp.arange(key_ids.shape[0], dtype=jnp.int32)
    same_clip = query_ids[:, None] == key_ids[None, :]
    visible = (key_valid[None, :] == 1) | (key_pos[None, :] == query_pos[:, None] + tok_span)
    return same_clip & visible


def window_ids(clip_ids, frame_mask, tok_span):
    offset = lax.axis_index("dp") * tok_span
    ids_pad = padded(clip_ids, tok_span, -1)
    valid_pad = padded(frame_mask, tok_span, 0)
    return (
        lax.dynamic_slice_in_dim(ids_pad, offset + tok_span, tok_span, 0),
        lax.dynamic_slice_in_dim(ids_pad, offset, 3 * tok_span, 0),
        lax.dynamic_slice_in_dim(valid_pad, offset, 3 * tok_span, 0),
    )


def fetch_weights(qkv_weight, proj_weight, up_weight, down_weight, depth):
    return (
        lax.all_gather(qkv_weight[depth], "dp", axis=0, tiled=True),
        lax.all_gather(proj_weight[depth], "dp", axis=0, tiled=True),
        lax.all_gather(up_weight[depth], "dp", axis=0, tiled=True),
        lax.all_gather(down_weight[depth], "dp", axis=0, tiled=True),
    )


def gather_rows(values):
    return lax.all_gather(values, "mp", axis=0, tiled=True)


def sum_rows(left, right):
    return lax.psum_scatter(
        jnp.dot(left, right, preferred_element_type=jnp.float32),
        "mp",
        scatter_dimension=0,
        tiled=True,
    )


def block_scores(query, keys, query_ids, key_ids, key_valid, offset):
    tok_span = query.shape[0]
    allowed = block_mask(query_ids, offset, key_ids, key_valid, tok_span)
    scores = jnp.einsum("qhd,khd->hqk", query, keys, preferred_element_type=jnp.float32) * HD ** (
        -0.5
    )
    return (query, jnp.where(allowed[None], scores, -1e30))


def attend(query, key_vals, query_ids, key_ids, key_valid):
    tok_span = query.shape[0]
    n_blocks = (tok_span + 1023) // 1024
    block_rows = tok_span // n_blocks
    keys = key_vals[:, 0]
    values = key_vals[:, 1]

    def one_block(block_id):
        offset = block_id * block_rows
        query_block, scores = block_scores(query, keys, query_ids, key_ids, key_valid, offset)
        row_max = jnp.max(scores, axis=-1, keepdims=True)
        log_total = row_max + jnp.log(jnp.sum(jnp.exp(scores - row_max), axis=-1, keepdims=True))
        prob_low = jnp.exp(scores - log_total).astype(jnp.bfloat16)
        attended = jnp.einsum(
            "hqk,khd->qhd", prob_low, values, preferred_element_type=jnp.float32
        ).astype(jnp.bfloat16)
        return (attended, log_total[..., 0])

    attended, log_totals = lax.map(one_block, jnp.arange(n_blocks, dtype=jnp.int32))
    return (attended.reshape(query.shape), log_totals)


def attend_back(query, key_vals, attended, grad_attn, log_totals, query_ids, key_ids, key_valid):
    tok_span = query.shape[0]
    n_blocks = (tok_span + 1023) // 1024
    block_rows = tok_span // n_blocks
    score_scale = HD ** (-0.5)
    keys = key_vals[:, 0]
    values = key_vals[:, 1]

    def one_block(key_grads, block_id):
        offset = block_id * block_rows
        query_block, scores = block_scores(query, keys, query_ids, key_ids, key_valid, offset)
        prob_full = jnp.exp(scores - log_totals[block_id][..., None])
        prob_low = prob_full.astype(jnp.bfloat16)
        grad_prob = jnp.einsum(
            "qhd,khd->hqk", grad_attn, values, preferred_element_type=jnp.float32
        )
        delta_row = jnp.sum(grad_attn.astype(jnp.float32) * attended.astype(jnp.float32), axis=-1).T
        score_low = (prob_full * (grad_prob - delta_row[..., None])).astype(jnp.bfloat16)
        grad_query = (
            jnp.einsum("hqk,khd->qhd", score_low, keys, preferred_element_type=jnp.float32)
            * score_scale
        )
        grad_key = (
            jnp.einsum("hqk,qhd->khd", score_low, query_block, preferred_element_type=jnp.float32)
            * score_scale
        )
        grad_value = jnp.einsum(
            "hqk,qhd->khd", prob_low, grad_attn, preferred_element_type=jnp.float32
        )
        return (key_grads + jnp.stack([grad_key, grad_value], axis=1), grad_query)

    start = jnp.zeros((3 * tok_span, 2) + query.shape[1:], jnp.float32)
    key_grads, grad_query = lax.scan(one_block, start, jnp.arange(n_blocks, dtype=jnp.int32))
    return (grad_query.reshape(query.shape), key_grads)


def widen(piece, full_width, mp_index):
    out_shape = piece.shape[:-1] + (full_width,)
    return lax.dynamic_update_slice_in_dim(
        jnp.zeros(out_shape, jnp.float32), piece, mp_index * piece.shape[-1], piece.ndim - 1
    )


def layer_forward(
    state, matrices, gain_pair, bias_pair, qv_pair, up_vec, out_pair, query_ids, key_ids, key_valid
):
    qkv_mat, proj_mat, up_mat, down_mat = matrices
    head_cols = qkv_mat.shape[-1]
    first_norm, hat_one, inv_one = norm_forward(state, gain_pair[0], bias_pair[0])
    first_full = gather_rows(first_norm)
    tok_span = first_full.shape[0]
    bias_three = jnp.stack([qv_pair[0], jnp.zeros_like(qv_pair[0]), qv_pair[1]])
    qkv_proj = jnp.dot(
        first_full,
        qkv_mat.reshape(qkv_mat.shape[0], 3 * head_cols),
        preferred_element_type=jnp.float32,
    )
    qkv_proj = (qkv_proj.reshape(tok_span, 3, head_cols) + bias_three).astype(jnp.bfloat16)
    query = qkv_proj[:, 0].reshape(tok_span, head_cols // HD, HD)
    key_vals = qkv_proj[:, 1:].reshape(tok_span, 2 * head_cols)
    key_vals = padded_2(key_vals, (("dp", 0),), tok_span)
    key_vals = key_vals.reshape(3 * tok_span, 2, head_cols // HD, HD)
    attended, log_totals = attend(query, key_vals, query_ids, key_ids, key_valid)
    attn_flat = attended.reshape(tok_span, head_cols)
    middle = state + sum_rows(attn_flat, proj_mat) + out_pair[0]
    second_norm, hat_two, inv_two = norm_forward(middle, gain_pair[1], bias_pair[1])
    second_full = gather_rows(second_norm)
    preact = jnp.dot(second_full, up_mat, preferred_element_type=jnp.float32) + up_vec
    hidden = gelu_value(preact).astype(jnp.bfloat16)
    result = middle + sum_rows(hidden, down_mat) + out_pair[1]
    stored = {
        "hat_one": hat_one,
        "inv_one": inv_one,
        "first_full": first_full,
        "query": query,
        "key_vals": key_vals,
        "attended": attended,
        "log_totals": log_totals,
        "hat_two": hat_two,
        "inv_two": inv_two,
        "second_full": second_full,
        "preact": preact,
        "hidden": hidden,
    }
    return (stored, result)


def layer_backward(gradient, stored, matrices, gain_pair, query_ids, key_ids, key_valid):
    qkv_mat, proj_mat, up_mat, down_mat = matrices
    head_cols = qkv_mat.shape[-1]
    grad_full = gather_rows(gradient.astype(jnp.bfloat16))
    grad_down = jnp.dot(stored["hidden"].T, grad_full, preferred_element_type=jnp.float32)
    grad_pre = jnp.dot(grad_full, down_mat.T, preferred_element_type=jnp.float32) * gelu_slope(
        stored["preact"]
    )
    grad_upb = jnp.sum(grad_pre, axis=0)
    pre_low = grad_pre.astype(jnp.bfloat16)
    grad_up = jnp.dot(stored["second_full"].T, pre_low, preferred_element_type=jnp.float32)
    grad_second = sum_rows(pre_low, up_mat.T)
    back_two, gain_two, shift_two = norm_backward(
        grad_second, stored["hat_two"], stored["inv_two"], gain_pair[1]
    )
    grad_middle = gradient + back_two
    middle_full = gather_rows(grad_middle.astype(jnp.bfloat16))
    attended = stored["attended"]
    tok_span = attended.shape[0]
    grad_proj = jnp.dot(
        attended.reshape(tok_span, head_cols).T, middle_full, preferred_element_type=jnp.float32
    )
    grad_attn = jnp.dot(middle_full, proj_mat.T, preferred_element_type=jnp.float32).astype(
        jnp.bfloat16
    )
    grad_attn = grad_attn.reshape(attended.shape)
    grad_query, key_grads = attend_back(
        stored["query"],
        stored["key_vals"],
        attended,
        grad_attn,
        stored["log_totals"],
        query_ids,
        key_ids,
        key_valid,
    )
    key_grads = key_grads.reshape(3 * tok_span, 2 * head_cols)
    own_grads = key_grads[tok_span : 2 * tok_span]
    for step_by, piece in ((1, key_grads[2 * tok_span :]), (-1, key_grads[:tok_span])):
        own_grads = own_grads + shifted(piece.astype(jnp.bfloat16), "dp", step_by).astype(
            piece.dtype
        )
    grad_query = grad_query.reshape(tok_span, head_cols)
    grad_key = own_grads[:, :head_cols]
    grad_value = own_grads[:, head_cols:]
    grad_qv = jnp.stack([jnp.sum(grad_query, axis=0), jnp.sum(grad_value, axis=0)])
    qkv_low = (
        jnp.stack([grad_query, grad_key, grad_value], axis=1)
        .astype(jnp.bfloat16)
        .reshape(tok_span, 3 * head_cols)
    )
    grad_qkv = jnp.dot(stored["first_full"].T, qkv_low, preferred_element_type=jnp.float32).reshape(
        -1, 3, head_cols
    )
    grad_first = sum_rows(qkv_low, qkv_mat.reshape(-1, 3 * head_cols).T)
    back_one, gain_one, shift_one = norm_backward(
        grad_first, stored["hat_one"], stored["inv_one"], gain_pair[0]
    )
    new_grad = grad_middle + back_one
    mp_index = lax.axis_index("mp")
    mp_count = lax.axis_size("mp")
    small = (
        jnp.stack([gain_one, gain_two]),
        jnp.stack([shift_one, shift_two]),
        jnp.stack([jnp.sum(grad_middle, axis=0), jnp.sum(gradient, axis=0)]),
        widen(grad_qv, head_cols * mp_count, mp_index),
        widen(grad_upb, grad_upb.shape[0] * mp_count, mp_index),
    )
    return (new_grad, (grad_qkv, grad_proj, grad_up, grad_down), small)


def body(
    frames_in,
    frames_cot,
    clip_ids,
    frame_mask,
    norm_gain,
    norm_bias,
    qkv_weight,
    qv_bias,
    proj_weight,
    up_weight,
    up_bias,
    down_weight,
    out_biases,
):
    layers = qkv_weight.shape[0]
    tok_span = frames_in.shape[0] * lax.axis_size("mp")
    query_ids, key_ids, key_valid = window_ids(clip_ids, frame_mask, tok_span)
    stored_all = []
    state = frames_in
    for depth in range(layers):
        matrices = fetch_weights(qkv_weight, proj_weight, up_weight, down_weight, depth)
        stored, state = layer_forward(
            state,
            matrices,
            norm_gain[depth],
            norm_bias[depth],
            qv_bias[depth],
            up_bias[depth],
            out_biases[depth],
            query_ids,
            key_ids,
            key_valid,
        )
        stored_all.append(stored)
    gradient = frames_cot
    weight_grads = []
    small_grads = []
    for depth in range(layers - 1, -1, -1):
        matrices = fetch_weights(qkv_weight, proj_weight, up_weight, down_weight, depth)
        gradient, mats_grad, small = layer_backward(
            gradient, stored_all[depth], matrices, norm_gain[depth], query_ids, key_ids, key_valid
        )
        mats_grad = (
            lax.psum_scatter(mats_grad[0], "dp", scatter_dimension=0, tiled=True),
            lax.psum_scatter(mats_grad[1], "dp", scatter_dimension=0, tiled=True),
            lax.psum_scatter(mats_grad[2], "dp", scatter_dimension=0, tiled=True),
            lax.psum_scatter(mats_grad[3], "dp", scatter_dimension=0, tiled=True),
        )
        small = lax.psum((small[0], small[1], small[2], small[3], small[4]), ("dp", "mp"))
        weight_grads.insert(0, mats_grad)
        small_grads.insert(0, small)
    stacked_w = tuple((jnp.stack([entry[slot] for entry in weight_grads]) for slot in range(4)))
    stacked_s = tuple((jnp.stack([entry[slot] for entry in small_grads]) for slot in range(5)))
    mp_index = lax.axis_index("mp")
    head_cols = qv_bias.shape[-1]
    up_cols = up_bias.shape[-1]
    grad_qv = lax.dynamic_slice_in_dim(stacked_s[3], mp_index * head_cols, head_cols, 2)
    grad_upb = lax.dynamic_slice_in_dim(stacked_s[4], mp_index * up_cols, up_cols, 1)
    return (
        state,
        gradient,
        stacked_w[0],
        grad_qv,
        stacked_w[1],
        stacked_w[2],
        grad_upb,
        stacked_w[3],
        stacked_s[0],
        stacked_s[1],
        stacked_s[2],
    )


def solution(mesh):
    placed = (
        P(("dp", "mp"), None),
        P(("dp", "mp"), None),
        P(),
        P(),
        P(),
        P(),
        P(None, "dp", None, "mp"),
        P(None, None, "mp"),
        P(None, ("mp", "dp"), None),
        P(None, "dp", "mp"),
        P(None, "mp"),
        P(None, ("mp", "dp"), None),
        P(),
    )
    return jax.shard_map(
        body,
        mesh=mesh,
        in_specs=placed,
        out_specs=(
            P(("dp", "mp"), None),
            P(("dp", "mp"), None),
            P(None, "dp", None, "mp"),
            P(None, None, "mp"),
            P(None, ("mp", "dp"), None),
            P(None, "dp", "mp"),
            P(None, "mp"),
            P(None, ("mp", "dp"), None),
            P(),
            P(),
            P(),
        ),
        check_vma=False,
    )
```

profile of v0, /device:TPU:0, one launch (start us, length us, event | category | flops | bytes accessed | tf_op | source)
XLA Modules:
  0.0 1947.3 jit_solution(16931985044161411071)
XLA Ops:
  14.8 39.2 %all-gather.39.cloned.1.call-done = bf16[1,768,3,384]{3,1,2,0:T(8,128)(2,1)} async-done(((bf16[1,48,3,384]{3,1,2,0:T(8,128)(2,1)}), bf16[1,768,3,384]{3,1,2,0:T(8,128)(2,1)}) %all-gather.39.cloned.1.call-update) | async-done | bytes 1769488 | tf_op jit(solution)/shard_map/all_gather | solution.py:86
  56.7 21.0 %all-gather.23.cloned.1.call-done = bf16[768,768]{1,0:T(8,128)(2,1)} async-done(((bf16[384,768]{1,0:T(8,128)(2,1)}), bf16[768,768]{1,0:T(8,128)(2,1)}) %all-gather.23.cloned.1.call-update) | async-done | bytes 1179664 | tf_op jit(solution)/shard_map/all_gather | solution.py:94
  84.2 4.1 collective-permute-start
  88.5 39.6 %all-gather.1 = bf16[1,384,768]{2,1,0:T(8,128)(2,1)} all-gather(bf16[1,24,768]{2,1,0:T(8,128)(2,1)S(1)} %get-tuple-element.207), channel_id=3, replica_groups=mesh['dp'=16,'mp'=2] {'dp'}, dimensions={1}, use_global_device_ids=true | all-gather | bytes 626688 | tf_op jit(solution)/shard_map/all_gather | solution.py:87
  132.2 3.6 pad_maximum_fusion.2
  135.8 18.2 fusion.2
  153.9 20.5 %exponential_reduce_fusion.1 = f32[6,768]{1,0:T(8,128)S(1)} fusion(f32[6,768,2304]{2,1,0:T(8,128)} %get-tuple-element.215, f32[6,768]{1,0:T(8,128)} %get-tuple-element.214, pred[768,2304]{1,0:T(8,128)(4,1)S(1)} %fusion.7), kind=kLoop, calls=%fused_computation.6 | loop fusion | flops 42462720 | bytes 44273664 | tf_op jit(solution)/shard_map/while/body/eval_jaxpr/reduce_sum | solution.py:126
  175.1 17.3 fusion.59
  192.4 3.5 fusion.76
  198.3 32.1 %reduce-scatter.17.cloned.1.call-done = f32[384,768]{1,0:T(8,128)} async-done(((f32[768,768]{1,0:T(8,128)}), f32[384,768]{1,0:T(8,128)}) %reduce-scatter.17.cloned.1.call-update) | async-done | bytes 1179664 | tf_op jit(solution)/shard_map/reduce_scatter | solution.py:98
  236.0 39.4 %all-gather.41.cloned.1.call-done = bf16[1,768,1536]{2,1,0:T(8,128)(2,1)} async-done(((bf16[1,48,1536]{2,1,0:T(8,128)(2,1)}), bf16[1,768,1536]{2,1,0:T(8,128)(2,1)}) %all-gather.41.cloned.1.call-update) | async-done | bytes 2359312 | tf_op jit(solution)/shard_map/all_gather | solution.py:88
  275.4 23.5 %all-gather.25.cloned.1.call-done = bf16[768,768]{1,0:T(8,128)(2,1)} async-done(((bf16[384,768]{1,0:T(8,128)(2,1)}), bf16[768,768]{1,0:T(8,128)(2,1)}) %all-gather.25.cloned.1.call-update) | async-done | bytes 1179664 | tf_op jit(solution)/shard_map/all_gather | solution.py:94
  298.9 7.0 multiply_convert_fusion.3
  305.9 38.0 %all-gather.43.cloned.1.call-done = bf16[1,1536,768]{2,1,0:T(8,128)(2,1)} async-done(((bf16[1,96,768]{2,1,0:T(8,128)(2,1)}), bf16[1,1536,768]{2,1,0:T(8,128)(2,1)}) %all-gather.43.cloned.1.call-update) | async-done | bytes 2359312 | tf_op jit(solution)/shard_map/all_gather | solution.py:89
  343.9 5.8 fusion.30
  350.5 32.9 %reduce-scatter.19.cloned.1.call-done = f32[384,768]{1,0:T(8,128)} async-done(((f32[768,768]{1,0:T(8,128)}), f32[384,768]{1,0:T(8,128)}) %reduce-scatter.19.cloned.1.call-update) | async-done | bytes 1179664 | tf_op jit(solution)/shard_map/reduce_scatter | solution.py:98
  387.1 39.1 %all-gather.45.cloned.1.call-done = bf16[1,768,3,384]{3,1,2,0:T(8,128)(2,1)} async-done(((bf16[1,48,3,384]{3,1,2,0:T(8,128)(2,1)}), bf16[1,768,3,384]{3,1,2,0:T(8,128)(2,1)}) %all-gather.45.cloned.1.call-update) | async-done | bytes 1769488 | tf_op jit(solution)/shard_map/all_gather | solution.py:86
  428.8 21.0 %all-gather.27.cloned.1.call-done = bf16[768,768]{1,0:T(8,128)(2,1)} async-done(((bf16[384,768]{1,0:T(8,128)(2,1)}), bf16[768,768]{1,0:T(8,128)(2,1)}) %all-gather.27.cloned.1.call-update) | async-done | bytes 1179664 | tf_op jit(solution)/shard_map/all_gather | solution.py:94
  457.2 39.2 %all-gather.5 = bf16[1,384,768]{2,1,0:T(8,128)(2,1)S(1)} all-gather(bf16[1,24,768]{2,1,0:T(8,128)(2,1)S(1)} %copy-done.50), channel_id=7, replica_groups=mesh['dp'=16,'mp'=2] {'dp'}, dimensions={1}, use_global_device_ids=true | all-gather | bytes 626688 | tf_op jit(solution)/shard_map/all_gather | solution.py:87
  498.4 17.7 fusion.3
  516.1 19.9 %exponential_reduce_fusion = f32[6,768]{1,0:T(8,128)S(1)} fusion(f32[6,768,2304]{2,1,0:T(8,128)} %get-tuple-element.219, f32[6,768]{1,0:T(8,128)S(1)} %get-tuple-element.218, pred[768,2304]{1,0:T(8,128)(4,1)S(1)} %fusion.7), kind=kLoop, calls=%fused_computation.3 | loop fusion | flops 42462720 | bytes 44273664 | tf_op jit(solution)/shard_map/while/body/eval_jaxpr/reduce_sum | solution.py:126
  536.7 17.3 fusion.58
  557.9 33.6 %reduce-scatter.21.cloned.1.call-done = f32[384,768]{1,0:T(8,128)} async-done(((f32[768,768]{1,0:T(8,128)}), f32[384,768]{1,0:T(8,128)}) %reduce-scatter.21.cloned.1.call-update) | async-done | bytes 1179664 | tf_op jit(solution)/shard_map/reduce_scatter | solution.py:98
  599.2 37.5 %all-gather.47.cloned.1.call-done = bf16[1,768,1536]{2,1,0:T(8,128)(2,1)} async-done(((bf16[1,48,1536]{2,1,0:T(8,128)(2,1)}), bf16[1,768,1536]{2,1,0:T(8,128)(2,1)}) %all-gather.47.cloned.1.call-update) | async-done | bytes 2359312 | tf_op jit(solution)/shard_map/all_gather | solution.py:88
  636.7 23.5 %all-gather.29.cloned.1.call-done = bf16[768,768]{1,0:T(8,128)(2,1)} async-done(((bf16[384,768]{1,0:T(8,128)(2,1)}), bf16[768,768]{1,0:T(8,128)(2,1)}) %all-gather.29.cloned.1.call-update) | async-done | bytes 1179664 | tf_op jit(solution)/shard_map/all_gather | solution.py:94
  660.2 6.9 multiply_convert_fusion.2
  667.0 18.0 all-gather.31.cloned.1.call-done
  685.1 44.5 %all-gather.49.cloned.1.call-done = bf16[1,1536,768]{2,1,0:T(8,128)(2,1)} async-done(((bf16[1,96,768]{2,1,0:T(8,128)(2,1)}), bf16[1,1536,768]{2,1,0:T(8,128)(2,1)}) %all-gather.49.cloned.1.call-update) | async-done | bytes 2359312 | tf_op jit(solution)/shard_map/all_gather | solution.py:89
  729.5 6.4 fusion.103
  740.9 5.8 fusion.23
  746.7 27.8 %reduce-scatter.25.cloned.1.call-done = f32[384,768]{1,0:T(8,128)} async-done(((f32[768,768]{1,0:T(8,128)}), f32[384,768]{1,0:T(8,128)}) %reduce-scatter.25.cloned.1.call-update) | async-done | bytes 1179664 | tf_op jit(solution)/shard_map/reduce_scatter | solution.py:98
  777.8 33.6 %reduce-scatter.23.cloned.1.call-done = f32[384,768]{1,0:T(8,128)} async-done(((f32[768,768]{1,0:T(8,128)}), f32[384,768]{1,0:T(8,128)}) %reduce-scatter.23.cloned.1.call-update) | async-done | bytes 1179664 | tf_op jit(solution)/shard_map/reduce_scatter | solution.py:98
  811.4 4.5 fusion.91
  818.2 22.5 %all-gather.33.cloned.1.call-done = bf16[768,768]{1,0:T(8,128)(2,1)} async-done(((bf16[384,768]{1,0:T(8,128)(2,1)}), bf16[768,768]{1,0:T(8,128)(2,1)}) %all-gather.33.cloned.1.call-update) | async-done | bytes 1179664 | tf_op jit(solution)/shard_map/all_gather | solution.py:94
  843.1 19.4 convolution_bitcast_fusion.1
  862.5 28.0 %multiply_convert_fusion.1 = bf16[6,768,2304]{2,1,0:T(8,128)(2,1)} fusion(f32[6,768,2304]{2,1,0:T(8,128)} %get-tuple-element.219, bf16[768,6,64]{0,2,1:T(8,128)(2,1)S(1)} %bitcast.283, f32[6,768]{1,0:T(8,128)S(1)} %bitcast.293, f32[6,768]{1,0:T(8,128)S(1)} %copy-done.74, pred[768,2304]{1,0:T(8,128)(4,1)S(1)} %fusion.7, ...), kind=kOutput, calls=%fused_computation.1 | convolution fusion | flops 1422655488 | bytes 67866624 | tf_op jit(solution)/shard_map/while/body/eval_jaxpr/qhd,khd->hqk/dot_general | solution.py:150
  890.5 9.2 fusion.19
  909.2 4.2 collective-permute-start.4
  913.4 11.2 bitcast_reduce_fusion.1
  941.3 41.2 %reduce-scatter.27.cloned.1.call-done = f32[384,768]{1,0:T(8,128)} async-done(((f32[768,768]{1,0:T(8,128)}), f32[384,768]{1,0:T(8,128)}) %reduce-scatter.27.cloned.1.call-update) | async-done | bytes 1179664 | tf_op jit(solution)/shard_map/reduce_scatter | solution.py:98
  988.1 22.9 %all-gather.35.cloned.1.call-done = bf16[768,768]{1,0:T(8,128)(2,1)} async-done(((bf16[384,768]{1,0:T(8,128)(2,1)}), bf16[768,768]{1,0:T(8,128)(2,1)}) %all-gather.35.cloned.1.call-update) | async-done | bytes 1179664 | tf_op jit(solution)/shard_map/all_gather | solution.py:94
  1010.9 6.4 fusion.102
  1022.2 34.9 %reduce-scatter.29.cloned.1.call-done = f32[384,768]{1,0:T(8,128)} async-done(((f32[768,768]{1,0:T(8,128)}), f32[384,768]{1,0:T(8,128)}) %reduce-scatter.29.cloned.1.call-update) | async-done | bytes 1179664 | tf_op jit(solution)/shard_map/reduce_scatter | solution.py:98
  1062.9 22.6 %all-gather.37.cloned.1.call-done = bf16[768,768]{1,0:T(8,128)(2,1)} async-done(((bf16[384,768]{1,0:T(8,128)(2,1)}), bf16[768,768]{1,0:T(8,128)(2,1)}) %all-gather.37.cloned.1.call-update) | async-done | bytes 1179664 | tf_op jit(solution)/shard_map/all_gather | solution.py:94
  1087.7 19.4 convolution_bitcast_fusion
  1107.1 28.2 %multiply_convert_fusion = bf16[6,768,2304]{2,1,0:T(8,128)(2,1)} fusion(f32[6,768,2304]{2,1,0:T(8,128)} %get-tuple-element.215, bf16[768,6,64]{0,2,1:T(8,128)(2,1)S(1)} %bitcast.280, f32[6,768]{1,0:T(8,128)S(1)} %bitcast.292, f32[6,768]{1,0:T(8,128)S(1)} %copy-done.73, pred[768,2304]{1,0:T(8,128)(4,1)S(1)} %fusion.7, ...), kind=kOutput, calls=%fused_computation | convolution fusion | flops 1422655488 | bytes 67866624 | tf_op jit(solution)/shard_map/while/body/eval_jaxpr/qhd,khd->hqk/dot_general | solution.py:150
  1135.3 9.2 fusion.18
  1150.7 4.5 collective-permute-start.6
  1155.2 11.8 bitcast_reduce_fusion
  1183.6 5.8 fusion.107
  1190.7 5.9 fusion.106
  1197.9 5.9 fusion.69
  1205.2 5.8 fusion.66
  1246.1 4.9 fusion.36
  1254.8 5.4 fusion.38
  1260.2 42.7 %reduce-scatter.47.cloned.1.call-done = f32[96,768]{1,0:T(8,128)} async-done(((f32[1536,768]{1,0:T(8,128)}), f32[96,768]{1,0:T(8,128)}) %reduce-scatter.47.cloned.1.call-update) | async-done | bytes 294928 | tf_op jit(solution)/shard_map/reduce_scatter | solution.py:342
  1302.9 78.5 %reduce-scatter.45.cloned.1.call-done = f32[96,768]{1,0:T(8,128)} async-done(((f32[1536,768]{1,0:T(8,128)}), f32[96,768]{1,0:T(8,128)}) %reduce-scatter.45.cloned.1.call-update) | async-done | bytes 294928 | tf_op jit(solution)/shard_map/reduce_scatter | solution.py:342
  1383.3 76.7 %reduce-scatter.43.cloned.1.call-done = f32[48,1536]{1,0:T(8,128)} async-done(((f32[768,1536]{1,0:T(8,128)}), f32[48,1536]{1,0:T(8,128)}) %reduce-scatter.43.cloned.1.call-update) | async-done | bytes 294928 | tf_op jit(solution)/shard_map/reduce_scatter | solution.py:341
  1460.1 78.5 %reduce-scatter.41.cloned.1.call-done = f32[48,1536]{1,0:T(8,128)} async-done(((f32[768,1536]{1,0:T(8,128)}), f32[48,1536]{1,0:T(8,128)}) %reduce-scatter.41.cloned.1.call-update) | async-done | bytes 294928 | tf_op jit(solution)/shard_map/reduce_scatter | solution.py:341
  1540.5 59.0 %reduce-scatter.39.cloned.1.call-done = f32[24,768]{1,0:T(8,128)} async-done(((f32[384,768]{1,0:T(8,128)}), f32[24,768]{1,0:T(8,128)}) %reduce-scatter.39.cloned.1.call-update) | async-done | bytes 73744 | tf_op jit(solution)/shard_map/reduce_scatter | solution.py:340
  1599.5 60.9 %reduce-scatter.37.cloned.1.call-done = f32[24,768]{1,0:T(8,128)} async-done(((f32[384,768]{1,0:T(8,128)}), f32[24,768]{1,0:T(8,128)}) %reduce-scatter.37.cloned.1.call-update) | async-done | bytes 73744 | tf_op jit(solution)/shard_map/reduce_scatter | solution.py:340
  1664.6 128.0 %all-reduce.3.cloned.1.call-done = (f32[1,2,768]{2,1,0:T(2,128)}, f32[1,2,768]{2,1,0:T(2,128)}, f32[1,3072]{1,0:T(1,128)}, f32[1,3072]{1,0:T(1,128)}, f32[1,2,76...) async-done(((f32[1,2,768]{2,1,0:T(2,128)}, f32[1,2,768]{2,1,0:T(2,128)}, ...) | async-done | bytes 73744 | tf_op jit(solution)/shard_map/psum | solution.py:344
  1799.2 68.4 %reduce-scatter.35.cloned.1.call-done = f32[48,3,384]{2,0,1:T(8,128)} async-done(((f32[768,3,384]{2,0,1:T(8,128)}), f32[48,3,384]{2,0,1:T(8,128)}) %reduce-scatter.35.cloned.1.call-update) | async-done | bytes 221200 | tf_op jit(solution)/shard_map/reduce_scatter | solution.py:339
  1867.6 70.9 %reduce-scatter.33.cloned.1.call-done = f32[48,3,384]{2,0,1:T(8,128)} async-done(((f32[768,3,384]{2,0,1:T(8,128)}), f32[48,3,384]{2,0,1:T(8,128)}) %reduce-scatter.33.cloned.1.call-update) | async-done | bytes 221200 | tf_op jit(solution)/shard_map/reduce_scatter | solution.py:339
  (412 shorter events, 197.1 us)
Async XLA Ops:
  7.2 46.9 %all-gather.39.cloned.1.call-start = ((), (), s32[]{:S(2)}) async-start(), calls=%async_computation.40 | async-start | bytes 1880064 | tf_op jit(solution)/shard_map/all_gather | solution.py:86
  9.0 68.7 %all-gather.23.cloned.1.call-start = ((), (), s32[]{:S(2)}) async-start(), calls=%async_computation.16 | async-start | bytes 1769472 | tf_op jit(solution)/shard_map/all_gather | solution.py:94
  11.3 220.9 %copy-start.52 = (f32[768]{0:T(1024)}, f32[768]{0:T(1024)S(1)}, u32[]{:S(2)}) copy-start(f32[768]{0:T(1024)S(1)} %get-tuple-element.148) | copy-start | bytes 9220
  11.3 373.9 %copy-start.54 = (f32[768]{0:T(1024)}, f32[768]{0:T(1024)S(1)}, u32[]{:S(2)}) copy-start(f32[768]{0:T(1024)S(1)} %get-tuple-element.150) | copy-start | bytes 9220
  13.4 217.0 %reduce-scatter.17.cloned.1.call-start = ((), (), s32[]{:S(2)}) async-start(), calls=%async_computation.17 | async-start | bytes 3538944 | tf_op jit(solution)/shard_map/reduce_scatter | solution.py:98
  82.9 49.3 %collective-permute-start.1 = (bf16[768,768]{0,1:T(8,128)(2,1)}, bf16[768,768]{0,1:T(8,128)(2,1)}, u32[]{:S(2)}, u32[]{:S(2)}) collective-permute-start(bf16[768,768]{0,1:T(8,128)(2,1)} %bitcast.6), channel_id=1, source_target_pairs={{2,0},{4,2},{6,4},{8,6},{10,8},{12,10},{14,12},{16,14},{18,16},{20... | collective-permute-start | bytes 3538952 | tf_op jit(solution)/shard_map/ppermute | solution.py:20
  84.2 48.0 %collective-permute-start = (bf16[768,768]{0,1:T(8,128)(2,1)}, bf16[768,768]{0,1:T(8,128)(2,1)}, u32[]{:S(2)}, u32[]{:S(2)}) collective-permute-start(bf16[768,768]{0,1:T(8,128)(2,1)} %bitcast.6), channel_id=1, source_target_pairs={{0,2},{2,4},{4,6},{6,8},{8,10},{10,12},{12,14},{14,16},{16,18},{18... | collective-permute-start | bytes 3538952 | tf_op jit(solution)/shard_map/ppermute | solution.py:17
  195.9 79.5 %all-gather.41.cloned.1.call-start = ((), (), s32[]{:S(2)}) async-start(), calls=%async_computation.41 | async-start | bytes 2506752 | tf_op jit(solution)/shard_map/all_gather | solution.py:88
  197.6 101.3 %all-gather.25.cloned.1.call-start = ((), (), s32[]{:S(2)}) async-start(), calls=%async_computation.18 | async-start | bytes 1769472 | tf_op jit(solution)/shard_map/all_gather | solution.py:94
  232.2 73.7 %copy-start.69 = (f32[384]{0:T(512)}, f32[384]{0:T(512)S(1)}, u32[]{:S(2)}) copy-start(f32[384]{0:T(512)S(1)} %add_rsqrt_fusion.2) | copy-start | bytes 4612
  234.0 109.9 %all-gather.43.cloned.1.call-start = ((), (), s32[]{:S(2)}) async-start(), calls=%async_computation.42 | async-start | bytes 2506752 | tf_op jit(solution)/shard_map/all_gather | solution.py:89
  234.8 148.6 %reduce-scatter.19.cloned.1.call-start = ((), (), s32[]{:S(2)}) async-start(), calls=%async_computation.19 | async-start | bytes 3538944 | tf_op jit(solution)/shard_map/reduce_scatter | solution.py:98
  236.0 69.9 %copy-start.88 = (f32[1536]{0:T(1024)}, f32[1536]{0:T(1024)S(1)}, u32[]{:S(2)}) copy-start(f32[1536]{0:T(1024)S(1)} %get-tuple-element.146) | copy-start | bytes 18436
  349.7 33.7 %copy-start.3 = (f32[384,768]{1,0:T(8,128)S(1)}, f32[384,768]{1,0:T(8,128)}, u32[]{:S(2)}) copy-start(f32[384,768]{1,0:T(8,128)} %copy-done.2) | copy-start | bytes 3538948
  349.7 76.4 %all-gather.45.cloned.1.call-start = ((), (), s32[]{:S(2)}) async-start(), calls=%async_computation.43 | async-start | bytes 1880064 | tf_op jit(solution)/shard_map/all_gather | solution.py:86
  350.5 99.3 %all-gather.27.cloned.1.call-start = ((), (), s32[]{:S(2)}) async-start(), calls=%async_computation.20 | async-start | bytes 1769472 | tf_op jit(solution)/shard_map/all_gather | solution.py:94
  387.0 62.8 %copy-start.92 = (f32[3,384]{1,0:T(4,128)S(1)}, f32[3,384]{1,0:T(4,128)}, u32[]{:S(2)}) copy-start(f32[3,384]{1,0:T(4,128)} %get-tuple-element.212) | copy-start | bytes 13828
  387.0 204.5 %reduce-scatter.21.cloned.1.call-start = ((), (), s32[]{:S(2)}) async-start(), calls=%async_computation.21 | async-start | bytes 3538944 | tf_op jit(solution)/shard_map/reduce_scatter | solution.py:98
  452.7 43.7 %collective-permute-start.3 = (bf16[768,768]{0,1:T(8,128)(2,1)S(1)}, bf16[768,768]{0,1:T(8,128)(2,1)S(1)}, u32[]{:S(2)}, u32[]{:S(2)}) collective-permute-start(bf16[768,768]{0,1:T(8,128)(2,1)S(1)} %bitcast.267), channel_id=1, source_target_pairs={{2,0},{4,2},{6,4},{8,6},{10,8},{12,10},{14,12},{16,14},{18,16},{20... | collective-permute-start | bytes 3538952 | tf_op jit(solution)/shard_map/ppermute | solution.py:20
  454.0 42.4 %collective-permute-start.2 = (bf16[768,768]{0,1:T(8,128)(2,1)S(1)}, bf16[768,768]{0,1:T(8,128)(2,1)S(1)}, u32[]{:S(2)}, u32[]{:S(2)}) collective-permute-start(bf16[768,768]{0,1:T(8,128)(2,1)S(1)} %bitcast.268), channel_id=1, source_target_pairs={{0,2},{2,4},{4,6},{6,8},{8,10},{10,12},{12,14},{14,16},{16,18},{18... | collective-permute-start | bytes 3538952 | tf_op jit(solution)/shard_map/ppermute | solution.py:17
  496.4 57.6 %copy-start.32 = (bf16[1,384,768]{2,1,0:T(8,128)(2,1)}, bf16[1,384,768]{2,1,0:T(8,128)(2,1)S(1)}, u32[]{:S(2)}) copy-start(bf16[1,384,768]{2,1,0:T(8,128)(2,1)S(1)} %all-gather.5) | copy-start | bytes 1769476
  557.0 34.5 %copy-start.6 = (f32[384,768]{1,0:T(8,128)S(1)}, f32[384,768]{1,0:T(8,128)}, u32[]{:S(2)}) copy-start(f32[384,768]{1,0:T(8,128)} %copy-done.5) | copy-start | bytes 3538948
  557.0 34.5 %copy-start.82 = (f32[768]{0:T(1024)S(1)}, f32[768]{0:T(1024)}, u32[]{:S(2)}) copy-start(f32[768]{0:T(1024)} %get-tuple-element.144) | copy-start | bytes 9220
  557.1 79.6 %all-gather.47.cloned.1.call-start = ((), (), s32[]{:S(2)}) async-start(), calls=%async_computation.44 | async-start | bytes 2506752 | tf_op jit(solution)/shard_map/all_gather | solution.py:88
  557.8 102.4 %all-gather.29.cloned.1.call-start = ((), (), s32[]{:S(2)}) async-start(), calls=%async_computation.22 | async-start | bytes 1769472 | tf_op jit(solution)/shard_map/all_gather | solution.py:94
  595.1 90.0 %all-gather.31.cloned.1.call-start = ((), (), s32[]{:S(2)}) async-start(), calls=%async_computation.24 | async-start | bytes 1769472 | tf_op jit(solution)/shard_map/all_gather | solution.py:94
  598.4 131.2 %all-gather.49.cloned.1.call-start = ((), (), s32[]{:S(2)}) async-start(), calls=%async_computation.45 | async-start | bytes 2506752 | tf_op jit(solution)/shard_map/all_gather | solution.py:89
  598.9 175.5 %reduce-scatter.25.cloned.1.call-start = ((), (), s32[]{:S(2)}) async-start(), calls=%async_computation.25 | async-start | bytes 3538944 | tf_op jit(solution)/shard_map/reduce_scatter | solution.py:98
  740.8 70.6 %reduce-scatter.23.cloned.1.call-start = ((), (), s32[]{:S(2)}) async-start(), calls=%async_computation.23 | async-start | bytes 3538944 | tf_op jit(solution)/shard_map/reduce_scatter | solution.py:98
  746.6 64.8 %copy-start.75 = (f32[768]{0:T(1024)S(1)}, f32[768]{0:T(1024)}, u32[]{:S(2)}) copy-start(f32[768]{0:T(1024)} %get-tuple-element.129) | copy-start | bytes 9220
  746.7 94.0 %all-gather.33.cloned.1.call-start = ((), (), s32[]{:S(2)}) async-start(), calls=%async_computation.26 | async-start | bytes 1769472 | tf_op jit(solution)/shard_map/all_gather | solution.py:94
  817.8 164.6 %reduce-scatter.27.cloned.1.call-start = ((), (), s32[]{:S(2)}) async-start(), calls=%async_computation.27 | async-start | bytes 3538944 | tf_op jit(solution)/shard_map/reduce_scatter | solution.py:98
  907.9 24.0 %collective-permute-start.5 = (bf16[768,768]{1,0:T(8,128)(2,1)}, bf16[768,768]{1,0:T(8,128)(2,1)}, u32[]{:S(2)}, u32[]{:S(2)}) collective-permute-start(bf16[768,768]{1,0:T(8,128)(2,1)} %copy.38), channel_id=1, source_target_pairs={{2,0},{4,2},{6,4},{8,6},{10,8},{12,10},{14,12},{16,14},{18,16},{20... | collective-permute-start | bytes 3538952 | tf_op jit(solution)/shard_map/ppermute | solution.py:28
  909.2 22.7 %collective-permute-start.4 = (bf16[768,768]{1,0:T(8,128)(2,1)}, bf16[768,768]{1,0:T(8,128)(2,1)}, u32[]{:S(2)}, u32[]{:S(2)}) collective-permute-start(bf16[768,768]{1,0:T(8,128)(2,1)} %copy.36), channel_id=1, source_target_pairs={{0,2},{2,4},{4,6},{6,8},{8,10},{10,12},{12,14},{14,16},{16,18},{18... | collective-permute-start | bytes 3538952 | tf_op jit(solution)/shard_map/ppermute | solution.py:28
  941.2 41.2 %copy-start.55 = (f32[768]{0:T(1024)S(1)}, f32[768]{0:T(1024)}, u32[]{:S(2)}) copy-start(f32[768]{0:T(1024)} %copy-done.54) | copy-start | bytes 9220
  941.2 41.2 %copy-start.63 = (f32[384]{0:T(512)S(1)}, f32[384]{0:T(512)}, u32[]{:S(2)}) copy-start(f32[384]{0:T(512)} %copy-done.62) | copy-start | bytes 4612
  941.2 41.2 %copy-start.72 = (f32[384]{0:T(512)S(1)}, f32[384]{0:T(512)}, u32[]{:S(2)}) copy-start(f32[384]{0:T(512)} %copy-done.71) | copy-start | bytes 4612
  941.2 69.7 %all-gather.35.cloned.1.call-start = ((), (), s32[]{:S(2)}) async-start(), calls=%async_computation.28 | async-start | bytes 1769472 | tf_op jit(solution)/shard_map/all_gather | solution.py:94
  986.1 24.9 %copy-start.89 = (f32[1536]{0:T(1024)S(1)}, f32[1536]{0:T(1024)}, u32[]{:S(2)}) copy-start(f32[1536]{0:T(1024)} %copy-done.88) | copy-start | bytes 18436
  988.0 69.1 %reduce-scatter.29.cloned.1.call-start = ((), (), s32[]{:S(2)}) async-start(), calls=%async_computation.29 | async-start | bytes 3538944 | tf_op jit(solution)/shard_map/reduce_scatter | solution.py:98
  1022.1 35.0 %copy-start.4 = (f32[384,768]{1,0:T(8,128)S(1)}, f32[384,768]{1,0:T(8,128)}, u32[]{:S(2)}) copy-start(f32[384,768]{1,0:T(8,128)} %copy-done.2) | copy-start | bytes 3538948
  1022.1 35.0 %copy-start.53 = (f32[768]{0:T(1024)S(1)}, f32[768]{0:T(1024)}, u32[]{:S(2)}) copy-start(f32[768]{0:T(1024)} %copy-done.52) | copy-start | bytes 9220
  1022.1 35.0 %copy-start.61 = (f32[384]{0:T(512)S(1)}, f32[384]{0:T(512)}, u32[]{:S(2)}) copy-start(f32[384]{0:T(512)} %copy-done.60) | copy-start | bytes 4612
  1022.1 35.0 %copy-start.70 = (f32[384]{0:T(512)S(1)}, f32[384]{0:T(512)}, u32[]{:S(2)}) copy-start(f32[384]{0:T(512)} %copy-done.69) | copy-start | bytes 4612
  1022.1 63.4 %all-gather.37.cloned.1.call-start = ((), (), s32[]{:S(2)}) async-start(), calls=%async_computation.30 | async-start | bytes 1769472 | tf_op jit(solution)/shard_map/all_gather | solution.py:94
  1060.8 24.8 %copy-start.29 = (bf16[1,384,768]{2,1,0:T(8,128)(2,1)S(1)}, bf16[1,384,768]{2,1,0:T(8,128)(2,1)}, u32[]{:S(2)}) copy-start(bf16[1,384,768]{2,1,0:T(8,128)(2,1)} %all-gather.1) | copy-start | bytes 1769476
  1062.6 24.9 %copy-start.23 = (bf16[6,64,768]{2,1,0:T(8,128)(2,1)S(1)}, bf16[6,64,768]{2,1,0:T(8,128)(2,1)}, u32[]{:S(2)}) copy-start(bf16[6,64,768]{2,1,0:T(8,128)(2,1)} %copy-done.22) | copy-start | bytes 1769476
  1062.7 25.0 %copy-start.73 = (f32[6,768]{1,0:T(8,128)S(1)}, f32[6,768]{1,0:T(8,128)}, u32[]{:S(2)}) copy-start(f32[6,768]{1,0:T(8,128)} %log_add_fusion.1) | copy-start | bytes 55300
  1062.7 179.0 %reduce-scatter.31.cloned.1.call-start = ((), (), s32[]{:S(2)}) async-start(), calls=%async_computation.31 | async-start | bytes 3538944 | tf_op jit(solution)/shard_map/reduce_scatter | solution.py:98
  1107.1 28.2 %copy-start.21 = (bf16[768,1,384]{0,2,1:T(8,128)(2,1)S(1)}, bf16[768,1,384]{0,2,1:T(8,128)(2,1)}, u32[]{:S(2)}) copy-start(bf16[768,1,384]{0,2,1:T(8,128)(2,1)} %copy-done.20) | copy-start | bytes 1769476
  1149.4 24.2 %collective-permute-start.7 = (bf16[768,768]{1,0:T(8,128)(2,1)}, bf16[768,768]{1,0:T(8,128)(2,1)S(1)}, u32[]{:S(2)}, u32[]{:S(2)}) collective-permute-start(bf16[768,768]{1,0:T(8,128)(2,1)} %copy.42), channel_id=1, source_target_pairs={{2,0},{4,2},{6,4},{8,6},{10,8},{12,10},{14,12},{16,14},{18,16},{20... | collective-permute-start | bytes 3538952 | tf_op jit(solution)/shard_map/ppermute | solution.py:28
  1150.7 22.9 %collective-permute-start.6 = (bf16[768,768]{1,0:T(8,128)(2,1)}, bf16[768,768]{1,0:T(8,128)(2,1)}, u32[]{:S(2)}, u32[]{:S(2)}) collective-permute-start(bf16[768,768]{1,0:T(8,128)(2,1)} %copy.40), channel_id=1, source_target_pairs={{0,2},{2,4},{4,6},{6,8},{8,10},{10,12},{12,14},{14,16},{16,18},{18... | collective-permute-start | bytes 3538952 | tf_op jit(solution)/shard_map/ppermute | solution.py:28
  1182.4 120.5 %reduce-scatter.47.cloned.1.call-start = ((), (), s32[]{:S(2)}) async-start(), calls=%async_computation.39 | async-start | bytes 5013504 | tf_op jit(solution)/shard_map/reduce_scatter | solution.py:342
  1189.5 191.9 %reduce-scatter.45.cloned.1.call-start = ((), (), s32[]{:S(2)}) async-start(), calls=%async_computation.38 | async-start | bytes 5013504 | tf_op jit(solution)/shard_map/reduce_scatter | solution.py:342
  1196.7 263.4 %reduce-scatter.43.cloned.1.call-start = ((), (), s32[]{:S(2)}) async-start(), calls=%async_computation.37 | async-start | bytes 5013504 | tf_op jit(solution)/shard_map/reduce_scatter | solution.py:341
  1203.9 334.7 %reduce-scatter.41.cloned.1.call-start = ((), (), s32[]{:S(2)}) async-start(), calls=%async_computation.36 | async-start | bytes 5013504 | tf_op jit(solution)/shard_map/reduce_scatter | solution.py:341
  1211.0 388.4 %reduce-scatter.39.cloned.1.call-start = ((), (), s32[]{:S(2)}) async-start(), calls=%async_computation.35 | async-start | bytes 1253376 | tf_op jit(solution)/shard_map/reduce_scatter | solution.py:340
  1214.1 446.2 %reduce-scatter.37.cloned.1.call-start = ((), (), s32[]{:S(2)}) async-start(), calls=%async_computation.34 | async-start | bytes 1253376 | tf_op jit(solution)/shard_map/reduce_scatter | solution.py:340
  1217.8 574.8 %all-reduce.3.cloned.1.call-start = ((), (), s32[]{:S(2)}) async-start(), calls=%async_computation.46 | async-start | bytes 147456 | tf_op jit(solution)/shard_map/psum | solution.py:344
  1246.0 621.6 %reduce-scatter.35.cloned.1.call-start = ((), (), s32[]{:S(2)}) async-start(), calls=%async_computation.33 | async-start | bytes 3760128 | tf_op jit(solution)/shard_map/reduce_scatter | solution.py:339
  1251.0 687.5 %reduce-scatter.33.cloned.1.call-start = ((), (), s32[]{:S(2)}) async-start(), calls=%async_computation.32 | async-start | bytes 3760128 | tf_op jit(solution)/shard_map/reduce_scatter | solution.py:339
  1260.2 401.8 %copy-start.87 = (f32[384]{0:T(512)S(1)}, f32[384]{0:T(512)}, u32[]{:S(2)}) copy-start(f32[384]{0:T(512)} %get-tuple-element.102) | copy-start | bytes 4612
  1260.2 401.7 %copy-start.86 = (f32[384]{0:T(512)S(1)}, f32[384]{0:T(512)}, u32[]{:S(2)}) copy-start(f32[384]{0:T(512)} %get-tuple-element.124) | copy-start | bytes 4612
  1260.2 401.8 %copy-start.13 = (f32[384,768]{1,0:T(8,128)S(1)}, f32[384,768]{1,0:T(8,128)}, u32[]{:S(2)}) copy-start(f32[384,768]{1,0:T(8,128)} %copy-done.12) | copy-start | bytes 3538948
  (72 other events, 273.7 us)
Sparse Core Ops, SparseCore 0:
  10.9 43.1 all-gather.38
  56.2 21.4 all-gather.22
  196.0 34.2 reduce-scatter.16
  233.1 42.2 all-gather.40
  277.3 21.4 all-gather.24
  301.6 42.2 all-gather.42
  349.9 33.5 reduce-scatter.18
  385.7 40.4 all-gather.44
  428.3 21.4 all-gather.26
  557.2 34.2 reduce-scatter.20
  594.4 42.2 all-gather.46
  638.7 21.4 all-gather.28
  662.3 22.7 all-gather.30
  687.2 42.2 all-gather.48
  740.9 33.5 reduce-scatter.24
  776.6 34.7 reduce-scatter.22
  817.9 22.7 all-gather.32
  941.3 41.0 reduce-scatter.26
  988.1 22.7 all-gather.34
  1022.3 34.7 reduce-scatter.28
  1062.8 22.7 all-gather.36
  1182.5 40.8 reduce-scatter.30
  1227.3 75.5 reduce-scatter.46
  1306.6 74.7 reduce-scatter.44
  1385.3 74.7 reduce-scatter.42
  1463.8 74.7 reduce-scatter.40
  1542.1 57.3 reduce-scatter.38
  1603.1 57.1 reduce-scatter.36
  1667.9 124.6 all-reduce.2
  1796.3 71.2 reduce-scatter.34
  1871.5 66.9 reduce-scatter.32
where the time goes:
time: 1950 us
  waiting for transfers between devices  1310 us (67%)
  matrix products  312 us (16%)
  other arithmetic  129 us (7%)
  blocking collectives  78.8 us (4%)
  local copies, waits for them, and re-layouts  73.5 us (4%)
  starting transfers between devices  23.8 us (1%)
    reduce_scatter x8, waiting for transfers between devices, sum_rows(): lax.psum_scatter(jnp.dot(left, right, preferred_element_type=jnp.float32)...  236 us
    all_gather x8, waiting for transfers between devices, gather_rows(): return lax.all_gather(values, 'mp', axis=0, tiled=True)  175 us
    reduce_scatter x2, waiting for transfers between devices, body(): lax.psum_scatter(mats_grad[2], 'dp', scatter_dimension=0, tiled=True)  155 us
    reduce_scatter x2, waiting for transfers between devices, body(): lax.psum_scatter(mats_grad[0], 'dp', scatter_dimension=0, tiled=True)  139 us
    psum x1, waiting for transfers between devices, body(): lax.psum((small[0], small[1], small[2], small[3], small[4]), ('dp', 'mp'))  128 us
    reduce_scatter x2, waiting for transfers between devices, body(): lax.psum_scatter(mats_grad[3], 'dp', scatter_dimension=0, tiled=True)  121 us
    reduce_scatter x2, waiting for transfers between devices, body(): lax.psum_scatter(mats_grad[1], 'dp', scatter_dimension=0, tiled=True)  120 us
    all_gather x2, waiting for transfers between devices, fetch_weights(): lax.all_gather(down_weight[depth], 'dp', axis=0, tiled=True)  82.5 us
  transfers between devices with their start and end apart: 39, of which 30 were waited for; matrix products, arithmetic and copies ran while one was open for 9% of the time, Pallas kernels for 0%

commit v1 on v0

v1 whole, which is shorter than its diff:
```python
import jax, jax.numpy as jnp, functools
from jax import lax
from jax.experimental import pallas as pl
from jax.experimental.pallas import tpu as pltpu
from jax.sharding import Mesh, PartitionSpec as P
MESH = pl.DeviceIdType.MESH
f32 = jnp.float32
bf16 = jnp.bfloat16
EPS = 1e-05
VMEM = pl.BlockSpec(memory_space=pltpu.VMEM)

def place():
    return tuple(lax.axis_index(n) for n in ("z", "x", "core", "y"))

def chips():
    return lax.axis_size("z") * 4

def gather_kernel(count, y_first, *refs):
    n = len(y_first)
    ins, outs = refs[:n], refs[n+1:2*n+1]
    bias_in, bias_out = refs[n], refs[2*n+1]
    up_sem, down_sem, side_sem, mate_sem, recv_sem, own_send, own_recv, copy_sem, bias_sem = refs[2*n+2:]
    z, x, core, y = place()
    rows = count // 4
    quad = 2 * z + x
    dp = 2 * quad + core
    head = core == y
    sibling = (z, x, 1 - core, y)
    side = (z, 1 - x, core, y)
    above = (z + 1, x, core, y)
    below = (z - 1, x, core, y)
    mate = (z, x, core, 1 - y)
    has_up = z + 1 < rows
    has_down = z > 0
    bar = pltpu.get_barrier_semaphore()
    def sig(dev): pl.semaphore_signal(bar, inc=1, device_id=dev, device_id_type=MESH)
    sig(side)
    @pl.when(has_up)
    def _(): sig(above)
    @pl.when(has_down)
    def _(): sig(below)
    @pl.when(head)
    def _(): sig(sibling)
    @pl.when(jnp.logical_not(head))
    def _(): sig(mate)
    pl.semaphore_wait(bar, 2 + has_up.astype(jnp.int32) + has_down.astype(jnp.int32))

    def piece(m, q, sem, dev):
        part = outs[m].at[pl.ds(2 * q, 2)]
        return pltpu.make_async_remote_copy(part, part, sem.at[m, q], recv_sem.at[m, q], device_id=dev, device_id_type=MESH)

    bias_copy = pltpu.make_async_remote_copy(bias_in, bias_out, bias_sem.at[0], bias_sem.at[1], device_id=mate, device_id_type=MESH)
    @pl.when(head)
    def _():
        bias_copy.start()
        bias_out[...] = bias_in[...]
    @pl.when(jnp.logical_not(head))
    def _():
        for m in range(n):
            pltpu.make_async_remote_copy(ins[m], outs[m].at[dp], own_send.at[m], own_recv.at[m], device_id=sibling, device_id_type=MESH).start()
    def spread(m, q, up, down, across, to_mate):
        @pl.when(up)
        def _(): piece(m, q, up_sem, above).start()
        @pl.when(down)
        def _(): piece(m, q, down_sem, below).start()
        if across: piece(m, q, side_sem, side).start()
        if to_mate: piece(m, q, mate_sem, mate).start()
    def arrive(m, q): piece(m, q, up_sem, above).wait_recv()

    @pl.when(head)
    def _():
        for m in range(n):
            pltpu.make_async_copy(ins[m], outs[m].at[dp], copy_sem.at[m]).start()
        for m in range(n):
            pltpu.make_async_copy(ins[m], outs[m].at[dp], copy_sem.at[m]).wait()
            pltpu.make_async_remote_copy(ins[m], outs[m].at[dp + 1 - 2 * core], own_send.at[m], own_recv.at[m], device_id=sibling, device_id_type=MESH).wait_recv()
            spread(m, quad, has_up, has_down, True, True)

    def line(ms, last):
        def step(k, _):
            for m in ms:
                @pl.when(z - k >= 0)
                def _():
                    q = quad - 2 * k
                    arrive(m, q)
                    spread(m, q, has_up, False, True, last)
                @pl.when(z + k < rows)
                def _():
                    q = quad + 2 * k
                    arrive(m, q)
                    spread(m, q, False, has_down, True, last)
                if last:
                    @pl.when(z - k + 1 >= 0)
                    def _():
                        q = side_quad - 2 * (k - 1)
                        arrive(m, q)
                        spread(m, q, False, False, False, True)
                    @pl.when((z + k - 1 < rows) & (k > 1))
                    def _():
                        q = side_quad + 2 * (k - 1)
                        arrive(m, q)
                        spread(m, q, False, False, False, True)
            return 0
        lax.fori_loop(1, rows + (1 if last else 0), step, 0)
    side_quad = quad + 1 - 2 * x
    first = [m for m in range(n) if y_first[m]]
    later = [m for m in range(n) if not y_first[m]]
    @pl.when(head)
    def _():
        line(first, False)
        line(later, True)
    @pl.when(jnp.logical_not(head))
    def _():
        for m in first:
            arrive(m, quad)
            spread(m, quad, has_up, has_down, True, False)
        line(first, False)
        def step(q, _):
            for m in later: arrive(m, q)
            return 0
        lax.fori_loop(0, count // 2, step, 0)
    def step(k, _):
        for m in first: arrive(m, 2 * k + 1 - x)
        return 0
    lax.fori_loop(0, rows, step, 0)
    @pl.when(head)
    def _(): bias_copy.wait_send()
    @pl.when(jnp.logical_not(head))
    def _(): bias_copy.wait_recv()
    def step(k, _):
        for m in range(n):
            fam = head if not y_first[m] else True
            @pl.when(fam & (k <= z) & has_up)
            def _(): piece(m, 2 * k + x, up_sem, above).wait_send()
            @pl.when(fam & (k >= z) & has_down)
            def _(): piece(m, 2 * k + x, down_sem, below).wait_send()
            @pl.when(fam)
            def _(): piece(m, 2 * k + x, side_sem, side).wait_send()
            if not y_first[m]:
                @pl.when(head)
                def _():
                    piece(m, 2 * k, mate_sem, mate).wait_send()
                    piece(m, 2 * k + 1, mate_sem, mate).wait_send()
            else:
                @pl.when(head & (k == z))
                def _(): piece(m, quad, mate_sem, mate).wait_send()
        return 0
    lax.fori_loop(0, rows, step, 0)
    @pl.when(jnp.logical_not(head))
    def _():
        for m in range(n):
            pltpu.make_async_remote_copy(ins[m], outs[m].at[dp], own_send.at[m], own_recv.at[m], device_id=sibling, device_id_type=MESH).wait_send()

def gather(shards, bias, y_first, cid):
    count = chips()
    n = len(shards)
    dma = pltpu.SemaphoreType.DMA
    return pl.pallas_call(
        functools.partial(gather_kernel, count, y_first),
        out_shape=[jax.ShapeDtypeStruct((count,) + s.shape, s.dtype) for s in shards] + [jax.ShapeDtypeStruct(bias.shape, f32)],
        in_specs=[VMEM] * (n + 1),
        out_specs=[pl.BlockSpec(memory_space=pl.ANY)] * n + [VMEM],
        scratch_shapes=[dma((n, count // 2))] * 5 + [dma((n,))] * 3 + [dma((2,))],
        compiler_params=pltpu.CompilerParams(collective_id=cid, has_side_effects=True),
    )(*shards, bias)

def rcopy(src, dst, send, recv, dev):
    return pltpu.make_async_remote_copy(src, dst, send, recv, device_id=dev, device_id_type=MESH)

def ready(devs):
    bar = pltpu.get_barrier_semaphore()
    for dev, ok in devs:
        if ok is True:
            pl.semaphore_signal(bar, inc=1, device_id=dev, device_id_type=MESH)
        else:
            @pl.when(ok)
            def _(): pl.semaphore_signal(bar, inc=1, device_id=dev, device_id_type=MESH)
    return bar

def as_int(v): return v.astype(jnp.int32)

def halo_kernel(count, a_ref, win, sib_s, mate_s, far_s, recv, own_s):
    z, x, core, y = place()
    quad, quads = 2 * z + x, count // 2
    at_quad = lambda q: (q // 2, lax.rem(q, 2), core, y)
    sibling, mate = (z, x, 1 - core, y), (z, x, core, 1 - y)
    is1 = core == 1
    target, source = at_quad(quad - 1 + 2 * core), at_quad(quad + 1 - 2 * core)
    has_target = jnp.where(is1, quad + 1 < quads, quad > 0)
    has_source = jnp.where(is1, quad > 0, quad + 1 < quads)
    bar = ready([(sibling, True), (mate, True), (source, has_source)])
    own = 2 + 2 * core
    from_mate = 2 * core + 3 - 2 * y
    far = 6 - 6 * core
    passes = (core == y) & has_source
    extra = 5 - 4 * core
    takes = (core != y) & has_source
    @pl.when(quad == 0)
    def _():
        win[0] = jnp.zeros_like(win[0])
        @pl.when(y == 0)
        def _(): win[1] = jnp.zeros_like(win[1])
    @pl.when(quad == quads - 1)
    def _():
        win[6] = jnp.zeros_like(win[6])
        @pl.when(y == 1)
        def _(): win[5] = jnp.zeros_like(win[5])
    pl.semaphore_wait(bar, 2 + as_int(has_target))
    to_far = rcopy(a_ref, win.at[far], far_s.at[0], recv.at[far], target)
    to_mate = rcopy(a_ref, win.at[2 * core + 1 + 2 * y], mate_s.at[0], recv.at[2 * core + 1 + 2 * y], mate)
    to_sib = rcopy(a_ref, win.at[own], sib_s.at[own], recv.at[own], sibling)
    on = lambda w: rcopy(win.at[w], win.at[w], sib_s.at[w], recv.at[w], sibling)
    hand = rcopy(win.at[far], win.at[extra], mate_s.at[1], recv.at[extra], mate)
    @pl.when(has_target)
    def _(): to_far.start()
    to_mate.start()
    to_sib.start()
    win[own] = a_ref[...]
    on(from_mate).wait_recv()
    on(from_mate).start()
    @pl.when(has_source)
    def _():
        on(far).wait_recv()
        @pl.when(passes)
        def _(): hand.start()
        on(far).start()
    @pl.when(takes)
    def _():
        on(extra).wait_recv()
        on(extra).start()
    oc = 1 - core
    on(2 + 2 * oc).wait_recv()
    on(2 * oc + 3 - 2 * y).wait_recv()
    sib_source = jnp.where(is1, quad + 1 < quads, quad > 0)
    @pl.when(sib_source)
    def _():
        on(6 - 6 * oc).wait_recv()
    @pl.when(sib_source & (oc != y))
    def _(): on(5 - 4 * oc).wait_recv()
    @pl.when(has_target)
    def _(): to_far.wait_send()
    to_mate.wait_send()
    to_sib.wait_send()
    on(from_mate).wait_send()
    @pl.when(has_source)
    def _(): on(far).wait_send()
    @pl.when(passes)
    def _(): hand.wait_send()
    @pl.when(takes)
    def _(): on(extra).wait_send()

def halo(a, cid):
    count = chips()
    dma = pltpu.SemaphoreType.DMA
    return pl.pallas_call(
        functools.partial(halo_kernel, count),
        out_shape=jax.ShapeDtypeStruct((7,) + a.shape, a.dtype),
        in_specs=[VMEM], out_specs=VMEM,
        scratch_shapes=[dma((7,)), dma((2,)), dma((1,)), dma((7,)), dma((1,))],
        compiler_params=pltpu.CompilerParams(collective_id=cid, has_side_effects=True, vmem_limit_bytes=60 << 20),
    )(a)

def halo_back_kernel(count, p, out, sib_in, mate_in, far_in, stage, sib_s, sib_r, mate_s, mate_r, far_s, far_r):
    z, x, core, y = place()
    quad, quads = 2 * z + x, count // 2
    at_quad = lambda q: (q // 2, lax.rem(q, 2), core, y)
    sibling, mate = (z, x, 1 - core, y), (z, x, core, 1 - y)
    is1 = core == 1
    source, target = at_quad(quad - 1 + 2 * core), at_quad(quad + 1 - 2 * core)
    has_source = jnp.where(is1, quad + 1 < quads, quad > 0)
    has_target = jnp.where(is1, quad > 0, quad + 1 < quads)
    bar = ready([(sibling, True), (mate, True), (source, has_source)])
    pl.semaphore_wait(bar, 2 + as_int(has_target))
    own = 2 + 2 * core
    to_sib = lambda w: rcopy(p.at[w], sib_in.at[w], sib_s.at[w], sib_r.at[w], sibling)
    oc = 1 - core
    direct = lambda c: 2 * c + 3 - 2 * y
    far = lambda c: 6 - 6 * c
    extra = lambda c: 5 - 4 * c
    gives = (core != y) & has_target
    gets = (core == y) & has_target
    sib_has = has_source
    @pl.when(sib_has & (oc != y))
    def _(): to_sib(extra(oc)).start()
    to_sib(direct(oc)).start()
    @pl.when(sib_has)
    def _(): to_sib(far(oc)).start()
    to_sib(2 + 2 * oc).start()
    hand = rcopy(stage.at[0], mate_in.at[0], mate_s.at[0], mate_r.at[0], mate)
    to_mate = rcopy(stage.at[1], mate_in.at[1], mate_s.at[1], mate_r.at[1], mate)
    to_far = rcopy(stage.at[2], far_in, far_s.at[0], far_r.at[0], target)
    both = lambda w: p[w].astype(f32) + sib_in[w].astype(f32)
    @pl.when(gives)
    def _():
        to_sib(extra(core)).wait_recv()
        stage[0] = both(extra(core)).astype(bf16)
        hand.start()
    to_sib(direct(core)).wait_recv()
    stage[1] = both(direct(core)).astype(bf16)
    to_mate.start()
    @pl.when(has_target)
    def _():
        to_sib(far(core)).wait_recv()
        @pl.when(gets)
        def _():
            hand.wait_recv()
            stage[2] = (both(far(core)) + mate_in[0].astype(f32)).astype(bf16)
        @pl.when(core != y)
        def _(): stage[2] = both(far(core)).astype(bf16)
        to_far.start()
    to_sib(own).wait_recv()
    to_mate.wait_recv()
    out[...] = both(own) + mate_in[1].astype(f32)
    @pl.when(has_source)
    def _():
        to_far.wait_recv()
        out[...] = out[...] + far_in[...].astype(f32)
    @pl.when(sib_has & (oc != y))
    def _(): to_sib(extra(oc)).wait_send()
    to_sib(direct(oc)).wait_send()
    @pl.when(sib_has)
    def _(): to_sib(far(oc)).wait_send()
    to_sib(2 + 2 * oc).wait_send()
    @pl.when(gives)
    def _(): hand.wait_send()
    to_mate.wait_send()
    @pl.when(has_target)
    def _(): to_far.wait_send()

def halo_back(p, cid):
    count = chips()
    dma = pltpu.SemaphoreType.DMA
    one = p.shape[1:]
    return pl.pallas_call(
        functools.partial(halo_back_kernel, count),
        out_shape=jax.ShapeDtypeStruct(one, f32),
        in_specs=[VMEM], out_specs=VMEM,
        scratch_shapes=[pltpu.VMEM((7,) + one, bf16), pltpu.VMEM((2,) + one, bf16), pltpu.VMEM(one, bf16), pltpu.VMEM((3,) + one, bf16),
                        dma((7,)), dma((7,)), dma((2,)), dma((2,)), dma((1,)), dma((1,))],
        compiler_params=pltpu.CompilerParams(collective_id=cid, has_side_effects=True, vmem_limit_bytes=60 << 20),
    )(p)

def pair_gather_kernel(a_ref, out, send, recv):
    z, x, core, y = place()
    sibling = (z, x, 1 - core, y)
    pl.semaphore_wait(ready([(sibling, True)]), 1)
    copy = rcopy(a_ref, out.at[core], send, recv, sibling)
    copy.start()
    out[core] = a_ref[...]
    copy.wait()

def pair_gather(a, cid):
    return pl.pallas_call(
        pair_gather_kernel, out_shape=jax.ShapeDtypeStruct((2,) + a.shape, a.dtype), in_specs=[VMEM], out_specs=VMEM,
        scratch_shapes=[pltpu.SemaphoreType.DMA, pltpu.SemaphoreType.DMA],
        compiler_params=pltpu.CompilerParams(collective_id=cid, has_side_effects=True),
    )(a)

def pair_sum_kernel(p_ref, out, got, send, recv):
    z, x, core, y = place()
    sibling = (z, x, 1 - core, y)
    pl.semaphore_wait(ready([(sibling, True)]), 1)
    copy = rcopy(p_ref.at[1 - core], got, send, recv, sibling)
    copy.start()
    copy.wait()
    out[...] = p_ref[core] + got[...]

def pair_sum(p, cid):
    return pl.pallas_call(
        pair_sum_kernel, out_shape=jax.ShapeDtypeStruct(p.shape[1:], p.dtype), in_specs=[VMEM], out_specs=VMEM,
        scratch_shapes=[pltpu.VMEM(p.shape[1:], p.dtype), pltpu.SemaphoreType.DMA, pltpu.SemaphoreType.DMA],
        compiler_params=pltpu.CompilerParams(collective_id=cid, has_side_effects=True),
    )(p)


def reduce_kernel(count, early, *refs):
    n = len(early)
    rows = count // 4
    grads, outs = refs[:n], refs[n:2*n]
    k = 2*n
    mate_in, side_out, side_in, line_out, up_in, down_in, final_out = [refs[k+i*n:k+(i+1)*n] for i in range(7)]
    k += 7*n
    (mate_s, mate_r, side_s, side_r, up_s, up_r, down_s, down_r, last_s, last_r) = refs[k:]
    z, x, core, y = place()
    quad = 2 * z + x
    dp = 2 * quad + core
    head = core == y
    other = jnp.logical_not(head)
    sibling = (z, x, 1 - core, y)
    side = (z, 1 - x, core, y)
    above = (z + 1, x, core, y)
    below = (z - 1, x, core, y)
    mate = (z, x, core, 1 - y)
    has_up = z + 1 < rows
    has_down = z > 0
    for m in range(n):
        @pl.when(z == 0)
        def _(): up_in[m][...] = jnp.zeros_like(up_in[m])
        @pl.when(z == rows - 1)
        def _(): down_in[m][...] = jnp.zeros_like(down_in[m])
    bar = pltpu.get_barrier_semaphore()
    def sig(dev): pl.semaphore_signal(bar, inc=1, device_id=dev, device_id_type=MESH)
    sig(side)
    @pl.when(has_up)
    def _(): sig(above)
    @pl.when(has_down)
    def _(): sig(below)
    @pl.when(head)
    def _(): sig(mate)
    @pl.when(other)
    def _(): sig(sibling)
    pl.semaphore_wait(bar, 2 + has_up.astype(jnp.int32) + has_down.astype(jnp.int32))

    def rc(src, dst, s, r, dev):
        return pltpu.make_async_remote_copy(src, dst, s, r, device_id=dev, device_id_type=MESH)
    def to_mate(m, q):
        return rc(grads[m].at[pl.ds(2*q, 2)], mate_in[m].at[pl.ds(2*q, 2)], mate_s.at[m, q], mate_r.at[m, q], mate)
    def to_side(m, j):
        return rc(side_out[m].at[j], side_in[m].at[j], side_s.at[m, j], side_r.at[m, j], side)
    def to_up(m, j):
        return rc(line_out[m].at[j], up_in[m].at[j], up_s.at[m, j], up_r.at[m, j], above)
    def to_down(m, j):
        return rc(line_out[m].at[j], down_in[m].at[j], down_s.at[m, j], down_r.at[m, j], below)
    def late_mate(m):
        return rc(line_out[m].at[z], mate_in[m], mate_s.at[m, quad], mate_r.at[m, quad], mate)
    def last(m):
        return rc(final_out[m], outs[m], last_s.at[m], last_r.at[m], sibling)

    def far_first(fn):
        def step(i, _):
            d = rows - i
            for j, ok in ((z + d, z + d < rows), (z - d, z - d >= 0)):
                @pl.when(ok)
                def _(): fn(j)
            return 0
        lax.fori_loop(1, rows, step, 0)
        fn(z)

    order = [m for m in range(n) if early[m]], [m for m in range(n) if not early[m]]

    @pl.when(other)
    def _():
        def go(j):
            for m in order[0]:
                to_mate(m, 2 * j + 1 - x).start()
        def go2(j):
            for m in order[0]:
                to_mate(m, 2 * j + x).start()
        far_first(go); far_first(go2)

    def own(m, q, c, with_mate):
        t = grads[m][2*q+c].astype(f32)
        return t + mate_in[m][2*q+c].astype(f32) if with_mate else t

    def side_stage(ms, with_mate):
        def go(j):
            q = 2 * j + 1 - x
            for m in ms:
                if with_mate: to_mate(m, q).wait_recv()
                def half(c, _):
                    side_out[m][j, c] = own(m, q, c, with_mate).astype(bf16)
                    return 0
                lax.fori_loop(0, 2, half, 0)
            for m in ms:
                to_side(m, j).start()
        far_first(go)

    def line_stage(ms, with_mate):
        def go(j):
            q = 2 * j + x
            for m in ms:
                if with_mate: to_mate(m, q).wait_recv()
                to_side(m, j).wait_recv()
                @pl.when((j >= z) & has_down)
                def _(): to_up(m, j).wait_recv()
                @pl.when((j <= z) & has_up)
                def _(): to_down(m, j).wait_recv()
                def half(c, _):
                    t = own(m, q, c, with_mate) + side_in[m][j, c].astype(f32)
                    @pl.when(j > z)
                    def _(): line_out[m][j, c] = (t + up_in[m][j, c].astype(f32)).astype(bf16)
                    @pl.when(j < z)
                    def _(): line_out[m][j, c] = (t + down_in[m][j, c].astype(f32)).astype(bf16)
                    @pl.when(j == z)
                    def _():
                        u = t + up_in[m][j, c].astype(f32) + down_in[m][j, c].astype(f32)
                        if with_mate:
                            @pl.when(c == core)
                            def _(): outs[m][...] = u
                            @pl.when(c != core)
                            def _(): final_out[m][...] = u
                        else:
                            @pl.when(other)
                            def _(): line_out[m][j, c] = u.astype(bf16)
                            @pl.when(head & (c == core))
                            def _(): outs[m][...] = u
                            @pl.when(head & (c != core))
                            def _(): final_out[m][...] = u
                    return 0
                lax.fori_loop(0, 2, half, 0)
            for m in ms:
                @pl.when(j > z)
                def _(): to_up(m, j).start()
                @pl.when(j < z)
                def _(): to_down(m, j).start()
        far_first(go)

    side_stage(order[1], False)
    @pl.when(head)
    def _(): side_stage(order[0], True)
    line_stage(order[1], False)
    @pl.when(other)
    def _():
        for m in order[1]: late_mate(m).start()
    @pl.when(head)
    def _():
        line_stage(order[0], True)
        for m in order[1]:
            late_mate(m).wait_recv()
            outs[m][...] = outs[m][...] + mate_in[m][core].astype(f32)
            final_out[m][...] = final_out[m][...] + mate_in[m][1 - core].astype(f32)
        for m in range(n):
            last(m).start()
    @pl.when(other)
    def _():
        for m in range(n): last(m).wait_recv()
    def step(j, _):
        for m in range(n):
            fam = head if early[m] else True
            @pl.when(fam)
            def _(): to_side(m, j).wait_send()
            @pl.when(fam & (j > z))
            def _(): to_up(m, j).wait_send()
            @pl.when(fam & (j < z))
            def _(): to_down(m, j).wait_send()
            if early[m]:
                @pl.when(other)
                def _():
                    to_mate(m, 2 * j).wait_send()
                    to_mate(m, 2 * j + 1).wait_send()
        return 0
    lax.fori_loop(0, rows, step, 0)
    for m in range(n):
        @pl.when(head)
        def _(): last(m).wait_send()
        if not early[m]:
            @pl.when(other)
            def _(): late_mate(m).wait_send()

def scatter_sum(grads, early, cid):
    count = chips()
    n = len(grads)
    rows = count // 4
    dma = pltpu.SemaphoreType.DMA
    quads = [pltpu.VMEM((rows, 2) + g.shape[1:], bf16) for g in grads]
    mates = [pltpu.VMEM(((count if e else 2),) + g.shape[1:], bf16) for g, e in zip(grads, early)]
    lasts = [pltpu.VMEM(g.shape[1:], f32) for g in grads]
    return pl.pallas_call(
        functools.partial(reduce_kernel, count, early),
        out_shape=[jax.ShapeDtypeStruct(g.shape[1:], f32) for g in grads],
        in_specs=[pl.BlockSpec(memory_space=pltpu.VMEM)] * n,
        out_specs=[pl.BlockSpec(memory_space=pltpu.VMEM)] * n,
        scratch_shapes=mates + quads * 5 + lasts + [dma((n, count // 2))] * 2 + [dma((n, rows))] * 6 + [dma((n,))] * 2,
        compiler_params=pltpu.CompilerParams(collective_id=cid, has_side_effects=True, vmem_limit_bytes=60 << 20),
    )(*grads)
TQ, TK, BQ, BK = 384, 512, 384, 512
NEG = -1e30

def nt(a, b):
    return lax.dot_general(a, b, (((1,), (1,)), ((), ())), preferred_element_type=f32)
def tn(a, b):
    return lax.dot_general(a, b, (((0,), (0,)), ((), ())), preferred_element_type=f32)

def fold(t, op):
    out = t[:, :128]
    for i in range(1, t.shape[1] // 128):
        out = op(out, t[:, i*128:(i+1)*128])
    return out

def tiled(t, n):
    return t if n == 128 else jnp.concatenate([t] * (n // 128), axis=1)

def tile_at(lo, j, size, wide):
    want = lo + j * size
    start = jnp.minimum(want, wide - size)
    return pl.multiple_of(start, 128), want - start

def fwd_kernel(half, span_ref, q_ref, k_ref, v_ref, idq_ref, idk_ref, o_ref, lse_ref, s_scr, m_scr, l_scr, acc):
    i = pl.program_id(0)
    T = q_ref.shape[0]
    pairs = q_ref.shape[1] // 128
    wide = k_ref.shape[0]
    lo, steps = span_ref[0, i], span_ref[1, i]
    low = lax.broadcasted_iota(jnp.int32, (T, 128), 1) < 64
    qs = []
    for p in range(pairs):
        qp = q_ref[:, p*128:(p+1)*128] * jnp.bfloat16(0.125)
        z = jnp.zeros_like(qp)
        qs += [jnp.where(low, qp, z), jnp.where(low, z, qp)]
    gap = 2 * half + i * T + jnp.where(i >= half // T, half, 0)
    idq = idq_ref[...]
    col = lax.broadcasted_iota(jnp.int32, (T, TK), 1)
    rel = col - lax.broadcasted_iota(jnp.int32, (T, TK), 0)
    for h in range(2 * pairs):
        m_scr[h] = jnp.full((T, 128), NEG, f32)
        l_scr[h] = jnp.zeros((T, 128), f32)
    for p in range(pairs):
        acc[p] = jnp.zeros((T, 128), f32)
    def scores(j, _):
        start, fresh = tile_at(lo, j, TK, wide)
        ok = ((idq == idk_ref[0:1, pl.ds(start, TK)]) | (rel == gap - start)) & (col >= fresh)
        for h in range(2 * pairs):
            p = h // 2
            s = jnp.where(ok, nt(qs[h], k_ref[pl.ds(start, TK), p*128:(p+1)*128]), NEG)
            s_scr[h, j] = s
            m_scr[h] = jnp.maximum(m_scr[h], fold(s, jnp.maximum))
        return 0
    lax.fori_loop(0, steps, scores, 0)
    for h in range(2 * pairs):
        m_scr[h] = jnp.broadcast_to(jnp.max(m_scr[h], axis=1, keepdims=True), (T, 128))
    def values(j, _):
        start, fresh = tile_at(lo, j, TK, wide)
        for p in range(pairs):
            vp = v_ref[pl.ds(start, TK), p*128:(p+1)*128]
            out = []
            for h in (2*p, 2*p+1):
                e = jnp.exp(s_scr[h, j] - tiled(m_scr[h], TK))
                l_scr[h] = l_scr[h] + fold(e, jnp.add)
                out.append(jnp.dot(e.astype(bf16), vp, preferred_element_type=f32))
            acc[p] = acc[p] + jnp.where(low, out[0], out[1])
        return 0
    lax.fori_loop(0, steps, values, 0)
    for p in range(pairs):
        inv = [1.0 / jnp.sum(l_scr[h], axis=1, keepdims=True) for h in (2*p, 2*p+1)]
        o_ref[:, p*128:(p+1)*128] = (acc[p] * jnp.where(low, inv[0], inv[1])).astype(bf16)
    for h in range(2 * pairs):
        total = jnp.sum(l_scr[h].T, axis=0, keepdims=True)
        lse_ref[h:h+1, :] = m_scr[h].T[0:1, :] + jnp.log(total)

def attend(q, k, v, span, idq, idk):
    rows, cols = q.shape
    wide = k.shape[0]
    heads = cols // 64
    tiles = rows // TQ
    full = lambda a: pl.BlockSpec(a.shape, lambda i, s: (0,) * a.ndim)
    most = (4 * (rows // 2) + TQ + TK) // TK + 1
    return pl.pallas_call(
        functools.partial(fwd_kernel, rows // 2),
        grid_spec=pltpu.PrefetchScalarGridSpec(
            num_scalar_prefetch=1, grid=(tiles,),
            in_specs=[pl.BlockSpec((TQ, cols), lambda i, s: (i, 0)), full(k), full(v),
                      pl.BlockSpec((TQ, 1), lambda i, s: (i, 0)), full(idk)],
            out_specs=[pl.BlockSpec((TQ, cols), lambda i, s: (i, 0)), pl.BlockSpec((heads, TQ), lambda i, s: (0, i))],
            scratch_shapes=[pltpu.VMEM((heads, most, TQ, TK), f32), pltpu.VMEM((heads, TQ, 128), f32), pltpu.VMEM((heads, TQ, 128), f32),
                            pltpu.VMEM((heads // 2, TQ, 128), f32)]),
        out_shape=[jax.ShapeDtypeStruct((rows, cols), bf16), jax.ShapeDtypeStruct((heads, rows), f32)],
        compiler_params=pltpu.CompilerParams(vmem_limit_bytes=60 << 20, dimension_semantics=("arbitrary",)),
        cost_estimate=pl.CostEstimate(flops=4*rows*wide*cols, bytes_accessed=6*wide*cols, transcendentals=0),
    )(span, q, k, v, idq, idk)

def bwd_kernel(half, span_ref, q_ref, k_ref, v_ref, o_ref, da_ref, lse_ref, idq_ref, idk_ref, dq_ref, dk_ref, dv_ref, dk_acc, dv_acc, dq_acc):
    i = pl.program_id(0)
    T = q_ref.shape[0]
    pairs = q_ref.shape[1] // 128
    wide = k_ref.shape[0]
    lo, steps = span_ref[0, i], span_ref[1, i]
    low = lax.broadcasted_iota(jnp.int32, (T, 128), 1) < 64
    @pl.when(i == 0)
    def _():
        dk_acc[...] = jnp.zeros_like(dk_acc)
        dv_acc[...] = jnp.zeros_like(dv_acc)
    qs, das, delta = [], [], []
    for p in range(pairs):
        at = slice(p*128, (p+1)*128)
        qp = q_ref[:, at] * jnp.bfloat16(0.125)
        dp = da_ref[:, at]
        z = jnp.zeros_like(qp)
        qs += [jnp.where(low, qp, z), jnp.where(low, z, qp)]
        das += [jnp.where(low, dp, z), jnp.where(low, z, dp)]
        t = (dp.astype(f32) * o_ref[:, at].astype(f32)).T
        delta += [jnp.sum(t[:64], axis=0, keepdims=True), jnp.sum(t[64:], axis=0, keepdims=True)]
        dq_acc[p] = jnp.zeros((T, 128), f32)
    gap = 2 * half + i * T + jnp.where(i >= half // T, half, 0)
    idq = idq_ref[...]
    row = lax.broadcasted_iota(jnp.int32, (BK, T), 0)
    rel = row - lax.broadcasted_iota(jnp.int32, (BK, T), 1)
    def tile(j, _):
        start, fresh = tile_at(lo, j, BK, wide)
        at_rows = pl.ds(start, BK)
        ok = ((idk_ref[at_rows, :] == idq) | (rel == gap - start)) & (row >= fresh)
        for p in range(pairs):
            at = slice(p*128, (p+1)*128)
            kp, vp = k_ref[at_rows, at], v_ref[at_rows, at]
            kx = kp * jnp.bfloat16(0.125)
            dk = dv = 0
            dq = []
            for h in (2*p, 2*p+1):
                s = jnp.where(ok, nt(kp, qs[h]), NEG)
                pr = jnp.exp(s - lse_ref[h:h+1, :])
                ds = (pr * (nt(vp, das[h]) - delta[h])).astype(bf16)
                dv = dv + jnp.dot(pr.astype(bf16), das[h], preferred_element_type=f32)
                dk = dk + jnp.dot(ds, qs[h], preferred_element_type=f32)
                dq.append(tn(ds, kx))
            dq_acc[p] = dq_acc[p] + jnp.where(low, dq[0], dq[1])
            dk_acc[at_rows, at] = dk_acc[at_rows, at] + dk
            dv_acc[at_rows, at] = dv_acc[at_rows, at] + dv
        return 0
    lax.fori_loop(0, steps, tile, 0)
    for p in range(pairs):
        dq_ref[:, p*128:(p+1)*128] = dq_acc[p].astype(dq_ref.dtype)
    @pl.when(i == pl.num_programs(0) - 1)
    def _():
        dk_ref[...] = dk_acc[...].astype(bf16)
        dv_ref[...] = dv_acc[...].astype(bf16)

def attend_back(q, k, v, o, da, lse, span, idq_row, idk_col):
    rows, cols = q.shape
    wide = k.shape[0]
    heads = cols // 64
    tiles = rows // BQ
    full = lambda a: pl.BlockSpec(a.shape, lambda i, s: (0,) * a.ndim)
    qt = pl.BlockSpec((BQ, cols), lambda i, s: (i, 0))
    return pl.pallas_call(
        functools.partial(bwd_kernel, rows // 2),
        grid_spec=pltpu.PrefetchScalarGridSpec(
            num_scalar_prefetch=1, grid=(tiles,),
            in_specs=[qt, full(k), full(v), qt, qt, pl.BlockSpec((heads, BQ), lambda i, s: (0, i)),
                      pl.BlockSpec((1, BQ), lambda i, s: (0, i)), full(idk_col)],
            out_specs=[qt, full(k), full(v)],
            scratch_shapes=[pltpu.VMEM((wide, cols), f32), pltpu.VMEM((wide, cols), f32), pltpu.VMEM((heads // 2, BQ, 128), f32)]),
        out_shape=[jax.ShapeDtypeStruct((rows, cols), bf16), jax.ShapeDtypeStruct((wide, cols), bf16), jax.ShapeDtypeStruct((wide, cols), bf16)],
        compiler_params=pltpu.CompilerParams(vmem_limit_bytes=60 << 20, dimension_semantics=("arbitrary",)),
        cost_estimate=pl.CostEstimate(flops=10*rows*wide*cols, bytes_accessed=10*wide*cols, transcendentals=0),
    )(span, q, k, v, o, da, lse, idq_row, idk_col)

def spans(ids, mine, tq, tk):
    first, final = mine[::tq], mine[tq-1::tq]
    lo = jnp.sum((ids[None, :] < first[:, None]).astype(jnp.int32), axis=1) // 128 * 128
    hi = jnp.sum((ids[None, :] <= final[:, None]).astype(jnp.int32), axis=1)
    return jnp.stack([lo, (hi - lo + tk - 1) // tk])

def window_ids(clip_ids, frame_mask, half):
    z, x, core, y = place()
    start = (4 * (2 * z + x) + y) * half
    pad = 4 * half
    ids = jnp.pad(clip_ids, (2 * half, pad), constant_values=((-1, 1 << 30),))
    val = jnp.pad(frame_mask, (2 * half, pad))
    ids = lax.dynamic_slice_in_dim(ids, start, 7 * half)
    val = lax.dynamic_slice_in_dim(val, start, 7 * half)
    mine = jnp.concatenate([ids[2*half:3*half], ids[4*half:5*half]])
    keys = jnp.where(val == 1, ids, -2)
    return spans(ids, mine, TQ, TK), spans(ids, mine, BQ, BK), mine, keys

def norm_forward(values, gain_vec, bias_vec):
    row_mean = jnp.mean(values, axis=-1, keepdims=True)
    centred = values - row_mean
    inverse = lax.rsqrt(jnp.mean(centred * centred, axis=-1, keepdims=True) + EPS)
    normed = centred * inverse
    return ((normed * gain_vec + bias_vec).astype(bf16), normed, inverse)

def norm_backward(grad_out, normed, inverse, gain_vec):
    scaled = grad_out * gain_vec
    projected = (scaled - jnp.mean(scaled, axis=-1, keepdims=True)
                 - normed * jnp.mean(scaled * normed, axis=-1, keepdims=True))
    return (inverse * projected, jnp.sum(grad_out * normed, axis=0), jnp.sum(grad_out, axis=0))

def gelu_parts(z):
    half = 0.5 * (1.0 + jax.scipy.special.erf(z * 0.7071067811865476))
    return z * half, half + z * jnp.exp(-0.5 * z * z) * 0.3989422804014327

def mm(a, b):
    return jnp.dot(a, b, preferred_element_type=f32)

def pack(parts, width):
    return jnp.concatenate([p[..., i:i + width] for p in parts for i in range(0, p.shape[-1], width)], axis=1)

def unpack(packed, shapes, width):
    out, at = [], 0
    for r, c in shapes:
        n = c // width
        out.append(jnp.concatenate([packed[:, at + i * r:at + (i + 1) * r] for i in range(n)], axis=-1))
        at += n * r
    return out

def swap(t):
    return lax.ppermute(t, ("core", "y"), [(0, 0), (1, 2), (2, 1), (3, 3)])

def body(frames_in, frames_cot, clip_ids, frame_mask, norm_gain, norm_bias, qkv_weight, qv_bias,
         proj_weight, up_weight, up_bias, down_weight, out_biases):
    layers = qkv_weight.shape[0]
    half, width = frames_in.shape
    z, x, core, y = place()
    count = chips()
    group = ("z", "x", "y")
    hcols = qkv_weight.shape[-1]
    hidden = up_weight.shape[-1]
    span, span_back, mine, keys = window_ids(clip_ids, frame_mask, half)
    idk = keys[None, :]
    shards = [[qkv_weight[l].reshape(-1, 3 * hcols), proj_weight[l], up_weight[l], down_weight[l]] for l in range(layers)]
    bias = jnp.concatenate([up_bias, qv_bias.reshape(layers, 2 * hcols)], axis=1)
    moved = swap(pack([s[None] for s in shards[1]], hcols)[0])
    *full, bias = gather(shards[0], bias, [False, True, True, False], 0)
    full = [[w.reshape(-1, w.shape[-1]) for w in full]]
    moved, full[0] = lax.optimization_barrier((moved, full[0]))
    both = lax.all_gather(moved, group, axis=0, tiled=False)
    full.append([w.reshape(-1, w.shape[-1]) for w in unpack(both, [s.shape for s in shards[1]], hcols)])
    state = frames_in
    kept = []
    for l in range(layers):
        wqkv, wproj, wup, wdown = full[l]
        upb, qb, vb = bias[l, :hidden], bias[l, hidden:hidden+hcols], bias[l, hidden+hcols:]
        a, hat1, inv1 = norm_forward(state, norm_gain[l, 0], norm_bias[l, 0])
        win = halo(a, 1)
        a_own = jnp.concatenate([win[2], win[4]])
        a_win = win.reshape(-1, width)
        q = (mm(a_own, wqkv[:, :hcols]) + qb).astype(bf16)
        k = mm(a_win, wqkv[:, hcols:2*hcols]).astype(bf16)
        v = (mm(a_win, wqkv[:, 2*hcols:]) + vb).astype(bf16)
        o, lse = attend(q, k, v, span, mine[:, None], idk)
        middle = state + pair_sum(mm(o, wproj).reshape(2, half, width), 2) + out_biases[l, 0]
        c, hat2, inv2 = norm_forward(middle, norm_gain[l, 1], norm_bias[l, 1])
        c_full = pair_gather(c, 3).reshape(2 * half, width)
        zz = mm(c_full, wup) + upb
        g, slope = gelu_parts(zz)
        g, slope = g.astype(bf16), slope.astype(bf16)
        state = middle + pair_sum(mm(g, wdown).reshape(2, half, width), 2) + out_biases[l, 1]
        kept.append((a_own, a_win, hat1, inv1, q, k, v, o, lse, hat2, inv2, c_full, g, slope))
    grad = frames_cot
    wgrads, small = [None] * layers, [None] * layers
    for l in reversed(range(layers)):
        wqkv, wproj, wup, wdown = full[l]
        a_own, a_win, hat1, inv1, q, k, v, o, lse, hat2, inv2, c_full, g, slope = kept[l]
        e_full = pair_gather(grad.astype(bf16), 3).reshape(2 * half, width)
        g_down = mm(g.T, e_full)
        dz = mm(e_full, wdown.T) * slope.astype(f32)
        upb = jnp.sum(dz, axis=0)
        dzb = dz.astype(bf16)
        g_up = mm(c_full.T, dzb)
        dc = pair_sum(mm(dzb, wup.T).reshape(2, half, width), 2)
        back, gain2, shift2 = norm_backward(dc, hat2, inv2, norm_gain[l, 1])
        dh = grad + back
        dh_full = pair_gather(dh.astype(bf16), 3).reshape(2 * half, width)
        g_proj = mm(o.T, dh_full)
        da = mm(dh_full, wproj.T).astype(bf16)
        dq, dk, dv = attend_back(q, k, v, o, da, lse, span_back, mine[None, :], keys[:, None])
        qb = jnp.sum(dq.astype(f32), axis=0)
        vb = jnp.sum(dv.astype(f32), axis=0)
        g_qkv = jnp.concatenate([mm(a_own.T, dq), mm(a_win.T, dk), mm(a_win.T, dv)], axis=1)
        wq, wk, wv = wqkv[:, :hcols], wqkv[:, hcols:2*hcols], wqkv[:, 2*hcols:]
        part = mm(dk, wk.T) + mm(dv, wv.T)
        part = part.reshape(7, half, width)
        pq = mm(dq, wq.T).reshape(2, half, width)
        part = jnp.stack([part[0], part[1], part[2] + pq[0], part[3], part[4] + pq[1], part[5], part[6]]).astype(bf16)
        da1 = halo_back(part, 4)
        back, gain1, shift1 = norm_backward(da1, hat1, inv1, norm_gain[l, 0])
        parts = [jnp.stack([gain1, gain2]), jnp.stack([shift1, shift2]),
                 jnp.stack([jnp.sum(dh, axis=0), jnp.sum(grad, axis=0)])]
        grad = dh + back
        wide = lambda t, n: lax.dynamic_update_slice_in_dim(jnp.zeros(t.shape[:-1] + (n,), f32), t, core * t.shape[-1], t.ndim - 1)
        parts += [wide(jnp.stack([qb, vb]), 2 * hcols), wide(upb, 2 * hidden)]
        small[l] = parts
        grads = [t.astype(bf16).reshape(count, -1, t.shape[-1]) for t in (g_qkv, g_proj, g_up, g_down)]
        if l == 0:
            wgrads[l] = scatter_sum(grads, [False, True, False, True], 5)
        else:
            packed = pack(grads, hcols)
            packed, grad = lax.optimization_barrier((packed, grad))
            rows = packed.shape[1]
            own = lax.psum_scatter(packed.reshape(-1, hcols), group, scatter_dimension=0, tiled=True)
            wgrads[l] = [w[0] for w in unpack(swap(own)[None].astype(f32), [s.shape for s in shards[1]], hcols)]
    flat = jnp.concatenate([t.reshape(-1) for p in small for t in p])
    flat, arrived = lax.optimization_barrier((flat, own))
    flat = lax.psum(flat, ("z", "x", "core", "y"))
    outs, at = [], 0
    for p in small:
        got = []
        for t in p:
            got.append(flat[at:at + t.size].reshape(t.shape)); at += t.size
        outs.append(got)
    gains, shifts, obias, qvb, upb = [jnp.stack([o[i] for o in outs]) for i in range(5)]
    qvb = lax.dynamic_slice_in_dim(qvb, y * hcols, hcols, 2)
    upb = lax.dynamic_slice_in_dim(upb, y * hidden, hidden, 1)
    gq, gp, gu, gd = [jnp.stack([w[i] for w in wgrads]) for i in range(4)]
    return (state, grad, gq.reshape(layers, -1, 3, hcols), qvb, gp, gu, upb, gd, gains, shifts, obias)

def solution(mesh):
    dp, mp = mesh.shape["dp"], mesh.shape["mp"]
    named = Mesh(mesh.devices.reshape(dp // 4, 2, 2, mp), ("z", "x", "core", "y"))
    deep = ("z", "x", "core")
    rows = P(deep + ("y",), None)
    qkv, qv = P(None, deep, None, "y"), P(None, None, "y")
    tall, wide, upb = P(None, ("y",) + deep, None), P(None, deep, "y"), P(None, "y")
    return jax.shard_map(
        body, mesh=named,
        in_specs=(rows, rows, P(), P(), P(), P(), qkv, qv, tall, wide, upb, tall, P()),
        out_specs=(rows, rows, qkv, qv, tall, wide, upb, tall, P(), P(), P()),
        check_vma=False)
```

time: 1950 us -> 800 us (0.41)
  waiting for transfers between devices: 1310 us -> 35.3 us
  Pallas kernels: 0 us -> 477 us
  matrix products: 312 us -> 114 us
  blocking collectives: 78.8 us -> 0 us
  other arithmetic: 129 us -> 53 us
  local copies, waits for them, and re-layouts: 73.5 us -> 98.1 us
  starting transfers between devices: 23.8 us -> 1.63 us
    reduce_scatter x16 -> x1, waiting for transfers between devices: 772 us -> 0.01 us  [body(): lax.psum_scatter(packed.reshape(-1, hcols), group, scatter_dimension=0, t...]
    pallas_call x0 -> x22, Pallas kernels: none -> 477 us  [the longest x2 111 us: halo_back(): pl.pallas_call(functools.partial(halo_back_kernel, count), out_shape=jax....]
    all_gather x14 -> x1, waiting for transfers between devices: 413 us -> 0.01 us  [body(): both = lax.all_gather(moved, group, axis=0, tiled=False)]
    dot_general x36, matrix products: 312 us -> 114 us  [mm(): return jnp.dot(a, b, preferred_element_type=f32)]
    psum x1, waiting for transfers between devices: 128 us -> 35.2 us  [body(): flat = lax.psum(flat, ('z', 'x', 'core', 'y'))]
    all_gather x2 -> x0, blocking collectives: 78.8 us -> none  [fetch_weights(): lax.all_gather(proj_weight[depth], 'dp', axis=0, tiled=True)]
    reduce_sum x14 -> x11, other arithmetic: 54.7 us -> 9.75 us  [the longest x2 4.31 us: body(): vb = jnp.sum(dv.astype(f32), axis=0)]
    another operation x20 -> x16, other arithmetic: 27.9 us -> 8.14 us  [the longest x5 3.1 us: body(): jnp.stack([o[i] for o in outs])]
  transfers between devices with their start and end apart: 39 -> 5, of which waited for: 30 -> 1; matrix products, arithmetic and copies ran while one was open for 9% -> 19% of each run, Pallas kernels for 0% -> 45%
where the time goes in v1:
time: 800 us; the launch traced here: 794 us
  Pallas kernels  477 us (60%)
  matrix products  114 us (14%)
  local copies, waits for them, and re-layouts  98.1 us (12%)
  other arithmetic  53 us (7%)
  waiting for transfers between devices  35.3 us (4%)
  between operations  15.7 us (2%)
    dot_general x36, matrix products, mm(): return jnp.dot(a, b, preferred_element_type=f32)  114 us
    pallas_call x2, Pallas kernels, halo_back(): pl.pallas_call(functools.partial(halo_back_kernel, count), out_shape=jax....  111 us
    pallas_call x1, Pallas kernels, gather(): pl.pallas_call(functools.partial(gather_kernel, count, y_first), out_shap...  82.7 us
    pallas_call x1, Pallas kernels, scatter_sum(): pl.pallas_call(functools.partial(reduce_kernel, count, early), out_shape=...  80.3 us
    pallas_call x2, Pallas kernels, halo(): pl.pallas_call(functools.partial(halo_kernel, count), out_shape=jax.Shape...  69 us
    pallas_call x2, Pallas kernels, attend_back(): pl.pallas_call(functools.partial(bwd_kernel, rows // 2), grid_spec=pltpu....  45.5 us
    unnamed x241, local copies, waits for them, and re-layouts  42.2 us
    psum x1, waiting for transfers between devices, body(): flat = lax.psum(flat, ('z', 'x', 'core', 'y'))  35.2 us
  transfers between devices with their start and end apart: 5, of which 1 were waited for; matrix products, arithmetic and copies ran while one was open for 19% of the time, Pallas kernels for 45%

profile of v1, /device:TPU:0, one launch (start us, length us, event | category | flops | bytes accessed | tf_op | source)
XLA Modules:
  0.0 794.0 jit_solution(81595826224272833)
XLA Ops:
  21.3 82.7 %shard_map.213 = (bf16[16,48,1152]{2,1,0:T(8,128)(2,1)}, bf16[16,24,768]{2,1,0:T(8,128)(2,1)}, bf16[16,48,1536]{2,1,0:T(8,128)(2,1)}, bf16[16,96,768]{2,1,0:T(8,128)(2,1)}, f32[2,2304]{1,0:T(2,128)}) custom-call(bf16[48,1152]{1,0:T(8,128)(2,1)} %bitcast.290, bf16[24,768]{1,0:T(8,128)(2,1)} %slice_bitcast_fusion.17.refs_1_, ...), custom_call_target="tpu_custom_call" | custom-call | tf_op jit(solution)/shard_map/pallas_call | solution.py:158
  111.5 35.6 %shard_map.212 = bf16[7,384,768]{2,1,0:T(8,128)(2,1)} custom-call(bf16[384,768]{1,0:T(8,128)(2,1)} %add_convert_fusion.3.a_ref), custom_call_target="tpu_custom_call" | custom-call | tf_op jit(solution)/shard_map/pallas_call | solution.py:255
  154.2 3.7 convolution_convert_fusion.1.k_ref
  157.9 3.7 fusion.10.v_ref
  161.6 14.7 %shard_map.214 = (bf16[768,384]{1,0:T(8,128)(2,1)}, f32[6,768]{1,0:T(8,128)}) custom-call(s32[2,2]{1,0:T(2,128)} %pad_add_fusion.1.span_ref, bf16[768,384]{1,0:T(8,128)(2,1)} %fusion.20.q_ref, bf16[2688,384]{1,0:T(8,128)(2,1)} %convolution_convert_fusion.1.k_ref, bf16[2688,384]{1,0:T(8,128)(2,1)} %fusion.10.v_ref, s32[768,1]{1,0:T(8,128)} %broadcast_in_dim.23.idq_ref, ...), custom_call_target="tpu_custom_call" | custom-call | flops 3170893824 | bytes 6193152 | tf_op jit(solution)/shard_map/pallas_call | solution.py:647
  176.3 3.2 fusion.113
  179.5 5.7 shard_map.215
  188.0 4.1 shard_map.216
  192.2 6.4 multiply_convert_fusion.1
  198.6 3.4 fusion.114
  202.0 5.7 shard_map.217
  210.5 33.4 %shard_map.218 = bf16[7,384,768]{2,1,0:T(8,128)(2,1)} custom-call(bf16[384,768]{1,0:T(8,128)(2,1)} %add_convert_fusion.1.a_ref), custom_call_target="tpu_custom_call" | custom-call | tf_op jit(solution)/shard_map/pallas_call | solution.py:255
  243.9 6.9 copy.44
  250.8 2.1 slice_bitcast_fusion.11
  254.3 3.3 fusion.99
  257.6 4.0 fusion.100
  261.7 3.7 convolution_convert_fusion.k_ref
  265.4 3.6 fusion.11.v_ref
  270.7 14.3 %shard_map.219 = (bf16[768,384]{1,0:T(8,128)(2,1)}, f32[6,768]{1,0:T(8,128)}) custom-call(s32[2,2]{1,0:T(2,128)} %pad_add_fusion.1.span_ref, bf16[768,384]{1,0:T(8,128)(2,1)} %fusion.21.q_ref, bf16[2688,384]{1,0:T(8,128)(2,1)} %convolution_convert_fusion.k_ref, bf16[2688,384]{1,0:T(8,128)(2,1)} %fusion.11.v_ref, s32[768,1]{1,0:T(8,128)} %broadcast_in_dim.23.idq_ref, ...), custom_call_target="tpu_custom_call" | custom-call | flops 3170893824 | bytes 6193152 | tf_op jit(solution)/shard_map/pallas_call | solution.py:647
  285.0 3.2 fusion.115.p_ref
  288.3 5.7 shard_map.220
  294.0 3.6 fusion.96
  299.6 4.1 shard_map.221
  303.7 4.1 shard_map.223
  307.9 2.0 pad_maximum_fusion.1
  312.1 3.9 multiply_convert_fusion
  315.9 4.5 fusion.102
  320.4 3.4 convolution_convert_fusion.5
  323.8 3.4 fusion.117.p_ref
  327.2 5.7 shard_map.224
  333.0 5.6 convolution_convert_fusion.4
  338.6 3.4 fusion.116.p_ref
  342.0 5.7 shard_map.222
  347.7 2.6 multiply_reduce_fusion
  350.3 3.4 fusion.94
  355.6 4.2 shard_map.225
  359.8 2.8 convolution_convert_fusion.9
  364.3 22.8 %shard_map.226 = (bf16[768,384]{1,0:T(8,128)(2,1)}, bf16[2688,384]{1,0:T(8,128)(2,1)}, bf16[2688,384]{1,0:T(8,128)(2,1)}) custom-call(s32[2,2]{1,0:T(2,128)} %pad_add_fusion.1.span_ref, bf16[768,384]{1,0:T(8,128)(2,1)} %fusion.21.q_ref, bf16[2688,384]{1,0:T(8,128)(2,1)} %convolution_convert_fusion.k_ref, bf16[2688,384]{1,0:T(8,128)(2,1)} %fusion.11.v_ref, ...), custom_call_target="tpu_custom_call" | custom-call | flops 7927234560 | bytes 10321920 | tf_op jit(solution)/shard_map/pallas_call | solution.py:723
  391.0 2.3 fusion.67
  393.3 3.2 fusion.25
  396.5 3.2 fusion.31
  407.2 2.3 fusion.110
  415.8 56.2 %shard_map.227 = f32[384,768]{1,0:T(8,128)} custom-call(bf16[7,384,768]{2,1,0:T(8,128)(2,1)} %fusion.60.p), custom_call_target="tpu_custom_call" | custom-call | tf_op jit(solution)/shard_map/pallas_call | solution.py:334
  472.1 2.6 multiply_reduce_fusion.1
  475.2 6.6 copy.46
  482.7 2.3 convert_reduce_fusion
  487.8 4.1 shard_map.228
  491.9 6.4 fusion.112
  498.3 3.4 fusion.45
  501.7 5.8 shard_map.229
  512.6 4.2 shard_map.230
  516.9 2.9 convolution_convert_fusion.8.da_ref
  519.8 22.7 %shard_map.231 = (bf16[768,384]{1,0:T(8,128)(2,1)}, bf16[2688,384]{1,0:T(8,128)(2,1)}, bf16[2688,384]{1,0:T(8,128)(2,1)}) custom-call(s32[2,2]{1,0:T(2,128)} %pad_add_fusion.1.span_ref, bf16[768,384]{1,0:T(8,128)(2,1)} %fusion.20.q_ref, bf16[2688,384]{1,0:T(8,128)(2,1)} %convolution_convert_fusion.1.k_ref, bf16[2688,384]{1,0:T(8,128)(2,1)} %fusion.10.v_ref, ...), custom_call_target="tpu_custom_call" | custom-call | flops 7927234560 | bytes 10321920 | tf_op jit(solution)/shard_map/pallas_call | solution.py:723
  542.5 2.1 convert_reduce_fusion.1
  545.4 4.2 fusion.73
  549.6 2.3 fusion.111
  559.0 54.9 %shard_map.232 = f32[384,768]{1,0:T(8,128)} custom-call(bf16[7,384,768]{2,1,0:T(8,128)(2,1)} %fusion.55.p), custom_call_target="tpu_custom_call" | custom-call | tf_op jit(solution)/shard_map/pallas_call | solution.py:334
  614.0 2.5 multiply_reduce_fusion.3
  642.3 4.1 fusion.34
  646.4 2.3 fusion.37
  652.9 3.5 convolution_convert_fusion.2
  656.4 3.5 convolution_convert_fusion.3
  661.4 80.3 %shard_map.233 = (f32[48,1152]{1,0:T(8,128)}, f32[24,768]{1,0:T(8,128)}, f32[48,1536]{1,0:T(8,128)}, f32[96,768]{1,0:T(8,128)}) custom-call(bf16[16,48,1152]{2,1,0:T(8,128)(2,1)} %pad_maximum_fusion.3.refs_0_, bf16[16,24,768]{2,1,0:T(8,128)(2,1)} %bitcast.281, bf16[16,48,1536]{2,1,0:T(8,128)(2,1)} %bitcast.248, bf16[16,96,768]{2,1,0:T(8,128)(2,1)} %bitcast.247), custom_call_target="tpu_custom_call" | custom-call | tf_op jit(solution)/shard_map/pallas_call | solution.py:558
  743.4 35.2 %all-reduce.5.cloned.1.call-done = f32[18432]{0:T(1024)} async-done(((f32[18432]{0:T(1024)}), f32[18432]{0:T(1024)}) %all-reduce.5.cloned.1.call-update) | async-done | bytes 73744 | tf_op jit(solution)/shard_map/psum | solution.py:873
  (400 shorter events, 120.8 us)
Async XLA Ops:
  7.2 13.4 %copy-start.53 = (bf16[2,48,1536]{2,1,0:T(8,128)(2,1)S(1)}, bf16[2,48,1536]{2,1,0:T(8,128)(2,1)}, u32[]{:S(2)}) copy-start(bf16[2,48,1536]{2,1,0:T(8,128)(2,1)} %param.22) | copy-start | bytes 884740
  7.2 12.8 %copy-start.88 = (f32[2,1536]{1,0:T(2,128)S(1)}, f32[2,1536]{1,0:T(2,128)}, u32[]{:S(2)}) copy-start(f32[2,1536]{1,0:T(2,128)} %param.23) | copy-start | bytes 36868
  7.2 97.7 %copy-start.65 = (s32[12288]{0:T(1024)S(1)}, s32[12288]{0:T(1024)}, u32[]{:S(2)}) copy-start(s32[12288]{0:T(1024)} %param.16) | copy-start | bytes 147460
  7.2 97.7 %copy-start.66 = (s32[12288]{0:T(1024)S(1)}, s32[12288]{0:T(1024)}, u32[]{:S(2)}) copy-start(s32[12288]{0:T(1024)} %param.15) | copy-start | bytes 147460
  7.2 245.7 %all-gather.3.cloned.1.call-start = ((), (), s32[]{:S(2)}) async-start(), calls=%async_computation.3 | async-start | bytes 7520256 | tf_op jit(solution)/shard_map/all_gather | solution.py:805
  14.8 94.6 %copy-start = (f32[384,768]{1,0:T(8,128)S(1)}, f32[384,768]{1,0:T(8,128)}, u32[]{:S(2)}) copy-start(f32[384,768]{1,0:T(8,128)} %param.13) | copy-start | bytes 3538948
  14.8 89.3 %collective-permute-start = (bf16[576,384]{1,0:T(8,128)(2,1)S(1)}, bf16[576,384]{1,0:T(8,128)(2,1)S(1)}, u32[]{:S(2)}, u32[]{:S(2)}) collective-permute-start(bf16[576,384]{1,0:T(8,128)(2,1)S(1)} %bitcast.301), channel_id=1, source_target_pairs={{0,0},{1,2},{2,1},{3,3},{4,4},{5,6},{6,5},{7,7},{8,8},{9,10},{10,9... | collective-permute-start | bytes 1327112 | tf_op jit(solution)/shard_map/ppermute | solution.py:786
  21.3 88.2 %copy-start.84 = (f32[2,2,768]{2,1,0:T(2,128)S(1)}, f32[2,2,768]{2,1,0:T(2,128)}, u32[]{:S(2)}) copy-start(f32[2,2,768]{2,1,0:T(2,128)} %param.17) | copy-start | bytes 36868
  21.3 88.3 %copy-start.85 = (f32[2,2,768]{2,1,0:T(2,128)S(1)}, f32[2,2,768]{2,1,0:T(2,128)}, u32[]{:S(2)}) copy-start(f32[2,2,768]{2,1,0:T(2,128)} %param.18) | copy-start | bytes 36868
  104.8 555.0 %reduce-scatter.2.cloned.1.call-start = ((), (), s32[]{:S(2)}) async-start(), calls=%async_computation.1 | async-start | bytes 7520256 | tf_op jit(solution)/shard_map/reduce_scatter | solution.py:869
  109.6 37.6 %copy-start.57 = (f32[768]{0:T(1024)}, f32[768]{0:T(1024)S(1)}, u32[]{:S(2)}) copy-start(f32[768]{0:T(1024)S(1)} %get-tuple-element.115) | copy-start | bytes 9220
  110.2 37.0 %copy-start.59 = (f32[384]{0:T(512)}, f32[384]{0:T(512)S(1)}, u32[]{:S(2)}) copy-start(f32[384]{0:T(512)S(1)} %broadcast_multiply_fusion.11) | copy-start | bytes 4612
  110.5 36.8 %copy-start.67 = (f32[384]{0:T(512)}, f32[384]{0:T(512)S(1)}, u32[]{:S(2)}) copy-start(f32[384]{0:T(512)S(1)} %add_rsqrt_fusion.3) | copy-start | bytes 4612
  111.5 36.5 %copy-start.75 = (f32[2,2304]{1,0:T(2,128)S(1)}, f32[2,2304]{1,0:T(2,128)}, u32[]{:S(2)}) copy-start(f32[2,2304]{1,0:T(2,128)} %get-tuple-element.43) | copy-start | bytes 55300
  111.5 37.1 %copy-start.86 = (f32[2,2,768]{2,1,0:T(2,128)S(1)}, f32[2,2,768]{2,1,0:T(2,128)}, u32[]{:S(2)}) copy-start(f32[2,2,768]{2,1,0:T(2,128)} %param.25) | copy-start | bytes 36868
  147.2 4.1 copy-start.32
  149.9 42.2 %copy-start.89 = (f32[1536]{0:T(1024)}, f32[1536]{0:T(1024)S(1)}, u32[]{:S(2)}) copy-start(f32[1536]{0:T(1024)S(1)} %get-tuple-element.104) | copy-start | bytes 18436
  161.6 14.7 %copy-start.41 = (bf16[16,24,768]{2,1,0:T(8,128)(2,1)S(1)}, bf16[16,24,768]{2,1,0:T(8,128)(2,1)}, u32[]{:S(2)}) copy-start(bf16[16,24,768]{2,1,0:T(8,128)(2,1)} %get-tuple-element.39) | copy-start | bytes 1769476
  186.9 11.6 %copy-start.69 = (f32[384]{0:T(512)}, f32[384]{0:T(512)S(1)}, u32[]{:S(2)}) copy-start(f32[384]{0:T(512)S(1)} %add_rsqrt_fusion.2) | copy-start | bytes 4612
  192.1 6.4 copy-start.94
  209.2 34.8 %copy-start.61 = (f32[384]{0:T(512)}, f32[384]{0:T(512)S(1)}, u32[]{:S(2)}) copy-start(f32[384]{0:T(512)S(1)} %broadcast_multiply_fusion.9) | copy-start | bytes 4612
  209.4 34.5 %copy-start.71 = (f32[384]{0:T(512)}, f32[384]{0:T(512)S(1)}, u32[]{:S(2)}) copy-start(f32[384]{0:T(512)S(1)} %add_rsqrt_fusion.1) | copy-start | bytes 4612
  252.9 16.1 %copy-start.48 = (bf16[384,768]{1,0:T(8,128)(2,1)}, bf16[384,768]{1,0:T(8,128)(2,1)S(1)}, u32[]{:S(2)}) copy-start(bf16[384,768]{1,0:T(8,128)(2,1)S(1)} %get-tuple-element.146) | copy-start | bytes 1769476
  257.6 4.1 copy-start.3
  261.7 7.4 copy-start.12
  265.4 3.7 copy-start.50
  265.4 3.7 copy-start.92
  269.0 16.0 %copy-start.25 = (bf16[16,24,768]{2,1,0:T(8,128)(2,1)}, bf16[16,24,768]{2,1,0:T(8,128)(2,1)S(1)}, u32[]{:S(2)}) copy-start(bf16[16,24,768]{2,1,0:T(8,128)(2,1)S(1)} %pad_maximum_fusion.10) | copy-start | bytes 1769476
  293.9 4.5 copy-start.77
  309.9 6.0 copy-start.29
  312.1 3.9 copy-start.37
  333.0 5.6 copy-start.30
  333.0 5.6 copy-start.96
  353.7 6.1 copy-start.43
  355.6 7.0 copy-start.26
  364.3 22.8 %copy-start.49 = (bf16[384,768]{1,0:T(8,128)(2,1)S(1)}, bf16[384,768]{1,0:T(8,128)(2,1)}, u32[]{:S(2)}) copy-start(bf16[384,768]{1,0:T(8,128)(2,1)} %copy-done.48) | copy-start | bytes 1769476
  364.3 22.8 %copy-start.51 = (bf16[384,768]{1,0:T(8,128)(2,1)S(1)}, bf16[384,768]{1,0:T(8,128)(2,1)}, u32[]{:S(2)}) copy-start(bf16[384,768]{1,0:T(8,128)(2,1)} %get-tuple-element.147) | copy-start | bytes 1769476
  396.5 4.7 copy-start.27
  415.8 56.3 %copy-start.62 = (f32[384]{0:T(512)S(1)}, f32[384]{0:T(512)}, u32[]{:S(2)}) copy-start(f32[384]{0:T(512)} %copy-done.61) | copy-start | bytes 4612
  415.8 56.3 %copy-start.72 = (f32[384]{0:T(512)S(1)}, f32[384]{0:T(512)}, u32[]{:S(2)}) copy-start(f32[384]{0:T(512)} %copy-done.71) | copy-start | bytes 4612
  475.1 303.5 %all-reduce.5.cloned.1.call-start = ((), (), s32[]{:S(2)}) async-start(), calls=%async_computation.2 | async-start | bytes 147456 | tf_op jit(solution)/shard_map/psum | solution.py:873
  475.2 6.7 copy-start.78
  475.2 6.7 copy-start.80
  475.2 6.7 copy-start.81
  475.2 7.3 copy-start.79
  475.2 7.3 copy-start.23
  481.9 3.7 copy-start.83
  481.9 4.4 copy-start.82
  485.0 6.9 copy-start.90
  491.9 6.4 copy-start.93
  501.7 5.8 copy-start.70
  510.5 6.3 copy-start.42
  545.4 4.2 copy-start.31
  545.4 4.2 copy-start.33
  559.0 55.0 %copy-start.1 = (f32[384,768]{1,0:T(8,128)S(1)}, f32[384,768]{1,0:T(8,128)}, u32[]{:S(2)}) copy-start(f32[384,768]{1,0:T(8,128)} %param.13) | copy-start | bytes 3538948
  559.0 55.0 %copy-start.58 = (f32[768]{0:T(1024)S(1)}, f32[768]{0:T(1024)}, u32[]{:S(2)}) copy-start(f32[768]{0:T(1024)} %copy-done.57) | copy-start | bytes 9220
  559.0 55.0 %copy-start.60 = (f32[384]{0:T(512)S(1)}, f32[384]{0:T(512)}, u32[]{:S(2)}) copy-start(f32[384]{0:T(512)} %copy-done.59) | copy-start | bytes 4612
  559.0 55.0 %copy-start.68 = (f32[384]{0:T(512)S(1)}, f32[384]{0:T(512)}, u32[]{:S(2)}) copy-start(f32[384]{0:T(512)} %copy-done.67) | copy-start | bytes 4612
  614.0 25.9 %copy-start.46 = (bf16[384,768]{1,0:T(8,128)(2,1)S(1)}, bf16[384,768]{1,0:T(8,128)(2,1)}, u32[]{:S(2)}) copy-start(bf16[384,768]{1,0:T(8,128)(2,1)} %copy-done.45) | copy-start | bytes 1769476
  642.3 4.1 copy-start.10
  652.9 3.5 copy-start.34
  652.9 3.5 copy-start.100
  661.4 81.3 %copy-start.95 = (bf16[576,384]{1,0:T(8,128)(2,1)S(1)}, bf16[576,384]{1,0:T(8,128)(2,1)}, u32[]{:S(2)}) copy-start(bf16[576,384]{1,0:T(8,128)(2,1)} %reduce-scatter.2.cloned.1.call-done) | copy-start | bytes 1327108
  742.7 40.7 %collective-permute-start.1 = (bf16[576,384]{1,0:T(8,128)(2,1)S(1)}, bf16[576,384]{1,0:T(8,128)(2,1)S(1)}, u32[]{:S(2)}, u32[]{:S(2)}) collective-permute-start(bf16[576,384]{1,0:T(8,128)(2,1)S(1)} %copy-done.95), channel_id=1, source_target_pairs={{0,0},{1,2},{2,1},{3,3},{4,4},{5,6},{6,5},{7,7},{8,8},{9,10},{10,9... | collective-permute-start | bytes 1327112 | tf_op jit(solution)/shard_map/ppermute | solution.py:786
  (42 other events, 94.3 us)
Sparse Core Ops, SparseCore 0:
  105.0 105.4 all-gather.2
  475.2 166.2 reduce-scatter.1
  660.0 118.5 all-reduce.4

commit v2 on v1

--- a/solution.py
+++ b/solution.py
@@ -363,15 +363,84 @@
     copy = rcopy(p_ref.at[1 - core], got, send, recv, sibling)
     copy.start()
     copy.wait()
-    out[...] = p_ref[core] + got[...]
+    out[...] = p_ref[core].astype(f32) + got[...].astype(f32)
 
 def pair_sum(p, cid):
     return pl.pallas_call(
-        pair_sum_kernel, out_shape=jax.ShapeDtypeStruct(p.shape[1:], p.dtype), in_specs=[VMEM], out_specs=VMEM,
+        pair_sum_kernel, out_shape=jax.ShapeDtypeStruct(p.shape[1:], f32), in_specs=[VMEM], out_specs=VMEM,
         scratch_shapes=[pltpu.VMEM(p.shape[1:], p.dtype), pltpu.SemaphoreType.DMA, pltpu.SemaphoreType.DMA],
         compiler_params=pltpu.CompilerParams(collective_id=cid, has_side_effects=True),
     )(p)
 
+
+def small_sum_kernel(rows, layers, *refs):
+    per = 9
+    ins, refs = refs[:layers * per], refs[layers * per:]
+    gains, shifts, obias, qvb, upb, v, got, acc, zin, send, recv, z_s, z_r = refs
+    z, x, core, y = place()
+    width, half = v.shape[1], v.shape[1] // 2
+    spans_up = ins[per - 1].shape[1] // width
+    stride = 8 + 2 * spans_up
+    peers = [(z, x, 1 - core, y), (z, 1 - x, core, y), (z, x, core, 1 - y)]
+    others = [lax.rem(z + d, rows) for d in range(1, rows)]
+    at = lambda o: (o, x, core, y)
+    bar = ready([(p, True) for p in peers] + [(at(o), True) for o in others])
+    v[...] = jnp.zeros_like(v)
+    for l in range(layers):
+        one, b = ins[l * per:(l + 1) * per], l * stride
+        for i in range(6): v[b + i:b + i + 1, :] = one[i][...]
+        for c in range(2):
+            @pl.when(core == c)
+            def _():
+                for i in range(2): v[b + 6 + i:b + 7 + i, c * half:(c + 1) * half] = one[6 + i][...]
+                for i in range(spans_up):
+                    r = b + 8 + c * spans_up + i
+                    v[r:r + 1, :] = one[8][:, i * width:(i + 1) * width]
+    pl.semaphore_wait(bar, 3 + rows - 1)
+    src = v
+    for i, p in enumerate(peers):
+        copy = rcopy(src, got.at[i], send.at[i], recv.at[i], p)
+        copy.start()
+        copy.wait()
+        acc[i] = src[...] + got[i]
+        src = acc.at[i]
+    to = lambda o, slot: rcopy(src, zin.at[slot], z_s.at[o], z_r.at[slot], at(o))
+    for o in others: to(o, z).start()
+    zin[z] = src[...]
+    for o in others: to(o, o).wait_recv()
+    total = zin[0]
+    for i in range(1, rows): total = total + zin[i]
+    v[...] = total
+    for l in range(layers):
+        b = l * stride
+        for i in range(2):
+            gains[l, i:i + 1, :] = v[b + i:b + i + 1, :]
+            shifts[l, i:i + 1, :] = v[b + 2 + i:b + 3 + i, :]
+            obias[l, i:i + 1, :] = v[b + 4 + i:b + 5 + i, :]
+        for c in range(2):
+            @pl.when(y == c)
+            def _():
+                for i in range(2): qvb[l, i:i + 1, :] = v[b + 6 + i:b + 7 + i, c * half:(c + 1) * half]
+                for i in range(spans_up):
+                    r = b + 8 + c * spans_up + i
+                    upb[l:l + 1, i * width:(i + 1) * width] = v[r:r + 1, :]
+    for o in others: to(o, z).wait_send()
+
+def small_sum(parts, cid):
+    rows = lax.axis_size("z")
+    dma = pltpu.SemaphoreType.DMA
+    layers, width, hidden = len(parts), parts[0][0].shape[1], parts[0][8].shape[1]
+    flat = [t for p in parts for t in p]
+    one = (layers * (8 + 2 * hidden // width), width)
+    pair = jax.ShapeDtypeStruct((layers, 2, width), f32)
+    return pl.pallas_call(
+        functools.partial(small_sum_kernel, rows, layers),
+        out_shape=[pair, pair, pair, jax.ShapeDtypeStruct((layers, 2, width // 2), f32), jax.ShapeDtypeStruct((layers, hidden), f32)],
+        in_specs=[VMEM] * len(flat), out_specs=[VMEM] * 5,
+        scratch_shapes=[pltpu.VMEM(one, f32), pltpu.VMEM((3,) + one, f32), pltpu.VMEM((3,) + one, f32), pltpu.VMEM((rows,) + one, f32),
+                        dma((3,)), dma((3,)), dma((rows,)), dma((rows,))],
+        compiler_params=pltpu.CompilerParams(collective_id=cid, has_side_effects=True, vmem_limit_bytes=60 << 20),
+    )(*flat)
 
 def reduce_kernel(count, early, *refs):
     n = len(early)
@@ -762,7 +831,7 @@
     scaled = grad_out * gain_vec
     projected = (scaled - jnp.mean(scaled, axis=-1, keepdims=True)
                  - normed * jnp.mean(scaled * normed, axis=-1, keepdims=True))
-    return (inverse * projected, jnp.sum(grad_out * normed, axis=0), jnp.sum(grad_out, axis=0))
+    return (inverse * projected, jnp.sum(grad_out * normed, axis=0, keepdims=True), jnp.sum(grad_out, axis=0, keepdims=True))
 
 def gelu_parts(z):
     half = 0.5 * (1.0 + jax.scipy.special.erf(z * 0.7071067811865476))
@@ -798,16 +867,21 @@
     idk = keys[None, :]
     shards = [[qkv_weight[l].reshape(-1, 3 * hcols), proj_weight[l], up_weight[l], down_weight[l]] for l in range(layers)]
     bias = jnp.concatenate([up_bias, qv_bias.reshape(layers, 2 * hcols)], axis=1)
-    moved = swap(pack([s[None] for s in shards[1]], hcols)[0])
-    *full, bias = gather(shards[0], bias, [False, True, True, False], 0)
-    full = [[w.reshape(-1, w.shape[-1]) for w in full]]
-    moved, full[0] = lax.optimization_barrier((moved, full[0]))
-    both = lax.all_gather(moved, group, axis=0, tiled=False)
-    full.append([w.reshape(-1, w.shape[-1]) for w in unpack(both, [s.shape for s in shards[1]], hcols)])
+    halves = lambda t: t.reshape(-1, width)
+    soon = [shards[0][1], shards[0][3], halves(shards[1][0])]
+    late = shards[1][1:]
+    moved = swap(pack([t[None] for t in soon], width)[0])
+    moved_late = swap(pack([t[None] for t in late], width)[0])
+    wqkv0, wup0, bias = gather([shards[0][0], shards[0][2]], bias, [False, True], 0)
+    moved, wqkv0, wup0 = lax.optimization_barrier((moved, wqkv0, wup0))
+    every = lambda t: lax.all_gather(t, group, axis=0, tiled=False)
+    rows_of = lambda w: w.reshape(-1, w.shape[-1])
+    got = every(moved)
+    full = [[rows_of(wqkv0), None, rows_of(wup0), None], None]
     state = frames_in
     kept = []
     for l in range(layers):
-        wqkv, wproj, wup, wdown = full[l]
+        wqkv = full[l][0]
         upb, qb, vb = bias[l, :hidden], bias[l, hidden:hidden+hcols], bias[l, hidden+hcols:]
         a, hat1, inv1 = norm_forward(state, norm_gain[l, 0], norm_bias[l, 0])
         win = halo(a, 1)
@@ -817,13 +891,23 @@
         k = mm(a_win, wqkv[:, hcols:2*hcols]).astype(bf16)
         v = (mm(a_win, wqkv[:, 2*hcols:]) + vb).astype(bf16)
         o, lse = attend(q, k, v, span, mine[:, None], idk)
-        middle = state + pair_sum(mm(o, wproj).reshape(2, half, width), 2) + out_biases[l, 0]
+        o, got = lax.optimization_barrier((o, got))
+        if l == 0:
+            wproj, wdown, nxt = [rows_of(w) for w in unpack(got, [t.shape for t in soon], width)]
+            full = [[full[0][0], wproj, full[0][2], wdown], [nxt.reshape(-1, 3 * hcols)]]
+            moved_late, wproj = lax.optimization_barrier((moved_late, wproj))
+            full[0][1] = wproj
+            got = every(moved_late)
+        else:
+            full[1] += [rows_of(w) for w in unpack(got, [t.shape for t in late], width)]
+        wqkv, wproj, wup, wdown = full[l]
+        middle = state + pair_sum(mm(o, wproj).astype(bf16).reshape(2, half, width), 2) + out_biases[l, 0]
         c, hat2, inv2 = norm_forward(middle, norm_gain[l, 1], norm_bias[l, 1])
         c_full = pair_gather(c, 3).reshape(2 * half, width)
         zz = mm(c_full, wup) + upb
         g, slope = gelu_parts(zz)
         g, slope = g.astype(bf16), slope.astype(bf16)
-        state = middle + pair_sum(mm(g, wdown).reshape(2, half, width), 2) + out_biases[l, 1]
+        state = middle + pair_sum(mm(g, wdown).astype(bf16).reshape(2, half, width), 2) + out_biases[l, 1]
         kept.append((a_own, a_win, hat1, inv1, q, k, v, o, lse, hat2, inv2, c_full, g, slope))
     grad = frames_cot
     wgrads, small = [None] * layers, [None] * layers
@@ -833,18 +917,18 @@
         e_full = pair_gather(grad.astype(bf16), 3).reshape(2 * half, width)
         g_down = mm(g.T, e_full)
         dz = mm(e_full, wdown.T) * slope.astype(f32)
-        upb = jnp.sum(dz, axis=0)
+        upb = jnp.sum(dz, axis=0, keepdims=True)
         dzb = dz.astype(bf16)
         g_up = mm(c_full.T, dzb)
-        dc = pair_sum(mm(dzb, wup.T).reshape(2, half, width), 2)
+        dc = pair_sum(mm(dzb, wup.T).astype(bf16).reshape(2, half, width), 2)
         back, gain2, shift2 = norm_backward(dc, hat2, inv2, norm_gain[l, 1])
         dh = grad + back
         dh_full = pair_gather(dh.astype(bf16), 3).reshape(2 * half, width)
         g_proj = mm(o.T, dh_full)
         da = mm(dh_full, wproj.T).astype(bf16)
         dq, dk, dv = attend_back(q, k, v, o, da, lse, span_back, mine[None, :], keys[:, None])
-        qb = jnp.sum(dq.astype(f32), axis=0)
-        vb = jnp.sum(dv.astype(f32), axis=0)
+        qb = jnp.sum(dq.astype(f32), axis=0, keepdims=True)
+        vb = jnp.sum(dv.astype(f32), axis=0, keepdims=True)
         g_qkv = jnp.concatenate([mm(a_own.T, dq), mm(a_win.T, dk), mm(a_win.T, dv)], axis=1)
         wq, wk, wv = wqkv[:, :hcols], wqkv[:, hcols:2*hcols], wqkv[:, 2*hcols:]
         part = mm(dk, wk.T) + mm(dv, wv.T)
@@ -853,33 +937,19 @@
         part = jnp.stack([part[0], part[1], part[2] + pq[0], part[3], part[4] + pq[1], part[5], part[6]]).astype(bf16)
         da1 = halo_back(part, 4)
         back, gain1, shift1 = norm_backward(da1, hat1, inv1, norm_gain[l, 0])
-        parts = [jnp.stack([gain1, gain2]), jnp.stack([shift1, shift2]),
-                 jnp.stack([jnp.sum(dh, axis=0), jnp.sum(grad, axis=0)])]
+        small[l] = [gain1, gain2, shift1, shift2, jnp.sum(dh, axis=0, keepdims=True), jnp.sum(grad, axis=0, keepdims=True), qb, vb, upb]
         grad = dh + back
-        wide = lambda t, n: lax.dynamic_update_slice_in_dim(jnp.zeros(t.shape[:-1] + (n,), f32), t, core * t.shape[-1], t.ndim - 1)
-        parts += [wide(jnp.stack([qb, vb]), 2 * hcols), wide(upb, 2 * hidden)]
-        small[l] = parts
         grads = [t.astype(bf16).reshape(count, -1, t.shape[-1]) for t in (g_qkv, g_proj, g_up, g_down)]
         if l == 0:
+            own, grads[0] = lax.optimization_barrier((own, grads[0]))
+            wgrads[1] = [w[0] for w in unpack(swap(own)[None].astype(f32), [s.shape for s in shards[1]], hcols)]
             wgrads[l] = scatter_sum(grads, [False, True, False, True], 5)
         else:
             packed = pack(grads, hcols)
             packed, grad = lax.optimization_barrier((packed, grad))
             rows = packed.shape[1]
             own = lax.psum_scatter(packed.reshape(-1, hcols), group, scatter_dimension=0, tiled=True)
-            wgrads[l] = [w[0] for w in unpack(swap(own)[None].astype(f32), [s.shape for s in shards[1]], hcols)]
-    flat = jnp.concatenate([t.reshape(-1) for p in small for t in p])
-    flat, arrived = lax.optimization_barrier((flat, own))
-    flat = lax.psum(flat, ("z", "x", "core", "y"))
-    outs, at = [], 0
-    for p in small:
-        got = []
-        for t in p:
-            got.append(flat[at:at + t.size].reshape(t.shape)); at += t.size
-        outs.append(got)
-    gains, shifts, obias, qvb, upb = [jnp.stack([o[i] for o in outs]) for i in range(5)]
-    qvb = lax.dynamic_slice_in_dim(qvb, y * hcols, hcols, 2)
-    upb = lax.dynamic_slice_in_dim(upb, y * hidden, hidden, 1)
+    gains, shifts, obias, qvb, upb = small_sum(small, 6)
     gq, gp, gu, gd = [jnp.stack([w[i] for w in wgrads]) for i in range(4)]
     return (state, grad, gq.reshape(layers, -1, 3, hcols), qvb, gp, gu, upb, gd, gains, shifts, obias)
 

time: 800 us -> 754 us (0.943)
  local copies, waits for them, and re-layouts: 98.1 us -> 81.4 us
  waiting for transfers between devices: 35.3 us -> 22 us
    pallas_call x0 -> x1, Pallas kernels: none -> 36.7 us  [small_sum(): pl.pallas_call(functools.partial(small_sum_kernel, rows, layers), out_sha...]
    psum x1 -> x0, waiting for transfers between devices: 35.2 us -> none  [body(): flat = lax.psum(flat, ('z', 'x', 'core', 'y'))]
    pallas_call x1, Pallas kernels: 82.7 us -> 56.1 us  [gather(): pl.pallas_call(functools.partial(gather_kernel, count, y_first), out_shap...]
    all_gather x1 -> x2, waiting for transfers between devices: 0.01 us -> 21.9 us  [body(): every = lambda t: lax.all_gather(t, group, axis=0, tiled=False)]
    unnamed x241 -> x232, local copies, waits for them, and re-layouts: 42.2 us -> 25.2 us
    pallas_call x2, Pallas kernels: 111 us -> 97.4 us  [halo_back(): pl.pallas_call(functools.partial(halo_back_kernel, count), out_shape=jax....]
    broadcast_in_dim x0 -> x18, local copies, waits for them, and re-layouts: none -> 10.6 us  [the longest x4 2.35 us: norm_backward(): jnp.sum(grad_out, axis=0, keepdims=True)]
  transfers between devices with their start and end apart: 5 -> 6, of which waited for: 1 -> 1; matrix products, arithmetic and copies ran while one was open for 19% -> 19% of each run, Pallas kernels for 45% -> 50%
where the time goes in v2:
time: 754 us; the launch traced here: 748 us
  Pallas kernels  471 us (62%)
  matrix products  108 us (14%)
  local copies, waits for them, and re-layouts  81.4 us (11%)
  other arithmetic  46.3 us (6%)
  waiting for transfers between devices  22 us (3%)
  between operations  15.6 us (2%)
    dot_general x36, matrix products, mm(): return jnp.dot(a, b, preferred_element_type=f32)  108 us
    pallas_call x2, Pallas kernels, halo_back(): pl.pallas_call(functools.partial(halo_back_kernel, count), out_shape=jax....  97.4 us
    pallas_call x1, Pallas kernels, scatter_sum(): pl.pallas_call(functools.partial(reduce_kernel, count, early), out_shape=...  82.2 us
    pallas_call x2, Pallas kernels, halo(): pl.pallas_call(functools.partial(halo_kernel, count), out_shape=jax.Shape...  73 us
    pallas_call x1, Pallas kernels, gather(): pl.pallas_call(functools.partial(gather_kernel, count, y_first), out_shap...  56.1 us
    pallas_call x2, Pallas kernels, attend_back(): pl.pallas_call(functools.partial(bwd_kernel, rows // 2), grid_spec=pltpu....  45.4 us
    pallas_call x1, Pallas kernels, small_sum(): pl.pallas_call(functools.partial(small_sum_kernel, rows, layers), out_sha...  36.7 us
    pallas_call x2, Pallas kernels, attend(): pl.pallas_call(functools.partial(fwd_kernel, rows // 2), grid_spec=pltpu....  28.7 us
  transfers between devices with their start and end apart: 6, of which 1 were waited for; matrix products, arithmetic and copies ran while one was open for 19% of the time, Pallas kernels for 50%

profile of v2, /device:TPU:0, one launch (start us, length us, event | category | flops | bytes accessed | tf_op | source)
XLA Modules:
  0.0 747.9 jit_solution(9661227179652829402)
XLA Ops:
  13.2 56.1 %shard_map.213 = (bf16[16,48,1152]{2,1,0:T(8,128)(2,1)}, bf16[16,48,1536]{2,1,0:T(8,128)(2,1)}, f32[2,2304]{1,0:T(2,128)}) custom-call(bf16[48,1152]{1,0:T(8,128)(2,1)} %bitcast.279, bf16[48,1536]{1,0:T(8,128)(2,1)} %slice_bitcast_fusion.14.refs_1_, f32[2,2304]{1,0:T(2,128)} %pad_maximum_fusion.10.refs_2_), custom_call_target="tpu_custom_call" | custom-call | tf_op jit(solution)/shard_map/pallas_call | solution.py:158
  74.9 30.1 %shard_map.212 = bf16[7,384,768]{2,1,0:T(8,128)(2,1)} custom-call(bf16[384,768]{1,0:T(8,128)(2,1)} %add_convert_fusion.3.a_ref), custom_call_target="tpu_custom_call" | custom-call | tf_op jit(solution)/shard_map/pallas_call | solution.py:255
  107.3 6.3 convolution_convert_fusion.1.k_ref
  113.6 3.7 fusion.10.v_ref
  118.9 14.3 %shard_map.214 = (bf16[768,384]{1,0:T(8,128)(2,1)}, f32[6,768]{1,0:T(8,128)}) custom-call(s32[2,2]{1,0:T(2,128)} %pad_add_fusion.1.span_ref, bf16[768,384]{1,0:T(8,128)(2,1)} %fusion.20.q_ref, bf16[2688,384]{1,0:T(8,128)(2,1)} %convolution_convert_fusion.1.k_ref, bf16[2688,384]{1,0:T(8,128)(2,1)} %fusion.10.v_ref, s32[768,1]{1,0:T(8,128)} %broadcast_in_dim.127.idq_ref, ...), custom_call_target="tpu_custom_call" | custom-call | flops 3170893824 | bytes 6193152 | tf_op jit(solution)/shard_map/pallas_call | solution.py:716
  133.3 21.9 %all-gather.5.cloned.1.call-done = bf16[3072,768]{1,0:T(8,128)(2,1)} async-done(((bf16[192,768]{1,0:T(8,128)(2,1)}), bf16[3072,768]{1,0:T(8,128)(2,1)}) %all-gather.5.cloned.1.call-update) | async-done | bytes 4718608 | tf_op jit(solution)/shard_map/all_gather | solution.py:877
  158.0 2.0 broadcast_in_dim.128.idk_ref
  161.2 2.8 slice.362
  167.4 4.5 shard_map.215
  174.7 4.1 shard_map.216
  178.8 2.4 reshape_reshape.3
  181.2 6.3 multiply_convert_fusion.1
  187.6 3.0 convolution_convert_fusion.11
  190.6 4.4 shard_map.217
  197.9 42.9 %shard_map.218 = bf16[7,384,768]{2,1,0:T(8,128)(2,1)} custom-call(bf16[384,768]{1,0:T(8,128)(2,1)} %add_convert_fusion.1.a_ref), custom_call_target="tpu_custom_call" | custom-call | tf_op jit(solution)/shard_map/pallas_call | solution.py:255
  240.8 6.4 copy.44
  251.5 3.7 convolution_convert_fusion.k_ref
  255.2 3.8 fusion.11.v_ref
  259.0 14.3 %shard_map.219 = (bf16[768,384]{1,0:T(8,128)(2,1)}, f32[6,768]{1,0:T(8,128)}) custom-call(s32[2,2]{1,0:T(2,128)} %pad_add_fusion.1.span_ref, bf16[768,384]{1,0:T(8,128)(2,1)} %fusion.21.q_ref, bf16[2688,384]{1,0:T(8,128)(2,1)} %convolution_convert_fusion.k_ref, bf16[2688,384]{1,0:T(8,128)(2,1)} %fusion.11.v_ref, s32[768,1]{1,0:T(8,128)} %broadcast_in_dim.127.idq_ref, ...), custom_call_target="tpu_custom_call" | custom-call | flops 3170893824 | bytes 6193152 | tf_op jit(solution)/shard_map/pallas_call | solution.py:716
  274.4 3.4 slice.375
  277.9 3.2 fusion.98
  283.0 4.4 shard_map.220
  287.4 3.7 fusion.95
  293.0 4.1 shard_map.221
  297.1 4.1 shard_map.223
  303.2 2.7 multiply_convert_fusion
  305.9 3.0 convolution_convert_fusion.10
  308.9 3.5 convolution_convert_fusion.4
  312.4 4.5 fusion.111
  316.8 3.0 convolution_convert_fusion.9
  319.9 4.5 shard_map.224
  324.4 4.5 shard_map.222
  328.9 2.6 multiply_reduce_fusion
  331.5 3.4 fusion.93
  336.8 4.2 shard_map.225
  341.0 3.1 convolution_convert_fusion.17.da_ref
  345.4 3.4 convolution_convert_fusion.5
  348.9 22.8 %shard_map.226 = (bf16[768,384]{1,0:T(8,128)(2,1)}, bf16[2688,384]{1,0:T(8,128)(2,1)}, bf16[2688,384]{1,0:T(8,128)(2,1)}) custom-call(s32[2,2]{1,0:T(2,128)} %pad_add_fusion.1.span_ref, bf16[768,384]{1,0:T(8,128)(2,1)} %fusion.21.q_ref, bf16[2688,384]{1,0:T(8,128)(2,1)} %convolution_convert_fusion.k_ref, bf16[2688,384]{1,0:T(8,128)(2,1)} %fusion.11.v_ref, ...), custom_call_target="tpu_custom_call" | custom-call | flops 7927234560 | bytes 10321920 | tf_op jit(solution)/shard_map/pallas_call | solution.py:792
  371.7 2.2 convolution_convert_fusion.16
  375.6 2.3 fusion.68
  377.9 3.2 fusion.25
  381.1 3.2 fusion.31
  391.9 2.3 fusion.108
  400.4 46.1 %shard_map.227 = f32[384,768]{1,0:T(8,128)} custom-call(bf16[7,384,768]{2,1,0:T(8,128)(2,1)} %fusion.61.p), custom_call_target="tpu_custom_call" | custom-call | tf_op jit(solution)/shard_map/pallas_call | solution.py:334
  446.5 2.6 multiply_reduce_fusion.1
  449.6 6.6 copy.46
  464.6 4.1 shard_map.228
  468.8 5.8 fusion.110
  475.2 3.0 convolution_convert_fusion.8
  478.2 4.4 shard_map.229
  488.4 4.1 shard_map.230
  492.5 2.9 convolution_convert_fusion.14.da_ref
  495.4 22.6 %shard_map.231 = (bf16[768,384]{1,0:T(8,128)(2,1)}, bf16[2688,384]{1,0:T(8,128)(2,1)}, bf16[2688,384]{1,0:T(8,128)(2,1)}) custom-call(s32[2,2]{1,0:T(2,128)} %pad_add_fusion.1.span_ref, bf16[768,384]{1,0:T(8,128)(2,1)} %fusion.20.q_ref, bf16[2688,384]{1,0:T(8,128)(2,1)} %convolution_convert_fusion.1.k_ref, bf16[2688,384]{1,0:T(8,128)(2,1)} %fusion.10.v_ref, ...), custom_call_target="tpu_custom_call" | custom-call | flops 7927234560 | bytes 10321920 | tf_op jit(solution)/shard_map/pallas_call | solution.py:792
  518.0 2.1 convert_reduce_fusion.1
  522.5 3.6 fusion.76
  526.1 2.3 fusion.109
  535.5 51.3 %shard_map.232 = f32[384,768]{1,0:T(8,128)} custom-call(bf16[7,384,768]{2,1,0:T(8,128)(2,1)} %fusion.56.p), custom_call_target="tpu_custom_call" | custom-call | tf_op jit(solution)/shard_map/pallas_call | solution.py:334
  590.0 36.7 %shard_map.234 = (f32[2,2,768]{2,1,0:T(2,128)}, f32[2,2,768]{2,1,0:T(2,128)}, f32[2,2,768]{2,1,0:T(2,128)}, f32[2,2,384]{2,1,0:T(2,128)}, f32[2,1536]{1,0:T(2,128)}) custom-call(f32[1,768]{1,0:T(1,128)} %broadcast_in_dim.109.refs_0_, f32[1,768]{1,0:T(1,128)} %broadcast_in_dim.110.refs_1_, f32[1,768]{1,0:T(1,128)} %broadcast_in_dim.111.refs_2_, ...), custom_call_target="tpu_custom_call" | custom-call | tf_op jit(solution)/shard_map/pallas_call | solution.py:436
  628.8 3.1 convolution_convert_fusion.12
  631.8 2.3 fusion.34
  634.2 2.3 fusion.37
  640.7 3.5 convolution_convert_fusion.2
  645.8 5.1 convolution_convert_fusion.3
  651.0 82.2 %shard_map.233 = (f32[48,1152]{1,0:T(8,128)}, f32[24,768]{1,0:T(8,128)}, f32[48,1536]{1,0:T(8,128)}, f32[96,768]{1,0:T(8,128)}) custom-call(bf16[16,48,1152]{2,1,0:T(8,128)(2,1)} %pad_maximum_fusion.1.refs_0_, bf16[16,24,768]{2,1,0:T(8,128)(2,1)} %bitcast.273, bf16[16,48,1536]{2,1,0:T(8,128)(2,1)} %bitcast.234, bf16[16,96,768]{2,1,0:T(8,128)(2,1)} %bitcast.233), custom_call_target="tpu_custom_call" | custom-call | tf_op jit(solution)/shard_map/pallas_call | solution.py:627
  (362 shorter events, 100.8 us)
Async XLA Ops:
  7.2 3.9 copy-start.96
  7.2 4.0 copy-start.52
  7.2 5.4 copy-start.91
  7.2 148.0 %all-gather.5.cloned.1.call-start = ((), (), s32[]{:S(2)}) async-start(), calls=%async_computation.2 | async-start | bytes 5013504 | tf_op jit(solution)/shard_map/all_gather | solution.py:877
  9.1 61.8 %copy-start.65 = (s32[12288]{0:T(1024)S(1)}, s32[12288]{0:T(1024)}, u32[]{:S(2)}) copy-start(s32[12288]{0:T(1024)} %param.16) | copy-start | bytes 147460
  9.1 61.8 %copy-start.66 = (s32[12288]{0:T(1024)S(1)}, s32[12288]{0:T(1024)}, u32[]{:S(2)}) copy-start(s32[12288]{0:T(1024)} %param.15) | copy-start | bytes 147460
  9.3 63.4 %copy-start = (f32[384,768]{1,0:T(8,128)S(1)}, f32[384,768]{1,0:T(8,128)}, u32[]{:S(2)}) copy-start(f32[384,768]{1,0:T(8,128)} %param.13) | copy-start | bytes 3538948
  10.4 58.9 %collective-permute-start = (bf16[192,768]{1,0:T(8,128)(2,1)S(1)}, bf16[192,768]{1,0:T(8,128)(2,1)S(1)}, u32[]{:S(2)}, u32[]{:S(2)}) collective-permute-start(bf16[192,768]{1,0:T(8,128)(2,1)S(1)} %maximum_bitcast_fusion.1), channel_id=1, source_target_pairs={{0,0},{1,2},{2,1},{3,3},{4,4},{5,6},{6,5},{7,7},{8,8},{9,10},{10,9... | collective-permute-start | bytes 884744 | tf_op jit(solution)/shard_map/ppermute | solution.py:855
  11.1 61.7 %copy-start.84 = (f32[2,2,768]{2,1,0:T(2,128)S(1)}, f32[2,2,768]{2,1,0:T(2,128)}, u32[]{:S(2)}) copy-start(f32[2,2,768]{2,1,0:T(2,128)} %param.17) | copy-start | bytes 36868
  11.2 61.7 %copy-start.85 = (f32[2,2,768]{2,1,0:T(2,128)S(1)}, f32[2,2,768]{2,1,0:T(2,128)}, u32[]{:S(2)}) copy-start(f32[2,2,768]{2,1,0:T(2,128)} %param.18) | copy-start | bytes 36868
  70.1 203.3 %all-gather.7.cloned.1.call-start = ((), (), s32[]{:S(2)}) async-start(), calls=%async_computation.3 | async-start | bytes 5640192 | tf_op jit(solution)/shard_map/all_gather | solution.py:877
  70.2 86.2 %collective-permute-start.1 = (bf16[216,768]{1,0:T(8,128)(2,1)S(1)}, bf16[216,768]{1,0:T(8,128)(2,1)S(1)}, u32[]{:S(2)}, u32[]{:S(2)}) collective-permute-start(bf16[216,768]{1,0:T(8,128)(2,1)S(1)} %maximum_bitcast_fusion), channel_id=1, source_target_pairs={{0,0},{1,2},{2,1},{3,3},{4,4},{5,6},{6,5},{7,7},{8,8},{9,10},{10,9... | collective-permute-start | bytes 995336 | tf_op jit(solution)/shard_map/ppermute | solution.py:855
  72.9 32.1 %copy-start.57 = (f32[768]{0:T(1024)}, f32[768]{0:T(1024)S(1)}, u32[]{:S(2)}) copy-start(f32[768]{0:T(1024)S(1)} %get-tuple-element.131) | copy-start | bytes 9220
  73.5 31.5 %copy-start.59 = (f32[384]{0:T(512)}, f32[384]{0:T(512)S(1)}, u32[]{:S(2)}) copy-start(f32[384]{0:T(512)S(1)} %broadcast_multiply_fusion.11) | copy-start | bytes 4612
  73.8 31.2 %copy-start.67 = (f32[384]{0:T(512)}, f32[384]{0:T(512)S(1)}, u32[]{:S(2)}) copy-start(f32[384]{0:T(512)S(1)} %add_rsqrt_fusion.3) | copy-start | bytes 4612
  74.9 31.0 %copy-start.75 = (f32[2,2304]{1,0:T(2,128)S(1)}, f32[2,2304]{1,0:T(2,128)}, u32[]{:S(2)}) copy-start(f32[2,2304]{1,0:T(2,128)} %get-tuple-element.49) | copy-start | bytes 55300
  107.3 10.1 %copy-start.42 = (bf16[384,768]{1,0:T(8,128)(2,1)}, bf16[384,768]{1,0:T(8,128)(2,1)S(1)}, u32[]{:S(2)}) copy-start(bf16[384,768]{1,0:T(8,128)(2,1)S(1)} %get-tuple-element.153) | copy-start | bytes 1769476
  107.3 10.1 %copy-start.44 = (bf16[384,768]{1,0:T(8,128)(2,1)}, bf16[384,768]{1,0:T(8,128)(2,1)S(1)}, u32[]{:S(2)}) copy-start(bf16[384,768]{1,0:T(8,128)(2,1)S(1)} %get-tuple-element.154) | copy-start | bytes 1769476
  107.3 6.3 copy-start.2
  133.3 26.7 %copy-start.86 = (f32[2,2,768]{2,1,0:T(2,128)S(1)}, f32[2,2,768]{2,1,0:T(2,128)}, u32[]{:S(2)}) copy-start(f32[2,2,768]{2,1,0:T(2,128)} %param.25) | copy-start | bytes 36868
  156.3 9.3 %copy-start.30 = (bf16[16,24,768]{2,1,0:T(8,128)(2,1)}, bf16[16,24,768]{2,1,0:T(8,128)(2,1)S(1)}, u32[]{:S(2)}) copy-start(bf16[16,24,768]{2,1,0:T(8,128)(2,1)S(1)} %slice.351) | copy-start | bytes 1769476
  157.1 487.1 %reduce-scatter.2.cloned.1.call-start = ((), (), s32[]{:S(2)}) async-start(), calls=%async_computation.1 | async-start | bytes 7520256 | tf_op jit(solution)/shard_map/reduce_scatter | solution.py:951
  158.0 6.1 copy-start.16
  161.2 20.0 %copy-start.92 = (f32[1536]{0:T(1024)}, f32[1536]{0:T(1024)S(1)}, u32[]{:S(2)}) copy-start(f32[1536]{0:T(1024)S(1)} %get-tuple-element.120) | copy-start | bytes 18436
  173.6 5.2 copy-start.15
  173.6 7.6 %copy-start.69 = (f32[384]{0:T(512)}, f32[384]{0:T(512)S(1)}, u32[]{:S(2)}) copy-start(f32[384]{0:T(512)S(1)} %add_rsqrt_fusion.2) | copy-start | bytes 4612
  181.2 6.3 copy-start.26
  196.5 44.3 %copy-start.61 = (f32[384]{0:T(512)}, f32[384]{0:T(512)S(1)}, u32[]{:S(2)}) copy-start(f32[384]{0:T(512)S(1)} %broadcast_multiply_fusion.9) | copy-start | bytes 4612
  196.8 44.0 %copy-start.71 = (f32[384]{0:T(512)}, f32[384]{0:T(512)S(1)}, u32[]{:S(2)}) copy-start(f32[384]{0:T(512)S(1)} %add_rsqrt_fusion.1) | copy-start | bytes 4612
  274.4 6.7 copy-start.32
  287.4 4.5 copy-start.76
  334.9 6.1 copy-start.33
  336.8 7.3 copy-start.50
  341.0 3.8 copy-start.103
  348.9 22.8 %copy-start.47 = (bf16[384,768]{1,0:T(8,128)(2,1)S(1)}, bf16[384,768]{1,0:T(8,128)(2,1)}, u32[]{:S(2)}) copy-start(bf16[384,768]{1,0:T(8,128)(2,1)} %copy-done.46) | copy-start | bytes 1769476
  381.1 4.8 copy-start.29
  400.4 46.1 %copy-start.62 = (f32[384]{0:T(512)S(1)}, f32[384]{0:T(512)}, u32[]{:S(2)}) copy-start(f32[384]{0:T(512)} %copy-done.61) | copy-start | bytes 4612
  400.4 46.1 %copy-start.72 = (f32[384]{0:T(512)S(1)}, f32[384]{0:T(512)}, u32[]{:S(2)}) copy-start(f32[384]{0:T(512)} %copy-done.71) | copy-start | bytes 4612
  449.6 6.7 copy-start.78
  449.6 7.3 copy-start.95
  449.6 7.9 %copy-start.80 = (f32[768]{0:T(1024)S(1)}, f32[768]{0:T(1024)}, u32[]{:S(2)}) copy-start(f32[768]{0:T(1024)} %get-tuple-element.103) | copy-start | bytes 9220
  449.6 8.5 %copy-start.81 = (f32[768]{0:T(1024)S(1)}, f32[768]{0:T(1024)}, u32[]{:S(2)}) copy-start(f32[768]{0:T(1024)} %get-tuple-element.139) | copy-start | bytes 9220
  449.6 9.1 %copy-start.79 = (f32[768]{0:T(1024)S(1)}, f32[768]{0:T(1024)}, u32[]{:S(2)}) copy-start(f32[768]{0:T(1024)} %get-tuple-element.115) | copy-start | bytes 9220
  449.6 9.6 %copy-start.24 = (bf16[768,384]{1,0:T(8,128)(2,1)S(1)}, bf16[768,384]{1,0:T(8,128)(2,1)}, u32[]{:S(2)}) copy-start(bf16[768,384]{1,0:T(8,128)(2,1)} %get-tuple-element.61) | copy-start | bytes 1769476
  456.3 6.3 copy-start.83
  456.3 6.8 copy-start.82
  462.0 6.8 copy-start.93
  468.7 6.5 copy-start.98
  474.6 3.7 copy-start.101
  478.2 4.5 copy-start.70
  485.7 6.7 copy-start.31
  518.0 4.5 copy-start.20
  535.5 51.4 %copy-start.1 = (f32[384,768]{1,0:T(8,128)S(1)}, f32[384,768]{1,0:T(8,128)}, u32[]{:S(2)}) copy-start(f32[384,768]{1,0:T(8,128)} %param.13) | copy-start | bytes 3538948
  535.5 51.4 %copy-start.58 = (f32[768]{0:T(1024)S(1)}, f32[768]{0:T(1024)}, u32[]{:S(2)}) copy-start(f32[768]{0:T(1024)} %copy-done.57) | copy-start | bytes 9220
  535.5 51.4 %copy-start.60 = (f32[384]{0:T(512)S(1)}, f32[384]{0:T(512)}, u32[]{:S(2)}) copy-start(f32[384]{0:T(512)} %copy-done.59) | copy-start | bytes 4612
  535.5 51.4 %copy-start.68 = (f32[384]{0:T(512)S(1)}, f32[384]{0:T(512)}, u32[]{:S(2)}) copy-start(f32[384]{0:T(512)} %copy-done.67) | copy-start | bytes 4612
  586.9 39.8 %copy-start.43 = (bf16[384,768]{1,0:T(8,128)(2,1)S(1)}, bf16[384,768]{1,0:T(8,128)(2,1)}, u32[]{:S(2)}) copy-start(bf16[384,768]{1,0:T(8,128)(2,1)} %copy-done.42) | copy-start | bytes 1769476
  626.7 5.1 copy-start.18
  640.7 5.2 copy-start.36
  644.2 90.0 %collective-permute-start.2 = (bf16[576,384]{1,0:T(8,128)(2,1)}, bf16[576,384]{1,0:T(8,128)(2,1)S(1)}, u32[]{:S(2)}, u32[]{:S(2)}) collective-permute-start(bf16[576,384]{1,0:T(8,128)(2,1)} %reduce-scatter.2.cloned.1.call-done), channel_id=1, source_target_pairs={{0,0},{1,2},{2,1},{3,3},{4,4},{5,6},{6,5},{7,7},{8,8},{9,10},{10,9... | collective-permute-start | bytes 1327112 | tf_op jit(solution)/shard_map/ppermute | solution.py:855
  734.7 3.8 copy-start.90
  734.7 4.4 copy-start.89
  734.7 5.0 copy-start.88
  734.7 5.6 copy-start.87
  (46 other events, 102.9 us)
Sparse Core Ops, SparseCore 0:
  70.2 84.9 all-gather.4
  158.6 94.4 all-gather.6
  449.7 176.1 reduce-scatter.1

commit v3 on v2

--- a/solution.py
+++ b/solution.py
@@ -286,35 +286,46 @@
     @pl.when(sib_has)
     def _(): to_sib(far(oc)).start()
     to_sib(2 + 2 * oc).start()
-    hand = rcopy(stage.at[0], mate_in.at[0], mate_s.at[0], mate_r.at[0], mate)
-    to_mate = rcopy(stage.at[1], mate_in.at[1], mate_s.at[1], mate_r.at[1], mate)
-    to_far = rcopy(stage.at[2], far_in, far_s.at[0], far_r.at[0], target)
-    both = lambda w: p[w].astype(f32) + sib_in[w].astype(f32)
+    size = p.shape[1] // CUT
+    at = lambda c: pl.ds(c * size, size)
+    cuts = range(CUT)
+    hand = lambda c: rcopy(stage.at[0, at(c)], mate_in.at[0, at(c)], mate_s.at[0, c], mate_r.at[0, c], mate)
+    to_mate = lambda c: rcopy(stage.at[1, at(c)], mate_in.at[1, at(c)], mate_s.at[1, c], mate_r.at[1, c], mate)
+    to_far = lambda c: rcopy(stage.at[2, at(c)], far_in.at[at(c)], far_s.at[c], far_r.at[c], target)
+    both = lambda w, c: p[w, at(c)].astype(f32) + sib_in[w, at(c)].astype(f32)
     @pl.when(gives)
     def _():
         to_sib(extra(core)).wait_recv()
-        stage[0] = both(extra(core)).astype(bf16)
-        hand.start()
+        for c in cuts:
+            stage[0, at(c)] = both(extra(core), c).astype(bf16)
+            hand(c).start()
     to_sib(direct(core)).wait_recv()
-    stage[1] = both(direct(core)).astype(bf16)
-    to_mate.start()
+    for c in cuts:
+        stage[1, at(c)] = both(direct(core), c).astype(bf16)
+        to_mate(c).start()
     @pl.when(has_target)
     def _():
         to_sib(far(core)).wait_recv()
         @pl.when(gets)
         def _():
-            hand.wait_recv()
-            stage[2] = (both(far(core)) + mate_in[0].astype(f32)).astype(bf16)
+            for c in cuts:
+                hand(c).wait_recv()
+                stage[2, at(c)] = (both(far(core), c) + mate_in[0, at(c)].astype(f32)).astype(bf16)
+                to_far(c).start()
         @pl.when(core != y)
-        def _(): stage[2] = both(far(core)).astype(bf16)
-        to_far.start()
+        def _():
+            for c in cuts:
+                stage[2, at(c)] = both(far(core), c).astype(bf16)
+                to_far(c).start()
     to_sib(own).wait_recv()
-    to_mate.wait_recv()
-    out[...] = both(own) + mate_in[1].astype(f32)
+    for c in cuts:
+        to_mate(c).wait_recv()
+        out[at(c), :] = both(own, c) + mate_in[1, at(c)].astype(f32)
     @pl.when(has_source)
     def _():
-        to_far.wait_recv()
-        out[...] = out[...] + far_in[...].astype(f32)
+        for c in cuts:
+            to_far(c).wait_recv()
+            out[at(c), :] = out[at(c), :] + far_in[at(c), :].astype(f32)
     @pl.when(sib_has & (oc != y))
     def _(): to_sib(extra(oc)).wait_send()
     to_sib(direct(oc)).wait_send()
@@ -322,10 +333,14 @@
     def _(): to_sib(far(oc)).wait_send()
     to_sib(2 + 2 * oc).wait_send()
     @pl.when(gives)
-    def _(): hand.wait_send()
-    to_mate.wait_send()
+    def _():
+        for c in cuts: hand(c).wait_send()
+    for c in cuts: to_mate(c).wait_send()
     @pl.when(has_target)
-    def _(): to_far.wait_send()
+    def _():
+        for c in cuts: to_far(c).wait_send()
+
+CUT = 3
 
 def halo_back(p, cid):
     count = chips()
@@ -336,7 +351,7 @@
         out_shape=jax.ShapeDtypeStruct(one, f32),
         in_specs=[VMEM], out_specs=VMEM,
         scratch_shapes=[pltpu.VMEM((7,) + one, bf16), pltpu.VMEM((2,) + one, bf16), pltpu.VMEM(one, bf16), pltpu.VMEM((3,) + one, bf16),
-                        dma((7,)), dma((7,)), dma((2,)), dma((2,)), dma((1,)), dma((1,))],
+                        dma((7,)), dma((7,)), dma((2, CUT)), dma((2, CUT)), dma((CUT,)), dma((CUT,))],
         compiler_params=pltpu.CompilerParams(collective_id=cid, has_side_effects=True, vmem_limit_bytes=60 << 20),
     )(p)
 
@@ -379,7 +394,7 @@
     gains, shifts, obias, qvb, upb, v, got, acc, zin, send, recv, z_s, z_r = refs
     z, x, core, y = place()
     width, half = v.shape[1], v.shape[1] // 2
-    spans_up = ins[per - 1].shape[1] // width
+    spans_up = ins[per - 1].shape[0] // width
     stride = 8 + 2 * spans_up
     peers = [(z, x, 1 - core, y), (z, 1 - x, core, y), (z, x, core, 1 - y)]
     others = [lax.rem(z + d, rows) for d in range(1, rows)]
@@ -388,14 +403,14 @@
     v[...] = jnp.zeros_like(v)
     for l in range(layers):
         one, b = ins[l * per:(l + 1) * per], l * stride
-        for i in range(6): v[b + i:b + i + 1, :] = one[i][...]
+        for i in range(6): v[b + i, :] = one[i][...]
         for c in range(2):
             @pl.when(core == c)
             def _():
                 for i in range(2): v[b + 6 + i:b + 7 + i, c * half:(c + 1) * half] = one[6 + i][...]
                 for i in range(spans_up):
                     r = b + 8 + c * spans_up + i
-                    v[r:r + 1, :] = one[8][:, i * width:(i + 1) * width]
+                    v[r, :] = one[8][i * width:(i + 1) * width]
     pl.semaphore_wait(bar, 3 + rows - 1)
     src = v
     for i, p in enumerate(peers):
@@ -429,7 +444,7 @@
 def small_sum(parts, cid):
     rows = lax.axis_size("z")
     dma = pltpu.SemaphoreType.DMA
-    layers, width, hidden = len(parts), parts[0][0].shape[1], parts[0][8].shape[1]
+    layers, width, hidden = len(parts), parts[0][0].shape[0], parts[0][8].shape[0]
     flat = [t for p in parts for t in p]
     one = (layers * (8 + 2 * hidden // width), width)
     pair = jax.ShapeDtypeStruct((layers, 2, width), f32)
@@ -727,17 +742,19 @@
         cost_estimate=pl.CostEstimate(flops=4*rows*wide*cols, bytes_accessed=6*wide*cols, transcendentals=0),
     )(span, q, k, v, idq, idk)
 
-def bwd_kernel(half, span_ref, q_ref, k_ref, v_ref, o_ref, da_ref, lse_ref, idq_ref, idk_ref, dq_ref, dk_ref, dv_ref, dk_acc, dv_acc, dq_acc):
+def bwd_kernel(half, span_ref, q_ref, k_ref, v_ref, o_ref, da_ref, lse_ref, idq_ref, idk_ref, d_ref, qb_ref, vb_ref, dk_acc, dv_acc, dq_acc):
     i = pl.program_id(0)
     T = q_ref.shape[0]
     pairs = q_ref.shape[1] // 128
-    wide = k_ref.shape[0]
+    wide, cols = k_ref.shape
     lo, steps = span_ref[0, i], span_ref[1, i]
     low = lax.broadcasted_iota(jnp.int32, (T, 128), 1) < 64
     @pl.when(i == 0)
     def _():
         dk_acc[...] = jnp.zeros_like(dk_acc)
         dv_acc[...] = jnp.zeros_like(dv_acc)
+        d_ref[:, :cols] = jnp.zeros((wide, cols), bf16)
+        qb_ref[...] = jnp.zeros_like(qb_ref)
     qs, das, delta = [], [], []
     for p in range(pairs):
         at = slice(p*128, (p+1)*128)
@@ -776,11 +793,14 @@
         return 0
     lax.fori_loop(0, steps, tile, 0)
     for p in range(pairs):
-        dq_ref[:, p*128:(p+1)*128] = dq_acc[p].astype(dq_ref.dtype)
+        at = slice(p*128, (p+1)*128)
+        d_ref[pl.ds(pl.multiple_of(gap, 128), T), at] = dq_acc[p].astype(bf16)
+        qb_ref[:, at] = qb_ref[:, at] + jnp.sum(dq_acc[p], axis=0, keepdims=True)
     @pl.when(i == pl.num_programs(0) - 1)
     def _():
-        dk_ref[...] = dk_acc[...].astype(bf16)
-        dv_ref[...] = dv_acc[...].astype(bf16)
+        d_ref[:, cols:2*cols] = dk_acc[...].astype(bf16)
+        d_ref[:, 2*cols:] = dv_acc[...].astype(bf16)
+        vb_ref[...] = jnp.sum(dv_acc[...], axis=0, keepdims=True)
 
 def attend_back(q, k, v, o, da, lse, span, idq_row, idk_col):
     rows, cols = q.shape
@@ -795,9 +815,9 @@
             num_scalar_prefetch=1, grid=(tiles,),
             in_specs=[qt, full(k), full(v), qt, qt, pl.BlockSpec((heads, BQ), lambda i, s: (0, i)),
                       pl.BlockSpec((1, BQ), lambda i, s: (0, i)), full(idk_col)],
-            out_specs=[qt, full(k), full(v)],
+            out_specs=[pl.BlockSpec((wide, 3 * cols), lambda i, s: (0, 0))] + [pl.BlockSpec((1, cols), lambda i, s: (0, 0))] * 2,
             scratch_shapes=[pltpu.VMEM((wide, cols), f32), pltpu.VMEM((wide, cols), f32), pltpu.VMEM((heads // 2, BQ, 128), f32)]),
-        out_shape=[jax.ShapeDtypeStruct((rows, cols), bf16), jax.ShapeDtypeStruct((wide, cols), bf16), jax.ShapeDtypeStruct((wide, cols), bf16)],
+        out_shape=[jax.ShapeDtypeStruct((wide, 3 * cols), bf16)] + [jax.ShapeDtypeStruct((1, cols), f32)] * 2,
         compiler_params=pltpu.CompilerParams(vmem_limit_bytes=60 << 20, dimension_semantics=("arbitrary",)),
         cost_estimate=pl.CostEstimate(flops=10*rows*wide*cols, bytes_accessed=10*wide*cols, transcendentals=0),
     )(span, q, k, v, o, da, lse, idq_row, idk_col)
@@ -831,7 +851,7 @@
     scaled = grad_out * gain_vec
     projected = (scaled - jnp.mean(scaled, axis=-1, keepdims=True)
                  - normed * jnp.mean(scaled * normed, axis=-1, keepdims=True))
-    return (inverse * projected, jnp.sum(grad_out * normed, axis=0, keepdims=True), jnp.sum(grad_out, axis=0, keepdims=True))
+    return (inverse * projected, jnp.sum(grad_out * normed, axis=0), jnp.sum(grad_out, axis=0))
 
 def gelu_parts(z):
     half = 0.5 * (1.0 + jax.scipy.special.erf(z * 0.7071067811865476))
@@ -868,16 +888,16 @@
     shards = [[qkv_weight[l].reshape(-1, 3 * hcols), proj_weight[l], up_weight[l], down_weight[l]] for l in range(layers)]
     bias = jnp.concatenate([up_bias, qv_bias.reshape(layers, 2 * hcols)], axis=1)
     halves = lambda t: t.reshape(-1, width)
-    soon = [shards[0][1], shards[0][3], halves(shards[1][0])]
-    late = shards[1][1:]
+    soon = [shards[0][3], halves(shards[1][0])]
+    late = shards[1][2:]
     moved = swap(pack([t[None] for t in soon], width)[0])
     moved_late = swap(pack([t[None] for t in late], width)[0])
-    wqkv0, wup0, bias = gather([shards[0][0], shards[0][2]], bias, [False, True], 0)
-    moved, wqkv0, wup0 = lax.optimization_barrier((moved, wqkv0, wup0))
+    wqkv0, wproj0, wup0, wproj1, bias = gather(shards[0][:3] + shards[1][1:2], bias, [False, True, True, False], 0)
+    moved, wqkv0, wproj0, wup0 = lax.optimization_barrier((moved, wqkv0, wproj0, wup0))
     every = lambda t: lax.all_gather(t, group, axis=0, tiled=False)
     rows_of = lambda w: w.reshape(-1, w.shape[-1])
     got = every(moved)
-    full = [[rows_of(wqkv0), None, rows_of(wup0), None], None]
+    full = [[rows_of(wqkv0), rows_of(wproj0), rows_of(wup0), None], None]
     state = frames_in
     kept = []
     for l in range(layers):
@@ -891,15 +911,9 @@
         k = mm(a_win, wqkv[:, hcols:2*hcols]).astype(bf16)
         v = (mm(a_win, wqkv[:, 2*hcols:]) + vb).astype(bf16)
         o, lse = attend(q, k, v, span, mine[:, None], idk)
-        o, got = lax.optimization_barrier((o, got))
-        if l == 0:
-            wproj, wdown, nxt = [rows_of(w) for w in unpack(got, [t.shape for t in soon], width)]
-            full = [[full[0][0], wproj, full[0][2], wdown], [nxt.reshape(-1, 3 * hcols)]]
-            moved_late, wproj = lax.optimization_barrier((moved_late, wproj))
-            full[0][1] = wproj
-            got = every(moved_late)
-        else:
-            full[1] += [rows_of(w) for w in unpack(got, [t.shape for t in late], width)]
+        if l > 0:
+            o, got = lax.optimization_barrier((o, got))
+            full[1] += [rows_of(wproj1)] + [rows_of(w) for w in unpack(got, [t.shape for t in late], width)]
         wqkv, wproj, wup, wdown = full[l]
         middle = state + pair_sum(mm(o, wproj).astype(bf16).reshape(2, half, width), 2) + out_biases[l, 0]
         c, hat2, inv2 = norm_forward(middle, norm_gain[l, 1], norm_bias[l, 1])
@@ -907,6 +921,13 @@
         zz = mm(c_full, wup) + upb
         g, slope = gelu_parts(zz)
         g, slope = g.astype(bf16), slope.astype(bf16)
+        if l == 0:
+            g, got = lax.optimization_barrier((g, got))
+            wdown, nxt = [rows_of(w) for w in unpack(got, [t.shape for t in soon], width)]
+            moved_late, wdown = lax.optimization_barrier((moved_late, wdown))
+            full[0][3] = wdown
+            full[1] = [nxt.reshape(-1, 3 * hcols)]
+            got = every(moved_late)
         state = middle + pair_sum(mm(g, wdown).astype(bf16).reshape(2, half, width), 2) + out_biases[l, 1]
         kept.append((a_own, a_win, hat1, inv1, q, k, v, o, lse, hat2, inv2, c_full, g, slope))
     grad = frames_cot
@@ -917,7 +938,7 @@
         e_full = pair_gather(grad.astype(bf16), 3).reshape(2 * half, width)
         g_down = mm(g.T, e_full)
         dz = mm(e_full, wdown.T) * slope.astype(f32)
-        upb = jnp.sum(dz, axis=0, keepdims=True)
+        upb = jnp.sum(dz, axis=0)
         dzb = dz.astype(bf16)
         g_up = mm(c_full.T, dzb)
         dc = pair_sum(mm(dzb, wup.T).astype(bf16).reshape(2, half, width), 2)
@@ -926,29 +947,25 @@
         dh_full = pair_gather(dh.astype(bf16), 3).reshape(2 * half, width)
         g_proj = mm(o.T, dh_full)
         da = mm(dh_full, wproj.T).astype(bf16)
-        dq, dk, dv = attend_back(q, k, v, o, da, lse, span_back, mine[None, :], keys[:, None])
-        qb = jnp.sum(dq.astype(f32), axis=0, keepdims=True)
-        vb = jnp.sum(dv.astype(f32), axis=0, keepdims=True)
-        g_qkv = jnp.concatenate([mm(a_own.T, dq), mm(a_win.T, dk), mm(a_win.T, dv)], axis=1)
-        wq, wk, wv = wqkv[:, :hcols], wqkv[:, hcols:2*hcols], wqkv[:, 2*hcols:]
-        part = mm(dk, wk.T) + mm(dv, wv.T)
-        part = part.reshape(7, half, width)
-        pq = mm(dq, wq.T).reshape(2, half, width)
-        part = jnp.stack([part[0], part[1], part[2] + pq[0], part[3], part[4] + pq[1], part[5], part[6]]).astype(bf16)
+        dqkv, qb, vb = attend_back(q, k, v, o, da, lse, span_back, mine[None, :], keys[:, None])
+        g_qkv = mm(a_win.T, dqkv)
+        part = mm(dqkv, wqkv.T).astype(bf16).reshape(7, half, width)
         da1 = halo_back(part, 4)
         back, gain1, shift1 = norm_backward(da1, hat1, inv1, norm_gain[l, 0])
-        small[l] = [gain1, gain2, shift1, shift2, jnp.sum(dh, axis=0, keepdims=True), jnp.sum(grad, axis=0, keepdims=True), qb, vb, upb]
+        small[l] = [gain1, gain2, shift1, shift2, jnp.sum(dh, axis=0), jnp.sum(grad, axis=0), qb, vb, upb]
         grad = dh + back
         grads = [t.astype(bf16).reshape(count, -1, t.shape[-1]) for t in (g_qkv, g_proj, g_up, g_down)]
         if l == 0:
-            own, grads[0] = lax.optimization_barrier((own, grads[0]))
-            wgrads[1] = [w[0] for w in unpack(swap(own)[None].astype(f32), [s.shape for s in shards[1]], hcols)]
             wgrads[l] = scatter_sum(grads, [False, True, False, True], 5)
         else:
             packed = pack(grads, hcols)
             packed, grad = lax.optimization_barrier((packed, grad))
             rows = packed.shape[1]
             own = lax.psum_scatter(packed.reshape(-1, hcols), group, scatter_dimension=0, tiled=True)
+    wgrads[0] = list(wgrads[0])
+    own, wgrads[0][1] = lax.optimization_barrier((own, wgrads[0][1]))
+    wgrads[1] = [w[0] for w in unpack(swap(own)[None].astype(f32), [s.shape for s in shards[1]], hcols)]
+    wgrads[0][0], small[0][0] = lax.optimization_barrier((wgrads[0][0], small[0][0]))
     gains, shifts, obias, qvb, upb = small_sum(small, 6)
     gq, gp, gu, gd = [jnp.stack([w[i] for w in wgrads]) for i in range(4)]
     return (state, grad, gq.reshape(layers, -1, 3, hcols), qvb, gp, gu, upb, gd, gains, shifts, obias)

time: 754 us -> 686 us (0.910)
  local copies, waits for them, and re-layouts: 81.4 us -> 44.7 us
  Pallas kernels: 471 us -> 451 us
  waiting for transfers between devices: 22 us -> 10.8 us
  matrix products: 108 us -> 117 us
    pallas_call x2, Pallas kernels: 97.4 us -> 77.1 us  [halo_back(): pl.pallas_call(functools.partial(halo_back_kernel, count), out_shape=jax....]
    pallas_call x1, Pallas kernels: 36.7 us -> 17.7 us  [small_sum(): pl.pallas_call(functools.partial(small_sum_kernel, rows, layers), out_sha...]
    pallas_call x1, Pallas kernels: 82.2 us -> 95.5 us  [scatter_sum(): pl.pallas_call(functools.partial(reduce_kernel, count, early), out_shape=...]
    dot_general x2 -> x0, local copies, waits for them, and re-layouts: 13 us -> none  [mm(): return jnp.dot(a, b, preferred_element_type=f32)]
    all_gather x2, waiting for transfers between devices: 21.9 us -> 10.7 us  [body(): every = lambda t: lax.all_gather(t, group, axis=0, tiled=False)]
    broadcast_in_dim x18 -> x0, local copies, waits for them, and re-layouts: 10.6 us -> none  [the longest x4 2.35 us: norm_backward(): jnp.sum(grad_out, axis=0, keepdims=True)]
    pallas_call x1, Pallas kernels: 56.1 us -> 65.1 us  [gather(): pl.pallas_call(functools.partial(gather_kernel, count, y_first), out_shap...]
    dot_general x36 -> x28, matrix products: 108 us -> 117 us  [mm(): return jnp.dot(a, b, preferred_element_type=f32)]
  transfers between devices with their start and end apart: 6 -> 6, of which waited for: 1 -> 1; matrix products, arithmetic and copies ran while one was open for 19% -> 16% of each run, Pallas kernels for 50% -> 54%
where the time goes in v3:
time: 686 us; the launch traced here: 685 us
  Pallas kernels  451 us (66%)
  matrix products  117 us (17%)
  local copies, waits for them, and re-layouts  44.7 us (7%)
  other arithmetic  39.2 us (6%)
  between operations  15.2 us (2%)
  waiting for transfers between devices  10.8 us (2%)
  starting transfers between devices  6.89 us (1%)
    dot_general x28, matrix products, mm(): return jnp.dot(a, b, preferred_element_type=f32)  117 us
    pallas_call x1, Pallas kernels, scatter_sum(): pl.pallas_call(functools.partial(reduce_kernel, count, early), out_shape=...  95.5 us
    pallas_call x2, Pallas kernels, halo_back(): pl.pallas_call(functools.partial(halo_back_kernel, count), out_shape=jax....  77.1 us
    pallas_call x2, Pallas kernels, halo(): pl.pallas_call(functools.partial(halo_kernel, count), out_shape=jax.Shape...  68.3 us
    pallas_call x1, Pallas kernels, gather(): pl.pallas_call(functools.partial(gather_kernel, count, y_first), out_shap...  65.1 us
    pallas_call x2, Pallas kernels, attend_back(): pl.pallas_call(functools.partial(bwd_kernel, rows // 2), grid_spec=pltpu....  46.9 us
    pallas_call x2, Pallas kernels, attend(): pl.pallas_call(functools.partial(fwd_kernel, rows // 2), grid_spec=pltpu....  29.3 us
    pallas_call x6, Pallas kernels, pair_sum(): pl.pallas_call(pair_sum_kernel, out_shape=jax.ShapeDtypeStruct(p.shape[1:...  26.7 us
  transfers between devices with their start and end apart: 6, of which 1 were waited for; matrix products, arithmetic and copies ran while one was open for 16% of the time, Pallas kernels for 54%

profile of v3, /device:TPU:0, one launch (start us, length us, event | category | flops | bytes accessed | tf_op | source)
XLA Modules:
  0.0 684.7 jit_solution(17940164883289787891)
XLA Ops:
  13.1 65.1 %shard_map.213 = (bf16[16,48,1152]{2,1,0:T(8,128)(2,1)}, bf16[16,24,768]{2,1,0:T(8,128)(2,1)}, bf16[16,48,1536]{2,1,0:T(8,128)(2,1)}, bf16[16,24,768]{2,1,0:T(8,128)(2,1)}, f32[2,2304]{1,0:T(2,128)}) custom-call(bf16[48,1152]{1,0:T(8,128)(2,1)} %bitcast.188, bf16[24,768]{1,0:T(8,128)(2,1)} %get-tuple-element.187.refs_1_, ...), custom_call_target="tpu_custom_call" | custom-call | tf_op jit(solution)/shard_map/pallas_call | solution.py:158
  83.8 30.8 %shard_map.212 = bf16[7,384,768]{2,1,0:T(8,128)(2,1)} custom-call(bf16[384,768]{1,0:T(8,128)(2,1)} %add_convert_fusion.3.a_ref), custom_call_target="tpu_custom_call" | custom-call | tf_op jit(solution)/shard_map/pallas_call | solution.py:255
  118.0 1.6 fusion.12.q_ref
  120.4 3.7 convolution_convert_fusion.3.k_ref
  124.1 3.8 fusion.10.v_ref
  127.9 14.5 %shard_map.214 = (bf16[768,384]{1,0:T(8,128)(2,1)}, f32[6,768]{1,0:T(8,128)}) custom-call(s32[2,2]{1,0:T(2,128)} %pad_add_fusion.1.span_ref, bf16[768,384]{1,0:T(8,128)(2,1)} %fusion.12.q_ref, bf16[2688,384]{1,0:T(8,128)(2,1)} %convolution_convert_fusion.3.k_ref, bf16[2688,384]{1,0:T(8,128)(2,1)} %fusion.10.v_ref, s32[768,1]{1,0:T(8,128)} %broadcast_in_dim.23.idq_ref, ...), custom_call_target="tpu_custom_call" | custom-call | flops 3170893824 | bytes 6193152 | tf_op jit(solution)/shard_map/pallas_call | solution.py:731
  142.4 2.9 convolution_convert_fusion.11
  145.2 4.4 shard_map.215
  152.6 4.1 shard_map.216
  156.7 7.1 %multiply_convert_fusion.1 = (bf16[768,1536]{1,0:T(8,128)(2,1)}, f32[768,1536]{1,0:T(8,128)}) fusion(f32[1536]{0:T(1024)S(1)} %get-tuple-element.130, bf16[768,768]{1,0:T(8,128)(2,1)} %bitcast.164, bf16[768,1536]{1,0:T(8,128)(2,1)} %bitcast.194), kind=kOutput, calls=%fused_computation.18 | convolution fusion | flops 1819017216 | bytes 10622976 | tf_op jit(solution)/shard_map/dot_general | solution.py:861
  163.8 3.2 slice.243
  168.6 2.0 broadcast_in_dim.24.idk_ref
  172.2 2.4 reshape_reshape.3
  174.7 5.4 convolution_convert_fusion.15
  180.1 4.4 shard_map.217
  187.4 37.5 %shard_map.218 = bf16[7,384,768]{2,1,0:T(8,128)(2,1)} custom-call(bf16[384,768]{1,0:T(8,128)(2,1)} %add_convert_fusion.1.a_ref), custom_call_target="tpu_custom_call" | custom-call | tf_op jit(solution)/shard_map/pallas_call | solution.py:255
  226.8 1.6 fusion.13.q_ref
  229.2 3.7 convolution_convert_fusion.2.k_ref
  232.8 3.7 fusion.11.v_ref
  236.6 14.8 %shard_map.219 = (bf16[768,384]{1,0:T(8,128)(2,1)}, f32[6,768]{1,0:T(8,128)}) custom-call(s32[2,2]{1,0:T(2,128)} %pad_add_fusion.1.span_ref, bf16[768,384]{1,0:T(8,128)(2,1)} %fusion.13.q_ref, bf16[2688,384]{1,0:T(8,128)(2,1)} %convolution_convert_fusion.2.k_ref, bf16[2688,384]{1,0:T(8,128)(2,1)} %fusion.11.v_ref, s32[768,1]{1,0:T(8,128)} %broadcast_in_dim.23.idq_ref, ...), custom_call_target="tpu_custom_call" | custom-call | flops 3170893824 | bytes 6193152 | tf_op jit(solution)/shard_map/pallas_call | solution.py:731
  251.4 10.7 %all-gather.7.cloned.1.call-done = bf16[3072,768]{1,0:T(8,128)(2,1)} async-done(((bf16[192,768]{1,0:T(8,128)(2,1)}), bf16[3072,768]{1,0:T(8,128)(2,1)}) %all-gather.7.cloned.1.call-update) | async-done | bytes 4718608 | tf_op jit(solution)/shard_map/all_gather | solution.py:897
  262.1 3.4 slice.261
  267.2 1.8 convolution_convert_fusion.10
  269.0 4.5 shard_map.220
  273.5 3.7 fusion.41
  279.2 4.1 shard_map.221
  283.3 4.2 shard_map.223
  287.5 1.9 pad_maximum_fusion
  289.5 2.5 multiply_convert_fusion
  292.0 3.0 convolution_convert_fusion.14
  295.0 3.4 convolution_convert_fusion.7
  298.5 4.5 fusion.54
  302.9 3.0 convolution_convert_fusion.13
  306.0 4.5 shard_map.224
  310.5 4.4 shard_map.222
  315.0 2.6 multiply_reduce_fusion
  317.6 3.4 fusion.39
  322.9 4.1 shard_map.225
  327.0 3.1 convolution_convert_fusion.19.da_ref
  331.4 3.4 convolution_convert_fusion.8
  334.8 23.4 %shard_map.226 = (bf16[2688,1152]{1,0:T(8,128)(2,1)}, f32[1,384]{1,0:T(1,128)}, f32[1,384]{1,0:T(1,128)}) custom-call(s32[2,2]{1,0:T(2,128)} %pad_add_fusion.1.span_ref, bf16[768,384]{1,0:T(8,128)(2,1)} %fusion.13.q_ref, bf16[2688,384]{1,0:T(8,128)(2,1)} %convolution_convert_fusion.2.k_ref, bf16[2688,384]{1,0:T(8,128)(2,1)} %fusion.11.v_ref, ...), custom_call_target="tpu_custom_call" | custom-call | flops 7927234560 | bytes 10321920 | tf_op jit(solution)/shard_map/pallas_call | solution.py:812
  358.2 10.7 %convolution_convert_fusion.9 = bf16[768,1152]{1,0:T(8,128)(2,1)} fusion(bf16[2688,768]{1,0:T(8,128)(2,1)} %bitcast.135, bf16[2688,1152]{1,0:T(8,128)(2,1)} %get-tuple-element.69), kind=kOutput, calls=%fused_computation.31 | convolution fusion | flops 4757225472 | bytes 12091392 | tf_op jit(solution)/shard_map/dot_general | solution.py:861
  368.9 7.2 %convolution_convert_fusion.1 = bf16[2688,768]{1,0:T(8,128)(2,1)} fusion(bf16[2688,1152]{1,0:T(8,128)(2,1)S(1)} %copy-done.78, bf16[768,1152]{1,0:T(8,128)(2,1)S(1)} %copy-done.18), kind=kOutput, calls=%fused_computation.3 | convolution fusion | flops 4758405120 | bytes 12091392 | tf_op jit(solution)/shard_map/dot_general | solution.py:861
  376.1 34.8 %shard_map.227 = f32[384,768]{1,0:T(8,128)} custom-call(bf16[7,384,768]{2,1,0:T(8,128)(2,1)} %bitcast.144), custom_call_target="tpu_custom_call" | custom-call | tf_op jit(solution)/shard_map/pallas_call | solution.py:349
  411.0 2.5 multiply_reduce_fusion.1
  419.1 2.5 copy-done.8
  422.5 4.1 shard_map.228
  426.6 6.8 fusion.53
  433.5 3.0 convolution_convert_fusion.12
  436.5 4.4 shard_map.229
  441.0 2.5 multiply_reduce_fusion.2
  445.4 4.1 shard_map.230
  449.6 2.9 convolution_convert_fusion.17.da_ref
  452.5 23.5 %shard_map.231 = (bf16[2688,1152]{1,0:T(8,128)(2,1)}, f32[1,384]{1,0:T(1,128)}, f32[1,384]{1,0:T(1,128)}) custom-call(s32[2,2]{1,0:T(2,128)} %pad_add_fusion.1.span_ref, bf16[768,384]{1,0:T(8,128)(2,1)} %fusion.12.q_ref, bf16[2688,384]{1,0:T(8,128)(2,1)} %convolution_convert_fusion.3.k_ref, bf16[2688,384]{1,0:T(8,128)(2,1)} %fusion.10.v_ref, ...), custom_call_target="tpu_custom_call" | custom-call | flops 7927234560 | bytes 10321920 | tf_op jit(solution)/shard_map/pallas_call | solution.py:812
  476.0 9.7 %convolution_convert_fusion = bf16[2688,768]{1,0:T(8,128)(2,1)} fusion(bf16[2688,1152]{1,0:T(8,128)(2,1)} %get-tuple-element.72, bf16[768,1152]{1,0:T(8,128)(2,1)} %bitcast.196), kind=kOutput, calls=%fused_computation.2 | convolution fusion | flops 4758405120 | bytes 12091392 | tf_op jit(solution)/shard_map/dot_general | solution.py:861
  485.8 42.3 %shard_map.232 = f32[384,768]{1,0:T(8,128)} custom-call(bf16[7,384,768]{2,1,0:T(8,128)(2,1)} %bitcast.145), custom_call_target="tpu_custom_call" | custom-call | tf_op jit(solution)/shard_map/pallas_call | solution.py:349
  529.6 5.5 convolution_convert_fusion.4
  535.1 3.5 convolution_convert_fusion.5
  538.6 7.0 %convolution_convert_fusion.6 = bf16[768,1152]{1,0:T(8,128)(2,1)} fusion(bf16[2688,768]{1,0:T(8,128)(2,1)S(1)} %bitcast.134, bf16[2688,1152]{1,0:T(8,128)(2,1)S(1)} %bitcast.201), kind=kOutput, calls=%fused_computation.28 | convolution fusion | flops 4757225472 | bytes 12091392 | tf_op jit(solution)/shard_map/dot_general | solution.py:861
  545.6 95.5 %shard_map.233 = (f32[48,1152]{1,0:T(8,128)}, f32[24,768]{1,0:T(8,128)}, f32[48,1536]{1,0:T(8,128)}, f32[96,768]{1,0:T(8,128)}) custom-call(bf16[16,48,1152]{2,1,0:T(8,128)(2,1)} %bitcast.160, bf16[16,24,768]{2,1,0:T(8,128)(2,1)} %bitcast.180, bf16[16,48,1536]{2,1,0:T(8,128)(2,1)} %bitcast.147, bf16[16,96,768]{2,1,0:T(8,128)(2,1)} %bitcast.146), custom_call_target="tpu_custom_call" | custom-call | tf_op jit(solution)/shard_map/pallas_call | solution.py:642
  642.3 5.0 collective-permute-start.2
  648.6 17.7 %shard_map.234 = (f32[2,2,768]{2,1,0:T(2,128)}, f32[2,2,768]{2,1,0:T(2,128)}, f32[2,2,768]{2,1,0:T(2,128)}, f32[2,2,384]{2,1,0:T(2,128)}, f32[2,1536]{1,0:T(2,128)}) custom-call(f32[768]{0:T(1024)} %get-tuple-element.78.refs_0_, f32[768]{0:T(1024)} %get-tuple-element.117.refs_1_, f32[768]{0:T(1024)} %get-tuple-element.128.refs_2_, ...), custom_call_target="tpu_custom_call" | custom-call | tf_op jit(solution)/shard_map/pallas_call | solution.py:451
  666.4 1.7 stack.35
  668.1 2.1 multiply_add_fusion
  (278 shorter events, 53.8 us)
Async XLA Ops:
  7.2 3.2 copy-start.74
  7.2 3.2 copy-start.35
  7.2 3.9 copy-start.70
  7.2 5.2 copy-start.40
  7.2 156.6 %all-gather.5.cloned.1.call-start = ((), (), s32[]{:S(2)}) async-start(), calls=%async_computation.2 | async-start | bytes 4386816 | tf_op jit(solution)/shard_map/all_gather | solution.py:897
  8.5 71.2 %copy-start.50 = (s32[12288]{0:T(1024)S(1)}, s32[12288]{0:T(1024)}, u32[]{:S(2)}) copy-start(s32[12288]{0:T(1024)} %param.16) | copy-start | bytes 147460
  8.5 71.2 %copy-start.51 = (s32[12288]{0:T(1024)S(1)}, s32[12288]{0:T(1024)}, u32[]{:S(2)}) copy-start(s32[12288]{0:T(1024)} %param.15) | copy-start | bytes 147460
  9.6 72.0 %copy-start = (f32[384,768]{1,0:T(8,128)S(1)}, f32[384,768]{1,0:T(8,128)}, u32[]{:S(2)}) copy-start(f32[384,768]{1,0:T(8,128)} %param.13) | copy-start | bytes 3538948
  9.6 68.6 %collective-permute-start = (bf16[168,768]{1,0:T(8,128)(2,1)S(1)}, bf16[168,768]{1,0:T(8,128)(2,1)S(1)}, u32[]{:S(2)}, u32[]{:S(2)}) collective-permute-start(bf16[168,768]{1,0:T(8,128)(2,1)S(1)} %maximum_bitcast_fusion.1), channel_id=1, source_target_pairs={{0,0},{1,2},{2,1},{3,3},{4,4},{5,6},{6,5},{7,7},{8,8},{9,10},{10,9... | collective-permute-start | bytes 774152 | tf_op jit(solution)/shard_map/ppermute | solution.py:875
  12.5 69.3 %copy-start.63 = (f32[2,2,768]{2,1,0:T(2,128)S(1)}, f32[2,2,768]{2,1,0:T(2,128)}, u32[]{:S(2)}) copy-start(f32[2,2,768]{2,1,0:T(2,128)} %param.17) | copy-start | bytes 36868
  12.5 69.3 %copy-start.64 = (f32[2,2,768]{2,1,0:T(2,128)S(1)}, f32[2,2,768]{2,1,0:T(2,128)}, u32[]{:S(2)}) copy-start(f32[2,2,768]{2,1,0:T(2,128)} %param.18) | copy-start | bytes 36868
  78.9 183.2 %all-gather.7.cloned.1.call-start = ((), (), s32[]{:S(2)}) async-start(), calls=%async_computation.3 | async-start | bytes 5013504 | tf_op jit(solution)/shard_map/all_gather | solution.py:897
  79.0 88.0 %collective-permute-start.1 = (bf16[192,768]{1,0:T(8,128)(2,1)S(1)}, bf16[192,768]{1,0:T(8,128)(2,1)S(1)}, u32[]{:S(2)}, u32[]{:S(2)}) collective-permute-start(bf16[192,768]{1,0:T(8,128)(2,1)S(1)} %maximum_bitcast_fusion), channel_id=1, source_target_pairs={{0,0},{1,2},{2,1},{3,3},{4,4},{5,6},{6,5},{7,7},{8,8},{9,10},{10,9... | collective-permute-start | bytes 884744 | tf_op jit(solution)/shard_map/ppermute | solution.py:875
  81.8 32.8 %copy-start.42 = (f32[768]{0:T(1024)}, f32[768]{0:T(1024)S(1)}, u32[]{:S(2)}) copy-start(f32[768]{0:T(1024)S(1)} %get-tuple-element.141) | copy-start | bytes 9220
  82.4 32.1 %copy-start.44 = (f32[384]{0:T(512)}, f32[384]{0:T(512)S(1)}, u32[]{:S(2)}) copy-start(f32[384]{0:T(512)S(1)} %broadcast_multiply_fusion.11) | copy-start | bytes 4612
  82.7 31.9 %copy-start.52 = (f32[384]{0:T(512)}, f32[384]{0:T(512)S(1)}, u32[]{:S(2)}) copy-start(f32[384]{0:T(512)S(1)} %add_rsqrt_fusion.3) | copy-start | bytes 4612
  83.8 31.6 %copy-start.60 = (f32[2,2304]{1,0:T(2,128)S(1)}, f32[2,2304]{1,0:T(2,128)}, u32[]{:S(2)}) copy-start(f32[2,2304]{1,0:T(2,128)} %get-tuple-element.55) | copy-start | bytes 55300
  83.8 31.7 %copy-start.65 = (f32[2,2,768]{2,1,0:T(2,128)S(1)}, f32[2,2,768]{2,1,0:T(2,128)}, u32[]{:S(2)}) copy-start(f32[2,2,768]{2,1,0:T(2,128)} %param.25) | copy-start | bytes 36868
  114.6 3.4 copy-start.77
  116.7 40.0 %copy-start.71 = (f32[1536]{0:T(1024)}, f32[1536]{0:T(1024)S(1)}, u32[]{:S(2)}) copy-start(f32[1536]{0:T(1024)S(1)} %get-tuple-element.130) | copy-start | bytes 18436
  127.9 14.5 %copy-start.28 = (bf16[16,24,768]{2,1,0:T(8,128)(2,1)S(1)}, bf16[16,24,768]{2,1,0:T(8,128)(2,1)}, u32[]{:S(2)}) copy-start(bf16[16,24,768]{2,1,0:T(8,128)(2,1)} %get-tuple-element.57) | copy-start | bytes 1769476
  151.5 5.2 copy-start.54
  167.7 474.6 %reduce-scatter.2.cloned.1.call-start = ((), (), s32[]{:S(2)}) async-start(), calls=%async_computation.1 | async-start | bytes 7520256 | tf_op jit(solution)/shard_map/reduce_scatter | solution.py:964
  186.0 38.9 %copy-start.46 = (f32[384]{0:T(512)}, f32[384]{0:T(512)S(1)}, u32[]{:S(2)}) copy-start(f32[384]{0:T(512)S(1)} %broadcast_multiply_fusion.9) | copy-start | bytes 4612
  186.3 38.6 %copy-start.56 = (f32[384]{0:T(512)}, f32[384]{0:T(512)S(1)}, u32[]{:S(2)}) copy-start(f32[384]{0:T(512)S(1)} %add_rsqrt_fusion.1) | copy-start | bytes 4612
  262.1 3.4 copy-start.12
  273.5 4.6 copy-start.62
  292.0 3.0 copy-start.25
  302.9 3.0 copy-start.81
  314.9 2.6 copy-start.2
  314.9 2.6 copy-start.13
  314.9 2.6 copy-start.49
  322.0 5.0 copy-start.31
  327.0 3.1 copy-start.26
  327.0 3.1 copy-start.34
  327.0 3.7 copy-start.82
  358.2 10.7 %copy-start.18 = (bf16[768,1152]{1,0:T(8,128)(2,1)S(1)}, bf16[768,1152]{1,0:T(8,128)(2,1)}, u32[]{:S(2)}) copy-start(bf16[768,1152]{1,0:T(8,128)(2,1)} %reshape_reshape.3) | copy-start | bytes 5308420
  358.2 10.7 %copy-start.78 = (bf16[2688,1152]{1,0:T(8,128)(2,1)S(1)}, bf16[2688,1152]{1,0:T(8,128)(2,1)}, u32[]{:S(2)}) copy-start(bf16[2688,1152]{1,0:T(8,128)(2,1)} %get-tuple-element.69) | copy-start | bytes 18579460
  376.1 34.8 %copy-start.47 = (f32[384]{0:T(512)S(1)}, f32[384]{0:T(512)}, u32[]{:S(2)}) copy-start(f32[384]{0:T(512)} %copy-done.46) | copy-start | bytes 4612
  376.1 34.8 %copy-start.57 = (f32[384]{0:T(512)S(1)}, f32[384]{0:T(512)}, u32[]{:S(2)}) copy-start(f32[384]{0:T(512)} %copy-done.56) | copy-start | bytes 4612
  418.7 2.9 copy-start.8
  421.6 5.0 copy-start.72
  426.6 6.8 copy-start.76
  433.5 3.0 copy-start.79
  436.5 4.4 copy-start.55
  444.6 5.0 copy-start.29
  485.8 42.3 %copy-start.24 = (bf16[2,384,768]{2,1,0:T(8,128)(2,1)S(1)}, bf16[2,384,768]{2,1,0:T(8,128)(2,1)}, u32[]{:S(2)}) copy-start(bf16[2,384,768]{2,1,0:T(8,128)(2,1)} %shard_map.230) | copy-start | bytes 3538948
  485.8 42.3 %copy-start.32 = (bf16[768,384]{1,0:T(8,128)(2,1)S(1)}, bf16[768,384]{1,0:T(8,128)(2,1)}, u32[]{:S(2)}) copy-start(bf16[768,384]{1,0:T(8,128)(2,1)} %get-tuple-element.56.o_ref) | copy-start | bytes 1769476
  528.1 10.5 %slice-start = ((s8[6193152]{0:T(1024)(128)(4,1)}), s8[4194304]{0:T(1024)(128)(4,1)S(1)}, s32[]{:S(2)}) async-start(s8[6193152]{0:T(1024)(128)(4,1)} %bitcast.200), calls=%async_computation.4 | async-start | bytes 8388608
  529.6 5.6 copy-start.20
  529.6 5.6 copy-start.80
  529.6 9.0 %slice-start.1 = ((s8[6193152]{0:T(1024)(128)(4,1)}), s8[1998848]{0:T(1024)(128)(4,1)S(1)}, s32[]{:S(2)}) async-start(s8[6193152]{0:T(1024)(128)(4,1)} %bitcast.200), calls=%async_computation.5 | async-start | bytes 3997696
  535.1 3.5 copy-start.10
  545.6 95.5 %copy-start.1 = (f32[384,768]{1,0:T(8,128)S(1)}, f32[384,768]{1,0:T(8,128)}, u32[]{:S(2)}) copy-start(f32[384,768]{1,0:T(8,128)} %param.13) | copy-start | bytes 3538948
  545.6 95.5 %copy-start.4 = (f32[384,768]{1,0:T(8,128)S(1)}, f32[384,768]{1,0:T(8,128)}, u32[]{:S(2)}) copy-start(f32[384,768]{1,0:T(8,128)} %shard_map.232) | copy-start | bytes 3538948
  545.6 95.6 %copy-start.43 = (f32[768]{0:T(1024)S(1)}, f32[768]{0:T(1024)}, u32[]{:S(2)}) copy-start(f32[768]{0:T(1024)} %copy-done.42) | copy-start | bytes 9220
  545.6 95.6 %copy-start.45 = (f32[384]{0:T(512)S(1)}, f32[384]{0:T(512)}, u32[]{:S(2)}) copy-start(f32[384]{0:T(512)} %copy-done.44) | copy-start | bytes 4612
  545.6 95.6 %copy-start.53 = (f32[384]{0:T(512)S(1)}, f32[384]{0:T(512)}, u32[]{:S(2)}) copy-start(f32[384]{0:T(512)} %copy-done.52) | copy-start | bytes 4612
  642.3 27.8 %collective-permute-start.2 = (bf16[576,384]{1,0:T(8,128)(2,1)}, bf16[576,384]{1,0:T(8,128)(2,1)}, u32[]{:S(2)}, u32[]{:S(2)}) collective-permute-start(bf16[576,384]{1,0:T(8,128)(2,1)} %reduce-scatter.2.cloned.1.call-done), channel_id=1, source_target_pairs={{0,0},{1,2},{2,1},{3,3},{4,4},{5,6},{6,5},{7,7},{8,8},{9,10},{10,9... | collective-permute-start | bytes 1327112 | tf_op jit(solution)/shard_map/ppermute | solution.py:875
  671.7 3.2 copy-start.75
  671.7 3.8 copy-start.69
  671.7 4.4 copy-start.68
  671.7 5.0 copy-start.67
  671.7 5.6 copy-start.66
  (27 other events, 46.1 us)
Sparse Core Ops, SparseCore 0:
  79.1 80.7 all-gather.4
  167.9 94.1 all-gather.6
  421.7 167.7 reduce-scatter.1
